TPU v7x, 512 devices: a whole 4x8x8 slice. The times are simulated.
512 devices in a mesh: ctx: 64 (over z_hi, y, core), tp: 8 (over x, z_lo).
Axes of the slice: x: 4, y: 8, z: 8 (z_hi: 4, z_lo: 2; z = z_hi * 2 + z_lo), core: 2. Of those that a mesh axis runs over, the one named last changes fastest.
Arguments:
- query_in: bfloat16 [1024, 16384], P('tp', 'ctx'), may hold values from -6 to 6
- key_in: bfloat16 [1024, 16384], P('tp', 'ctx'), may hold values from -6 to 6
- value_in: bfloat16 [1024, 16384], P('tp', 'ctx'), may hold values from -6 to 6
- short_kernel: float32 [3, 1024, 7], P(None, 'tp'), may hold values from -2 to 2
- basis_weight: float32 [64, 33], replicated, may hold values from -96 to 96
- basis_bias: float32 [64], replicated, may hold values from -3.140625 to 3.140625
- filter_proj: float32 [1024, 64], P('tp'), may hold values from -0.75 to 0.75
- decay_rate: float32 [1024], P('tp'), as said below
- skip_gain: float32 [1024], P('tp'), may hold values from -3 to 3
- grad_out: bfloat16 [1024, 16384], P('tp', 'ctx'), may hold values from -6 to 6
Outputs:
- mixed: bfloat16 [1024, 16384], P('tp', 'ctx')
- grad_query: bfloat16 [1024, 16384], P('tp', 'ctx')
- grad_key: bfloat16 [1024, 16384], P('tp', 'ctx')
- grad_value: bfloat16 [1024, 16384], P('tp', 'ctx')
- grad_proj: float32 [1024, 64], P('tp')
- grad_basis: float32 [64, 33], replicated
Inputs may be any that keep to these rules, and one draw needn't show every extreme that they name: decay_rate is positive in every channel.
All inputs are finite; a program needn't handle non-finite values.
Results may differ from a plain program's by a relative error of at most 0.0066.
Values may be sent and summed in bfloat16 or wider, within the bound.
No kernel may reach another device: no remote copies, remote signals or barrier semaphores. Data moves between devices by JAX's collectives and lax.ppermute only.
A program may use at most 64 MiB of HBM per device.

v0:
```python
import math

import jax
import jax.numpy as jnp
from jax import lax
from jax.sharding import PartitionSpec as P

PRECISE = lax.Precision.HIGHEST


def passed_along(value, axis, steps):
    count = lax.axis_size(axis)
    leading, last = (max(0, -steps), min(count, count - steps))
    return lax.ppermute(value, axis, [(source, source + steps) for source in range(leading, last)])


def features(offset_pos, num_pos, seq_total, num_freq):
    positions = offset_pos + jnp.arange(num_pos, dtype=jnp.int32)
    pieces = [positions.astype(jnp.float32) / seq_total]
    for harmonic in range(1, num_freq + 1):
        angles = (harmonic * positions % seq_total).astype(jnp.float32) * (
            2.0 * math.pi / seq_total
        )
        pieces.append(jnp.cos(angles))
        pieces.append(jnp.sin(angles))
    return jnp.stack(pieces)


def window(decay_rate, offset_pos, num_pos, seq_total):
    positions = (offset_pos + jnp.arange(num_pos, dtype=jnp.int32)).astype(jnp.float32)
    energy = jnp.expm1(-2.0 * decay_rate) / jnp.expm1(-2.0 * decay_rate / seq_total)
    return (
        jnp.exp(-(decay_rate[:, None] * positions[None, :]) / seq_total) / jnp.sqrt(energy)[:, None]
    )


def featurize_rim(signal, before, kernel):
    extended = jnp.concatenate([before, signal], axis=1).astype(jnp.float32)
    num_taps = kernel.shape[1]
    rim_len = num_taps - 1
    num_tok = signal.shape[1]
    result = kernel[:, 0:1] * extended[:, rim_len:]
    for offset in range(1, num_taps):
        result = (
            result
            + kernel[:, offset : offset + 1]
            * extended[:, rim_len - offset : rim_len - offset + num_tok]
        )
    return result


def featurize_back(signal, following, kernel):
    extended = jnp.concatenate([signal, following], axis=1).astype(jnp.float32)
    num_taps = kernel.shape[1]
    num_tok = signal.shape[1]
    result = kernel[:, 0:1] * extended[:, :num_tok]
    for offset in range(1, num_taps):
        result = result + kernel[:, offset : offset + 1] * extended[:, offset : offset + num_tok]
    return result


def tables(num_rows, num_cols, modulus):
    row_ids = jnp.arange(num_rows, dtype=jnp.int32)[:, None]
    col_ids = jnp.arange(num_cols, dtype=jnp.int32)[None, :]
    angles = (row_ids * col_ids % modulus).astype(jnp.float32) * (-2.0 * math.pi / modulus)
    return (jnp.cos(angles), jnp.sin(angles))


def spectrum(signal, outer, twiddle, inner):
    num_chan = signal.shape[0]
    folded = signal.reshape(num_chan, outer[0].shape[1], inner[0].shape[0])
    section_re = jnp.einsum("kt,nts->nks", outer[0], folded, precision=PRECISE)
    section_im = jnp.einsum("kt,nts->nks", outer[1], folded, precision=PRECISE)
    turned_re = section_re * twiddle[0] - section_im * twiddle[1]
    turned_im = section_re * twiddle[1] + section_im * twiddle[0]
    spec_re = jnp.einsum("nks,sj->nkj", turned_re, inner[0], precision=PRECISE) - jnp.einsum(
        "nks,sj->nkj", turned_im, inner[1], precision=PRECISE
    )
    spec_im = jnp.einsum("nks,sj->nkj", turned_re, inner[1], precision=PRECISE) + jnp.einsum(
        "nks,sj->nkj", turned_im, inner[0], precision=PRECISE
    )
    return (spec_re, spec_im)


def restore(spec_re, spec_im, outer, twiddle, inner):
    num_chan = spec_re.shape[0]
    padded_len = outer[0].shape[0] * inner[0].shape[0]
    back_re = jnp.einsum("nkj,sj->nks", spec_re, inner[0], precision=PRECISE) + jnp.einsum(
        "nkj,sj->nks", spec_im, inner[1], precision=PRECISE
    )
    back_im = jnp.einsum("nkj,sj->nks", spec_im, inner[0], precision=PRECISE) - jnp.einsum(
        "nkj,sj->nks", spec_re, inner[1], precision=PRECISE
    )
    turned_re = back_re * twiddle[0] + back_im * twiddle[1]
    turned_im = back_im * twiddle[0] - back_re * twiddle[1]
    result = jnp.einsum("kt,nks->nts", outer[0], turned_re, precision=PRECISE) + jnp.einsum(
        "kt,nks->nts", outer[1], turned_im, precision=PRECISE
    )
    return result.reshape(num_chan, -1) * (1.0 / padded_len)


def convolve_forward(carried_chan, filter_chan, own_skip, transform_tables):
    outer, twiddle, inner = transform_tables
    carried_wide = carried_chan.astype(jnp.float32)
    carried_re, carried_im = spectrum(carried_wide, outer, twiddle, inner)
    filter_re, filter_im = spectrum(filter_chan.astype(jnp.float32), outer, twiddle, inner)
    conv_chan = restore(
        filter_re * carried_re - filter_im * carried_im,
        filter_re * carried_im + filter_im * carried_re,
        outer,
        twiddle,
        inner,
    )
    long_chan = (conv_chan + own_skip[:, None] * carried_wide).astype(jnp.bfloat16)
    return (long_chan, (carried_re, carried_im, filter_re, filter_im))


def convolve_backward(grad_chan, spectra, own_skip, transform_tables):
    outer, twiddle, inner = transform_tables
    carried_re, carried_im, filter_re, filter_im = spectra
    grad_chan_wide = grad_chan.astype(jnp.float32)
    grad_re, grad_im = spectrum(grad_chan_wide, outer, twiddle, inner)
    carried_grad_chan = (
        restore(
            filter_re * grad_re + filter_im * grad_im,
            filter_re * grad_im - filter_im * grad_re,
            outer,
            twiddle,
            inner,
        )
        + own_skip[:, None] * grad_chan_wide
    ).astype(jnp.bfloat16)
    filter_grad_chan = restore(
        carried_re * grad_re + carried_im * grad_im,
        carried_re * grad_im - carried_im * grad_re,
        outer,
        twiddle,
        inner,
    ).astype(jnp.bfloat16)
    return (carried_grad_chan, filter_grad_chan)


def on_device(
    query_in,
    key_in,
    value_in,
    short_kernel,
    basis_weight,
    basis_bias,
    filter_proj,
    decay_rate,
    skip_gain,
    grad_out,
):
    ctx_size = lax.axis_size("ctx")
    ctx_rank = lax.axis_index("ctx")
    tp_size = lax.axis_size("tp")
    num_tok = query_in.shape[1]
    chan_local = query_in.shape[0]
    seq_total = num_tok * ctx_size
    all_channels = chan_local * tp_size
    num_freq = (basis_weight.shape[1] - 1) // 2
    feat_width = basis_weight.shape[0]
    rim_len = short_kernel.shape[2] - 1
    tok_start = ctx_rank * num_tok
    rim_edge = num_tok - rim_len
    per_dev = chan_local // ctx_size
    chan_start = ctx_rank * per_dev
    own_skip = lax.dynamic_slice_in_dim(skip_gain, chan_start, per_dev)
    proj_scale = 1.0 / math.sqrt(seq_total)
    basis_scale = math.sqrt(feat_width / (seq_total * all_channels))
    before = passed_along(
        (query_in[:, rim_edge:], key_in[:, rim_edge:], value_in[:, rim_edge:]), "ctx", 1
    )
    query_feat = featurize_rim(query_in, before[0], short_kernel[0])
    key_feat = featurize_rim(key_in, before[1], short_kernel[1])
    value_feat = featurize_rim(value_in, before[2], short_kernel[2])
    carried = (key_feat * value_feat).astype(jnp.bfloat16)
    grad_wide = grad_out.astype(jnp.float32)
    grad_long = (grad_wide * query_feat).astype(jnp.bfloat16)
    basis_rows = features(tok_start, num_tok, seq_total, num_freq)
    hidden_in = (
        jnp.dot(basis_weight, basis_rows, precision=PRECISE, preferred_element_type=jnp.float32)
        + basis_bias[:, None]
    )
    activation = jnp.sin(hidden_in)
    envelope = window(decay_rate, tok_start, num_tok, seq_total)
    filter_tok = (
        jnp.dot(filter_proj, activation, precision=PRECISE, preferred_element_type=jnp.float32)
        * envelope
    ).astype(jnp.bfloat16)
    inner_len = 2 * ctx_size
    transform_tables = (
        tables(num_tok, num_tok // 2, num_tok),
        tables(num_tok, inner_len, 2 * seq_total),
        tables(inner_len, inner_len, inner_len),
    )
    spread = (
        lax.all_to_all(carried, "ctx", split_axis=0, concat_axis=1, tiled=True),
        lax.all_to_all(filter_tok, "ctx", split_axis=0, concat_axis=1, tiled=True),
    )
    carried_chan = spread[0]
    filter_chan = spread[1]
    long_chan, spectra = convolve_forward(carried_chan, filter_chan, own_skip, transform_tables)
    long_tok = lax.all_to_all(long_chan, "ctx", split_axis=1, concat_axis=0, tiled=True)
    grad_chan = lax.all_to_all(grad_long, "ctx", split_axis=0, concat_axis=1, tiled=True)
    carried_grad_chan, filter_grad_chan = convolve_backward(
        grad_chan, spectra, own_skip, transform_tables
    )
    returned = (
        lax.all_to_all(carried_grad_chan, "ctx", split_axis=1, concat_axis=0, tiled=True),
        lax.all_to_all(filter_grad_chan, "ctx", split_axis=1, concat_axis=0, tiled=True),
    )
    carried_grad = returned[0]
    filter_grad_tok = returned[1]
    long_wide = long_tok.astype(jnp.float32)
    mixed = (query_feat * long_wide).astype(jnp.bfloat16)
    grad_query_feat = (grad_wide * long_wide).astype(jnp.bfloat16)
    grad_raw = filter_grad_tok.astype(jnp.float32) * envelope
    part_proj = jnp.dot(
        grad_raw, activation.T, precision=PRECISE, preferred_element_type=jnp.float32
    )
    grad_hidden = jnp.dot(
        filter_proj.T, grad_raw, precision=PRECISE, preferred_element_type=jnp.float32
    ) * jnp.cos(hidden_in)
    part_basis = jnp.dot(
        grad_hidden, basis_rows.T, precision=PRECISE, preferred_element_type=jnp.float32
    )
    grad_proj = lax.psum(part_proj, "ctx") * proj_scale
    grad_basis = lax.psum(part_basis, ("ctx", "tp")) * basis_scale
    carried_grad_wide = carried_grad.astype(jnp.float32)
    grad_key_feat = (carried_grad_wide * value_feat).astype(jnp.bfloat16)
    grad_value_feat = (carried_grad_wide * key_feat).astype(jnp.bfloat16)
    following = passed_along(
        (grad_query_feat[:, :rim_len], grad_key_feat[:, :rim_len], grad_value_feat[:, :rim_len]),
        "ctx",
        -1,
    )
    grad_query = featurize_back(grad_query_feat, following[0], short_kernel[0]).astype(jnp.bfloat16)
    grad_key = featurize_back(grad_key_feat, following[1], short_kernel[1]).astype(jnp.bfloat16)
    grad_value = featurize_back(grad_value_feat, following[2], short_kernel[2]).astype(jnp.bfloat16)
    return (mixed, grad_query, grad_key, grad_value, grad_proj, grad_basis)


def solution(mesh):
    return jax.shard_map(
        on_device,
        mesh=mesh,
        in_specs=(
            P("tp", "ctx"),
            P("tp", "ctx"),
            P("tp", "ctx"),
            P(None, "tp", None),
            P(),
            P(),
            P("tp", None),
            P("tp"),
            P("tp"),
            P("tp", "ctx"),
        ),
        out_specs=(
            P("tp", "ctx"),
            P("tp", "ctx"),
            P("tp", "ctx"),
            P("tp", "ctx"),
            P("tp", None),
            P(),
        ),
        check_vma=False,
    )
```

profile of v0, /device:TPU:1, one launch (start us, length us, event | category | flops | bytes accessed | tf_op | source)
XLA Modules:
  0.0 538.5 jit_solution(8369667688324918726)
XLA Ops:
  0.6 0.8 slice.242
  1.5 4.6 collective-permute-start
  10.4 15.5 %all-to-all-start = ((bf16[64,2,256]{2,1,0:T(2,128)(2,1)}), bf16[64,2,256]{2,1,0:T(2,128)(2,1)S(1)}, u32[]{:S(2)}, u32[]{:S(2)}) async-start(bf16[64,2,256]{2,1,0:T(2,128)(2,1)} %all_to_all.60), calls=%async_computation | async-start | bytes 131072 | tf_op jit(solution)/shard_map/all_to_all | solution.py:200
  26.0 3.5 collective-permute-start.2
  29.6 2.2 collective-permute-start.1
  35.7 2.4 all-to-all-done
  38.1 9.7 %all-to-all-start.3 = ((bf16[64,2,256]{2,1,0:T(2,128)(2,1)}), bf16[64,2,256]{2,1,0:T(2,128)(2,1)S(1)}, u32[]{:S(2)}, u32[]{:S(2)}) async-start(bf16[64,2,256]{2,1,0:T(2,128)(2,1)} %all_to_all.67), calls=%async_computation.3 | async-start | bytes 131072 | tf_op jit(solution)/shard_map/all_to_all | solution.py:206
  47.8 0.8 convolution_bitcast_fusion.4
  48.6 0.8 convolution_bitcast_fusion.5
  49.4 0.8 fusion.144
  50.1 0.8 convolution_subtract_fusion.5
  50.9 0.8 fusion.121
  51.7 7.9 %all-to-all-done.3 = bf16[64,2,256]{2,1,0:T(2,128)(2,1)S(1)} async-done(((bf16[64,2,256]{2,1,0:T(2,128)(2,1)}), bf16[64,2,256]{2,1,0:T(2,128)(2,1)S(1)}, u32[]{:S(2)}, u32[]{:S(2)}) %all-to-all-start.3) | async-done | bytes 65568 | tf_op jit(solution)/shard_map/all_to_all | solution.py:206
  59.6 0.8 convolution_bitcast_fusion
  60.4 0.8 convolution_bitcast_fusion.1
  61.2 0.8 fusion.134
  62.0 0.8 fusion.114
  62.7 0.8 convolution_subtract_fusion.2
  63.5 0.8 convolution_add_fusion.2
  64.3 0.8 multiply_add_fusion.1
  67.6 11.5 %fusion.19 = f32[2,128,128]{2,1,0:T(8,128)S(1)} fusion(f32[2,256,128]{1,2,0:T(8,128)S(1)} %convolution_subtract_fusion.1, f32[2,256,128]{1,2,0:T(8,128)S(1)} %convolution_add_fusion.1, f32[256,128]{0,1:T(8,128)S(1)} %copy.206, f32[256,128]{0,1:T(8,128)S(1)} %copy.204), kind=kOutput, calls=%fused_computation.45 | convolution fusion | flops 101318656 | bytes 917504 | tf_op jit(solution)/shard_map/kt,nks->nts/dot_general | solution.py:96
  79.1 0.9 fusion.2
  80.9 4.8 all-to-all-start.4
  86.0 12.0 %all-to-all-done.4 = bf16[2,64,256]{2,0,1:T(2,128)(2,1)S(1)} async-done(((bf16[2,64,256]{2,0,1:T(2,128)(2,1)}), bf16[2,64,256]{2,0,1:T(2,128)(2,1)S(1)}, u32[]{:S(2)}, u32[]{:S(2)}) %all-to-all-start.4) | async-done | bytes 65568 | tf_op jit(solution)/shard_map/all_to_all | solution.py:211
  98.5 2.3 collective-permute-start.5
  101.9 6.0 %all-to-all-start.1 = ((bf16[64,2,256]{2,1,0:T(2,128)(2,1)}), bf16[64,2,256]{2,1,0:T(2,128)(2,1)S(1)}, u32[]{:S(2)}, u32[]{:S(2)}) async-start(bf16[64,2,256]{2,1,0:T(2,128)(2,1)} %all_to_all.63), calls=%async_computation.1 | async-start | bytes 131072 | tf_op jit(solution)/shard_map/all_to_all | solution.py:199
  108.0 2.4 collective-permute-start.4
  110.4 1.0 fusion.37
  111.4 2.1 collective-permute-done.4
  113.5 1.0 fusion.44
  114.5 5.6 %all-to-all-done.1 = bf16[64,2,256]{2,1,0:T(2,128)(2,1)S(1)} async-done(((bf16[64,2,256]{2,1,0:T(2,128)(2,1)}), bf16[64,2,256]{2,1,0:T(2,128)(2,1)S(1)}, u32[]{:S(2)}, u32[]{:S(2)}) %all-to-all-start.1) | async-done | bytes 65568 | tf_op jit(solution)/shard_map/all_to_all | solution.py:199
  120.2 0.8 convolution_bitcast_fusion.2
  121.0 0.8 convolution_bitcast_fusion.3
  121.8 0.8 fusion.119
  122.5 0.8 fusion.142
  123.3 0.8 convolution_subtract_fusion.4
  124.0 0.8 multiply_add_fusion
  127.4 0.9 fusion.12
  128.3 0.9 fusion.8
  130.0 7.0 %all-to-all-start.5 = ((bf16[2,64,256]{2,0,1:T(2,128)(2,1)}), bf16[2,64,256]{2,0,1:T(2,128)(2,1)S(1)}, u32[]{:S(2)}, u32[]{:S(2)}) async-start(bf16[2,64,256]{2,0,1:T(2,128)(2,1)} %copy.242), calls=%async_computation.5 | async-start | bytes 131072 | tf_op jit(solution)/shard_map/all_to_all | solution.py:212
  139.6 0.9 fusion.26
  140.5 0.9 fusion.4
  142.3 6.9 %all-to-all-done.5 = bf16[2,64,256]{2,0,1:T(2,128)(2,1)S(1)} async-done(((bf16[2,64,256]{2,0,1:T(2,128)(2,1)}), bf16[2,64,256]{2,0,1:T(2,128)(2,1)S(1)}, u32[]{:S(2)}, u32[]{:S(2)}) %all-to-all-start.5) | async-done | bytes 65568 | tf_op jit(solution)/shard_map/all_to_all | solution.py:212
  149.2 5.8 %all-to-all-start.2 = ((bf16[2,64,256]{2,0,1:T(2,128)(2,1)}), bf16[2,64,256]{2,0,1:T(2,128)(2,1)S(1)}, u32[]{:S(2)}, u32[]{:S(2)}) async-start(bf16[2,64,256]{2,0,1:T(2,128)(2,1)} %copy.223), calls=%async_computation.2 | async-start | bytes 131072 | tf_op jit(solution)/shard_map/all_to_all | solution.py:205
  156.2 99.6 %psum.15 = f32[64,33]{0,1:T(8,128)S(1)} all-reduce(f32[64,33]{0,1:T(8,128)S(1)} %fusion.423), channel_id=1, replica_groups=mesh['ctx'=64,'tp'=8] {'ctx','tp'}, use_global_device_ids=true, to_apply=%region_1.2 | all-reduce | flops 2112 | bytes 16896 | tf_op jit(solution)/shard_map/psum | solution.py:230
  255.8 270.7 %psum.14 = f32[128,64]{0,1:T(8,128)S(1)} all-reduce(f32[128,64]{0,1:T(8,128)S(1)} %fusion.417), channel_id=1, replica_groups=mesh['ctx'=64,'tp'=8] {'ctx'}, use_global_device_ids=true, to_apply=%region_0.1 | all-reduce | flops 8192 | bytes 65536 | tf_op jit(solution)/shard_map/psum | solution.py:229
  528.0 8.4 %collective-permute-start.3 = (bf16[128,6]{1,0:T(8,128)(2,1)S(1)}, bf16[128,6]{1,0:T(8,128)(2,1)S(1)}, u32[]{:S(2)}, u32[]{:S(2)}) collective-permute-start(bf16[128,6]{1,0:T(8,128)(2,1)S(1)} %slice.333), channel_id=1, source_target_pairs={{8,0},{16,8},{24,16},{32,24},{40,32},{48,40},{56,48},{64,56},{72,6... | collective-permute-start | bytes 4616 | tf_op jit(solution)/shard_map/ppermute | solution.py:14
  537.3 1.0 fusion.51
  (116 shorter events, 23.9 us)
Async XLA Ops:
  0.6 8.8 %copy-start = (f32[128,64]{0,1:T(8,128)S(1)}, f32[128,64]{0,1:T(8,128)}, u32[]{:S(2)}) copy-start(f32[128,64]{0,1:T(8,128)} %param.16) | copy-start | bytes 98308
  1.5 32.3 %collective-permute-start = (bf16[128,6]{1,0:T(8,128)(2,1)S(1)}, bf16[128,6]{1,0:T(8,128)(2,1)S(1)}, u32[]{:S(2)}, u32[]{:S(2)}) collective-permute-start(bf16[128,6]{1,0:T(8,128)(2,1)S(1)} %slice.242), channel_id=1, source_target_pairs={{0,8},{8,16},{16,24},{24,32},{32,40},{40,48},{48,56},{56,64},{64,7... | collective-permute-start | bytes 4616 | tf_op jit(solution)/shard_map/ppermute | solution.py:14
  7.5 0.7 copy-start.9
  8.2 0.7 copy-start.5
  8.2 0.7 copy-start.7
  10.4 15.5 %copy-start.3 = (bf16[128,256]{1,0:T(8,128)(2,1)S(1)}, bf16[128,256]{1,0:T(8,128)(2,1)}, u32[]{:S(2)}) copy-start(bf16[128,256]{1,0:T(8,128)(2,1)} %param.12) | copy-start | bytes 196612
  10.4 27.7 %all-to-all-start = ((bf16[64,2,256]{2,1,0:T(2,128)(2,1)}), bf16[64,2,256]{2,1,0:T(2,128)(2,1)S(1)}, u32[]{:S(2)}, u32[]{:S(2)}) async-start(bf16[64,2,256]{2,1,0:T(2,128)(2,1)} %all_to_all.60), calls=%async_computation | async-start | bytes 131072 | tf_op jit(solution)/shard_map/all_to_all | solution.py:200
  25.9 3.6 copy-start.4
  26.0 59.8 %collective-permute-start.2 = (bf16[128,6]{1,0:T(8,128)(2,1)S(1)}, bf16[128,6]{1,0:T(8,128)(2,1)S(1)}, u32[]{:S(2)}, u32[]{:S(2)}) collective-permute-start(bf16[128,6]{1,0:T(8,128)(2,1)S(1)} %slice.274), channel_id=1, source_target_pairs={{0,8},{8,16},{16,24},{24,32},{32,40},{40,48},{48,56},{56,64},{64,7... | collective-permute-start | bytes 4616 | tf_op jit(solution)/shard_map/ppermute | solution.py:14
  29.6 2.7 copy-start.6
  29.6 56.3 %collective-permute-start.1 = (bf16[128,6]{1,0:T(8,128)(2,1)S(1)}, bf16[128,6]{1,0:T(8,128)(2,1)S(1)}, u32[]{:S(2)}, u32[]{:S(2)}) collective-permute-start(bf16[128,6]{1,0:T(8,128)(2,1)S(1)} %slice.258), channel_id=1, source_target_pairs={{0,8},{8,16},{16,24},{24,32},{32,40},{40,48},{48,56},{56,64},{64,7... | collective-permute-start | bytes 4616 | tf_op jit(solution)/shard_map/ppermute | solution.py:14
  33.0 0.9 copy-start.2
  33.1 0.7 copy-start.8
  33.8 0.8 copy-start.1
  38.1 21.5 %all-to-all-start.3 = ((bf16[64,2,256]{2,1,0:T(2,128)(2,1)}), bf16[64,2,256]{2,1,0:T(2,128)(2,1)S(1)}, u32[]{:S(2)}, u32[]{:S(2)}) async-start(bf16[64,2,256]{2,1,0:T(2,128)(2,1)} %all_to_all.67), calls=%async_computation.3 | async-start | bytes 131072 | tf_op jit(solution)/shard_map/all_to_all | solution.py:206
  80.9 17.0 %all-to-all-start.4 = ((bf16[2,64,256]{2,0,1:T(2,128)(2,1)}), bf16[2,64,256]{2,0,1:T(2,128)(2,1)S(1)}, u32[]{:S(2)}, u32[]{:S(2)}) async-start(bf16[2,64,256]{2,0,1:T(2,128)(2,1)} %copy.236), calls=%async_computation.4 | async-start | bytes 131072 | tf_op jit(solution)/shard_map/all_to_all | solution.py:211
  98.5 11.8 %collective-permute-start.5 = (bf16[128,6]{1,0:T(8,128)(2,1)S(1)}, bf16[128,6]{1,0:T(8,128)(2,1)S(1)}, u32[]{:S(2)}, u32[]{:S(2)}) collective-permute-start(bf16[128,6]{1,0:T(8,128)(2,1)S(1)} %slice.349), channel_id=1, source_target_pairs={{8,0},{16,8},{24,16},{32,24},{40,32},{48,40},{56,48},{64,56},{72,6... | collective-permute-start | bytes 4616 | tf_op jit(solution)/shard_map/ppermute | solution.py:14
  101.9 18.2 %all-to-all-start.1 = ((bf16[64,2,256]{2,1,0:T(2,128)(2,1)}), bf16[64,2,256]{2,1,0:T(2,128)(2,1)S(1)}, u32[]{:S(2)}, u32[]{:S(2)}) async-start(bf16[64,2,256]{2,1,0:T(2,128)(2,1)} %all_to_all.63), calls=%async_computation.1 | async-start | bytes 131072 | tf_op jit(solution)/shard_map/all_to_all | solution.py:199
  108.0 5.5 %collective-permute-start.4 = (bf16[128,6]{1,0:T(8,128)(2,1)S(1)}, bf16[128,6]{1,0:T(8,128)(2,1)S(1)}, u32[]{:S(2)}, u32[]{:S(2)}) collective-permute-start(bf16[128,6]{1,0:T(8,128)(2,1)S(1)} %slice.341), channel_id=1, source_target_pairs={{8,0},{16,8},{24,16},{32,24},{40,32},{48,40},{56,48},{64,56},{72,6... | collective-permute-start | bytes 4616 | tf_op jit(solution)/shard_map/ppermute | solution.py:14
  130.0 19.1 %all-to-all-start.5 = ((bf16[2,64,256]{2,0,1:T(2,128)(2,1)}), bf16[2,64,256]{2,0,1:T(2,128)(2,1)S(1)}, u32[]{:S(2)}, u32[]{:S(2)}) async-start(bf16[2,64,256]{2,0,1:T(2,128)(2,1)} %copy.242), calls=%async_computation.5 | async-start | bytes 131072 | tf_op jit(solution)/shard_map/all_to_all | solution.py:212
  149.2 378.0 %all-to-all-start.2 = ((bf16[2,64,256]{2,0,1:T(2,128)(2,1)}), bf16[2,64,256]{2,0,1:T(2,128)(2,1)S(1)}, u32[]{:S(2)}, u32[]{:S(2)}) async-start(bf16[2,64,256]{2,0,1:T(2,128)(2,1)} %copy.223), calls=%async_computation.2 | async-start | bytes 131072 | tf_op jit(solution)/shard_map/all_to_all | solution.py:205
  528.0 9.3 %collective-permute-start.3 = (bf16[128,6]{1,0:T(8,128)(2,1)S(1)}, bf16[128,6]{1,0:T(8,128)(2,1)S(1)}, u32[]{:S(2)}, u32[]{:S(2)}) collective-permute-start(bf16[128,6]{1,0:T(8,128)(2,1)S(1)} %slice.333), channel_id=1, source_target_pairs={{8,0},{16,8},{24,16},{32,24},{40,32},{48,40},{56,48},{64,56},{72,6... | collective-permute-start | bytes 4616 | tf_op jit(solution)/shard_map/ppermute | solution.py:14
where the time goes:
time: 544 us; the launch traced here: 539 us
  blocking collectives  370 us (68%)
  starting transfers between devices  72.2 us (13%)
  matrix products  39.1 us (7%)
  waiting for transfers between devices  37.1 us (7%)
  other arithmetic  9.16 us (2%)
  local copies, waits for them, and re-layouts  8.96 us (2%)
    psum x1, blocking collectives, on_device(): grad_proj = lax.psum(part_proj, 'ctx') * proj_scale  271 us
    psum x1, blocking collectives, on_device(): grad_basis = lax.psum(part_basis, ('ctx', 'tp')) * basis_scale  99.6 us
    ppermute x6, starting transfers between devices, passed_along(): lax.ppermute(value, axis, [(source, source + steps) for source in range(l...  23.4 us
    all_to_all x1, starting transfers between devices, on_device(): lax.all_to_all(filter_tok, 'ctx', split_axis=0, concat_axis=1, tiled=True)  15.5 us
    dot_general x3, matrix products, restore(): jnp.einsum('kt,nks->nts', outer[0], turned_re, precision=PRECISE)  13.3 us
    all_to_all x1, waiting for transfers between devices, on_device(): lax.all_to_all(carried_grad_chan, 'ctx', split_axis=1, concat_axis=0, til...  12 us
  transfers between devices with their start and end apart: 12, of which 7 were waited for; matrix products, arithmetic and copies ran while one was open for 7% of the time, Pallas kernels for 0%

commit v1 on v0

v1 whole, which is shorter than its diff:
```python
import math

import jax
import jax.numpy as jnp
import numpy as np
from jax import lax
from jax.experimental import pallas as pl
from jax.experimental.pallas import tpu as pltpu
from jax.sharding import Mesh
from jax.sharding import PartitionSpec as P
import ml_dtypes

F32 = jnp.float32
BF16 = jnp.bfloat16
EXACT = lax.Precision.HIGHEST

ROWS = 64
COLS = 256
TOTAL = ROWS * COLS
FEAT = 64
EMB = 33
TAPS = 7
CHAN = 2
GROUP = 40
TURN = 1.0 / (2.0 * math.pi)

SIN_COEF = (
    6.2831854820251465,
    -41.34170150756836,
    81.60513305664062,
    -76.70301818847656,
    42.02592849731445,
    -14.899847030639648,
    3.2381374835968018,
)
COS_COEF = (
    1.0,
    -19.73920440673828,
    64.93911743164062,
    -85.45014190673828,
    60.16762924194336,
    -25.967599868774414,
    6.528658390045166,
)


def halves(table, count):
    parts = []
    rest = np.asarray(table, np.float64)
    for _ in range(count):
        part = rest.astype(np.float32).astype(ml_dtypes.bfloat16)
        parts.append(part)
        rest = rest - part.astype(np.float64)
    return parts


def transform_tables():
    rows = np.arange(ROWS)
    cols = np.arange(COLS)
    first = 2.0 * np.pi * ((4 * rows[:, None] + 1) * rows[None, :] % (4 * ROWS)) / (4 * ROWS)
    first_re, first_im = np.cos(first), -np.sin(first)
    forward = np.concatenate([first_re, first_im], axis=0)
    forward_cat = np.concatenate(halves(forward, 2), axis=1)
    last = np.concatenate([first_re.T, -first_im.T], axis=1) / TOTAL
    last_hi, last_lo = halves(last, 2)
    last_cat = np.concatenate([last_hi, last_lo, last_hi], axis=1)
    turn = 2.0 * np.pi * ((4 * rows[:, None] + 1) * cols[None, :]) / (4 * TOTAL)
    twiddle = np.stack([np.cos(turn), -np.sin(turn)]).astype(np.float32)
    inner = 2.0 * np.pi * (cols[:, None] * cols[None, :] % COLS) / COLS
    inner_re, inner_im = np.cos(inner), -np.sin(inner)
    full = np.concatenate(
        [
            np.concatenate([inner_re, inner_im], axis=1),
            np.concatenate([-inner_im, inner_re], axis=1),
        ],
        axis=0,
    )
    full_hi, full_lo = halves(full, 2)
    return forward_cat, last_cat, twiddle, np.stack([full_hi, full_lo])


def basis_tables():
    freq = np.arange(1, 17)
    cols = np.arange(COLS)
    rows = np.arange(ROWS)
    inner = 2.0 * np.pi * (freq[:, None] * cols[None, :] % TOTAL) / TOTAL
    short = np.concatenate(
        [np.cos(inner), np.sin(inner), cols[None, :] / TOTAL, np.ones((1, COLS))], axis=0
    )
    width = short.shape[0]
    hi, mid, lo = halves(short, 3)
    right = np.zeros((256, COLS), ml_dtypes.bfloat16)
    for place, part in ((0, hi), (GROUP, hi), (2 * GROUP, hi)):
        right[place : place + width] = part
    for place, part in ((128, mid), (128 + GROUP, lo), (128 + 2 * GROUP, mid)):
        right[place : place + width] = part
    outer = 2.0 * np.pi * (freq[None, :] * rows[:, None] % ROWS) / ROWS
    cos_out, sin_out = np.cos(outer), np.sin(outer)
    one = np.ones((ROWS, 1))
    block = rows[:, None] / ROWS
    cos_row = np.concatenate([cos_out, cos_out, one, one], axis=1)
    sin_row = np.concatenate([sin_out, sin_out, 0 * one, block], axis=1)
    turn = np.zeros((2, ROWS, 128), np.float32)
    for place in (0, GROUP, 2 * GROUP):
        turn[0, :, place : place + width] = cos_row
        turn[1, :, place : place + width] = sin_row
    pick = np.zeros((2, 128, 128), np.float32)
    for place in (0, GROUP, 2 * GROUP):
        for index in range(16):
            pick[0, 2 * index + 1, place + index] = 1.0
            pick[0, 2 * index + 2, place + 16 + index] = 1.0
            pick[1, 2 * index + 2, place + index] = 1.0
            pick[1, 2 * index + 1, place + 16 + index] = -1.0
        pick[0, 0, place + 32] = 1.0
        pick[0, EMB, place + 33] = 1.0
        pick[1, 0, place + 33] = 1.0
    back = np.zeros((COLS, 128))
    back[:, :width] = short.T
    back[:, 64:80] = short[16:32].T
    back[:, 80:96] = short[:16].T
    back_hi, back_lo = halves(back, 2)
    back_cat = np.concatenate([back_hi, back_lo], axis=1)
    back_turn = np.zeros((ROWS, 128), np.float32)
    back_turn[:, :32] = cos_row[:, :32]
    back_turn[:, 32] = 1.0
    back_turn[:, 33] = rows / ROWS
    back_turn[:, 64:80] = -sin_out
    back_turn[:, 80:96] = sin_out
    place = np.zeros((8, 8, 128), np.float32)
    for wanted in range(EMB):
        row, group = divmod(wanted, 8)
        if wanted == 0:
            lanes = (32, 33)
        elif wanted % 2:
            lanes = ((wanted - 1) // 2, 64 + (wanted - 1) // 2)
        else:
            lanes = (16 + (wanted - 2) // 2, 80 + (wanted - 2) // 2)
        for lane in lanes:
            place[group, row, lane] = 1.0
    return right, turn, pick, back_cat, back_turn, place


def split(value):
    hi = value.astype(BF16)
    lo = (value - hi.astype(F32)).astype(BF16)
    return hi, lo


def dot(left, right):
    return jnp.dot(left, right, preferred_element_type=F32)


def spectrum(signals, forward, twiddle_re, twiddle_im, full_hi, full_lo):
    wide = jnp.concatenate(signals, axis=1)
    section = dot(forward, jnp.concatenate([wide, wide], axis=0))
    turned = []
    for index in range(len(signals)):
        part = section[:, index * COLS : (index + 1) * COLS]
        part_re, part_im = part[:ROWS], part[ROWS:]
        turned.append(
            jnp.concatenate(
                [
                    part_re * twiddle_re - part_im * twiddle_im,
                    part_re * twiddle_im + part_im * twiddle_re,
                ],
                axis=1,
            )
        )
    return full_product(jnp.concatenate(turned, axis=0), full_hi, full_lo)


def full_product(value, full_hi, full_lo):
    hi, lo = split(value)
    return dot(hi, full_hi) + dot(lo, full_hi) + dot(hi, full_lo)


def restore(conj_spec, count, last, twiddle_re, twiddle_im, full_hi, full_lo):
    back = full_product(conj_spec, full_hi, full_lo)
    stacked = []
    for index in range(count):
        part = back[index * ROWS : (index + 1) * ROWS]
        part_re, part_im = part[:, :COLS], part[:, COLS:]
        stacked.append(
            jnp.concatenate(
                [
                    part_re * twiddle_re - part_im * twiddle_im,
                    part_re * twiddle_im + part_im * twiddle_re,
                ],
                axis=0,
            )
        )
    hi, lo = split(jnp.concatenate(stacked, axis=1))
    result = dot(last, jnp.concatenate([hi, hi, lo], axis=0))
    return [result[:, index * COLS : (index + 1) * COLS] for index in range(count)]


def take(ref, start, count, stride):
    return jnp.concatenate(
        [ref[half, pl.ds(start, count, stride=stride), :] for half in range(2)], axis=1
    )


def put(ref, start, count, stride, value):
    for half in range(2):
        ref[half, pl.ds(start, count, stride=stride), :] = value[:, half * 128 : half * 128 + 128]


def fill(ref, value):
    for half in range(2):
        ref[half] = value[..., half * 128 : half * 128 + 128].reshape(ref.shape[1], 128)


def pack_kernel(query, key, value, grad, out, wide):
    for index, ref in enumerate((query, key, value, grad)):
        value = ref[...].astype(F32)
        for half in range(2):
            wide[half, index * 128 : (index + 1) * 128, :] = value[:, half * 128 : half * 128 + 128]
    for peer in range(ROWS):
        out[peer] = take(wide, peer, 8, ROWS).astype(BF16)


def filter_kernel(
    own,
    decay,
    norm,
    layer,
    proj,
    pick,
    turn,
    right,
    forward,
    twiddle,
    full,
    act_out,
    cos_out,
    env_out,
    spec_out,
    column_out,
    left,
    phase,
    filt,
):
    first = own[0]
    layer_all = layer[...]
    same = jnp.dot(layer_all, pick[0], precision=EXACT, preferred_element_type=F32) * TURN
    cross = jnp.dot(layer_all, pick[1], precision=EXACT, preferred_element_type=F32) * TURN
    lane = lax.broadcasted_iota(jnp.int32, (FEAT, 128), 1)
    sublane = lax.broadcasted_iota(jnp.int32, (8, 128), 0)
    proj_turned = proj[...].T
    columns = []
    for chan in range(CHAN):
        hit = lane == first + 64 * chan
        column = jnp.sum(jnp.where(hit, proj_turned, 0.0), axis=1, keepdims=True)
        column_wide = jnp.broadcast_to(column, (FEAT, 128))
        column_out[chan * FEAT : (chan + 1) * FEAT, :] = column_wide
        columns.append(column_wide)

    def make_left(block, carry):
        value = same * turn[0, pl.ds(block, 1), :] + cross * turn[1, pl.ds(block, 1), :]
        hi = value.astype(BF16).astype(F32)
        rest = value - hi
        mid = rest.astype(BF16).astype(F32)
        lo = rest - mid
        one = jnp.where(lane < GROUP, hi, jnp.where(lane < 2 * GROUP, mid, lo))
        two = jnp.where(lane < 2 * GROUP, hi, mid)
        start = pl.multiple_of(block * FEAT, FEAT)
        left[pl.ds(start, FEAT), 0:128] = one.astype(BF16)
        left[pl.ds(start, FEAT), 128:256] = two.astype(BF16)
        return carry

    lax.fori_loop(0, ROWS, make_left, 0, unroll=2)

    def chunk(index, carry):
        base = pl.multiple_of(index * 512, 512)
        phase[...] = dot(left[pl.ds(base, 512), :], right[...])

        def one_block(inner, sums):
            near = pl.multiple_of(inner * FEAT, FEAT)
            kept = []
            for half in range(2):
                lanes = slice(half * 128, half * 128 + 128)
                turns = phase[pl.ds(near, FEAT), lanes]
                rest = turns - jnp.round(turns)
                square = rest * rest
                sine = jnp.full_like(rest, SIN_COEF[-1])
                cosine = jnp.full_like(rest, COS_COEF[-1])
                for coef in SIN_COEF[-2::-1]:
                    sine = sine * square + coef
                for coef in COS_COEF[-2::-1]:
                    cosine = cosine * square + coef
                sine = sine * rest
                act_out[pl.ds(base + near, FEAT), lanes] = sine.astype(BF16)
                cos_out[pl.ds(base + near, FEAT), lanes] = cosine.astype(BF16)
                for chan in range(CHAN):
                    total = jnp.sum(sine * columns[chan], axis=0, keepdims=True)
                    kept.append(jnp.where(sublane == inner, total, sums[2 * half + chan]))
            return tuple(kept)

        sums = lax.fori_loop(0, 8, one_block, (jnp.zeros((8, 128), F32),) * 4)
        for half in range(2):
            for chan in range(CHAN):
                start = pl.multiple_of(chan * ROWS + index * 8, 8)
                filt[pl.ds(start, 8), half * 128 : half * 128 + 128] = sums[2 * half + chan]
        return carry

    lax.fori_loop(0, 8, chunk, 0)
    position = (
        lax.broadcasted_iota(jnp.int32, (ROWS, COLS), 0) * COLS
        + lax.broadcasted_iota(jnp.int32, (ROWS, COLS), 1)
    ).astype(F32)
    signals = []
    for chan in range(CHAN):
        rate = decay[first + 64 * chan]
        envelope = jnp.exp(-(rate * position) * (1.0 / TOTAL)) * norm[first + 64 * chan]
        env_out[chan * ROWS : (chan + 1) * ROWS, :] = envelope
        signals.append((filt[chan * ROWS : (chan + 1) * ROWS, :] * envelope).astype(BF16))
    spec_out[...] = spectrum(signals, forward[...], twiddle[0], twiddle[1], full[0], full[1])


def own_taps(first, short, taps, order):
    lane = lax.broadcasted_iota(jnp.int32, (8, 128), 1)
    taps[...] = jnp.where(lane == 0, 1.0, 0.0)
    for place, which in order:
        for chan in range(CHAN):
            taps[place + chan : place + chan + 1, 0:TAPS] = short[which, pl.ds(first + 64 * chan, 1), :]
    return taps[...]


def gradient_kernel(
    own,
    arrived,
    short,
    act,
    cosine,
    envelope,
    columns,
    back,
    back_turn,
    place,
    forward,
    last,
    twiddle,
    full,
    feat_out,
    spec_out,
    signal_out,
    proj_out,
    basis_out,
    taps,
    raw,
    raw_turned,
    part,
    product,
    proj_product,
):
    first = own[0]
    weights = own_taps(first, short, taps, ((0, 0), (2, 1), (4, 2)))
    signal = arrived[...].astype(F32)
    lane = lax.broadcasted_iota(jnp.int32, (ROWS, 8, COLS), 2)
    result = weights[None, :, 0:1] * signal
    zeros = jnp.zeros((1, 8, COLS), F32)
    for offset in range(1, TAPS):
        moved = pltpu.roll(signal, offset, 2)
        before = jnp.concatenate([zeros, moved[:-1]], axis=0)
        shifted = jnp.where(lane < offset, before, moved)
        result = result + weights[None, :, offset : offset + 1] * shifted
    fill(feat_out, result)

    def plane(index):
        return take(feat_out, index, ROWS, 8)

    signals = []
    for chan in range(CHAN):
        signals.append((plane(2 + chan) * plane(4 + chan)).astype(BF16))
    for chan in range(CHAN):
        signals.append((plane(chan) * plane(6 + chan)).astype(BF16))
    for index in range(4):
        signal_out[index] = signals[index].astype(F32)
    tables = (twiddle[0], twiddle[1], full[0], full[1])
    spec = spectrum(signals, forward[...], *tables)
    spec_out[...] = spec
    carried, grad = spec[: CHAN * ROWS], spec[CHAN * ROWS :]
    carried_re, carried_im = carried[:, :COLS], carried[:, COLS:]
    grad_re, grad_im = grad[:, :COLS], grad[:, COLS:]
    crossed = jnp.concatenate(
        [
            carried_re * grad_re + carried_im * grad_im,
            carried_im * grad_re - carried_re * grad_im,
        ],
        axis=1,
    )
    filter_grad = restore(crossed, CHAN, last[...], *tables)
    for chan in range(CHAN):
        rounded = filter_grad[chan].astype(BF16).astype(F32)
        scaled = rounded * envelope[chan * ROWS : (chan + 1) * ROWS, :]
        for half in range(2):
            raw[half, chan * ROWS : (chan + 1) * ROWS, :] = scaled[:, half * 128 : half * 128 + 128]
    raw_hi, raw_lo = split(jnp.concatenate([raw[half].T for half in range(2)], axis=0))
    raw_turned[:, 0:128] = raw_hi
    raw_turned[:, 128:256] = raw_lo
    column0 = columns[0:FEAT, :]
    column1 = columns[FEAT : 2 * FEAT, :]
    wide_lane = lax.broadcasted_iota(jnp.int32, (FEAT, COLS), 1) % ROWS

    def chunk(index, carry):
        base = pl.multiple_of(index * 512, 512)

        def one_block(inner, carry):
            near = pl.multiple_of(inner * FEAT, FEAT)
            block = index * 8 + inner
            for half in range(2):
                lanes = slice(half * 128, half * 128 + 128)
                value = (
                    column0 * raw[half, pl.ds(block, 1), :]
                    + column1 * raw[half, pl.ds(ROWS + block, 1), :]
                )
                value = value * cosine[pl.ds(base + near, FEAT), lanes].astype(F32)
                part[pl.ds(near, FEAT), lanes] = value.astype(BF16)
            return carry

        lax.fori_loop(0, 8, one_block, 0)
        product[...] = dot(part[...], back[...])
        proj_product[...] = dot(act[pl.ds(base, 512), :], raw_turned[...])

        def gather(inner, carry):
            basis_sum, proj_sum = carry
            near = pl.multiple_of(inner * FEAT, FEAT)
            block = index * 8 + inner
            angle = back_turn[pl.ds(block, 1), :]
            both = product[pl.ds(near, FEAT), 0:128] + product[pl.ds(near, FEAT), 128:256]
            basis_sum = basis_sum + both * angle
            proj_sum = proj_sum + jnp.where(
                wide_lane == block, proj_product[pl.ds(near, FEAT), :], 0.0
            )
            return basis_sum, proj_sum

        return lax.fori_loop(0, 8, gather, carry)

    basis_sum, proj_sum = lax.fori_loop(
        0, 8, chunk, (jnp.zeros((FEAT, 128), F32), jnp.zeros((FEAT, COLS), F32))
    )
    proj_both = proj_sum[:, 0:128] + proj_sum[:, 128:256]
    lane128 = lax.broadcasted_iota(jnp.int32, (FEAT, 128), 1)
    stacked = jnp.concatenate(
        [
            jnp.where(lane128 < ROWS, proj_both, 0.0),
            jnp.where(lane128 >= ROWS, proj_both, 0.0),
        ],
        axis=0,
    )
    proj_out[...] = lax.dot_general(
        jnp.ones((8, 128), F32),
        stacked,
        (((1,), (1,)), ((), ())),
        precision=EXACT,
        preferred_element_type=F32,
    )
    pieces = [
        lax.dot_general(
            place[group],
            basis_sum,
            (((1,), (1,)), ((), ())),
            precision=EXACT,
            preferred_element_type=F32,
        )
        for group in range(8)
    ]
    for core in range(2):
        row = jnp.concatenate([piece[:, core * 32 : core * 32 + 32] for piece in pieces], axis=1)
        for peer in range(8):
            basis_out[core * 8 + peer] = row


def output_kernel(
    own,
    skip,
    short,
    feat,
    spec,
    filter_spec,
    signals,
    proj_row,
    basis_parts,
    last,
    twiddle,
    full,
    out,
    taps,
    mate,
):
    first = own[0]
    weights = own_taps(first, short, taps, ((2, 2), (4, 1), (6, 0)))
    tables = (twiddle[0], twiddle[1], full[0], full[1])
    carried, grad = spec[0 : CHAN * ROWS, :], spec[CHAN * ROWS : 2 * CHAN * ROWS, :]
    filt = filter_spec[...]
    carried_re, carried_im = carried[:, :COLS], carried[:, COLS:]
    grad_re, grad_im = grad[:, :COLS], grad[:, COLS:]
    filt_re, filt_im = filt[:, :COLS], filt[:, COLS:]
    crossed = jnp.concatenate(
        [
            jnp.concatenate(
                [
                    filt_re * carried_re - filt_im * carried_im,
                    -(filt_re * carried_im + filt_im * carried_re),
                ],
                axis=1,
            ),
            jnp.concatenate(
                [
                    filt_re * grad_re + filt_im * grad_im,
                    filt_im * grad_re - filt_re * grad_im,
                ],
                axis=1,
            ),
        ],
        axis=0,
    )
    sums = restore(crossed, 2 * CHAN, last[...], *tables)
    for chan in range(CHAN):
        gain = skip[first + 64 * chan]
        long_out = (sums[chan] + gain * signals[chan]).astype(BF16).astype(F32)
        carried_grad = (sums[CHAN + chan] + gain * signals[CHAN + chan]).astype(BF16).astype(F32)
        put(mate, chan, ROWS, 8, long_out)
        put(mate, 2 + chan, ROWS, 8, carried_grad)
        put(mate, 4 + chan, ROWS, 8, carried_grad)
        put(mate, 6 + chan, ROWS, 8, long_out)
    signal = jnp.concatenate(
        [(feat[half] * mate[half]).astype(BF16).astype(F32).reshape(ROWS, 8, 128) for half in range(2)],
        axis=2,
    )
    lane = lax.broadcasted_iota(jnp.int32, (ROWS, 8, COLS), 2)
    result = weights[None, :, 0:1] * signal
    zeros = jnp.zeros((1, 8, COLS), F32)
    for offset in range(1, TAPS):
        moved = pltpu.roll(signal, COLS - offset, 2)
        after = jnp.concatenate([moved[1:], zeros], axis=0)
        shifted = jnp.where(lane >= COLS - offset, after, moved)
        result = result + weights[None, :, offset : offset + 1] * shifted
    basis = basis_parts[0]
    for source in range(1, 16):
        basis = basis + basis_parts[source]
    proj_wide = proj_row[...]
    proj_hi = proj_wide.astype(BF16).astype(F32)
    proj_lo = proj_wide - proj_hi
    row = lax.broadcasted_iota(jnp.int32, (8, COLS), 0)
    extra = jnp.where(row == 7, jnp.concatenate([proj_hi, proj_lo], axis=1), basis)
    wide = jnp.concatenate([result, jnp.broadcast_to(extra[None], (ROWS, 8, COLS))], axis=1)
    out[...] = wide.astype(BF16)


def unpack_kernel(arrived, mixed, grad_query, grad_key, grad_value, proj, basis, wide):
    fill(wide, arrived[...].astype(F32))
    for ref, start in ((mixed, 0), (grad_value, 2), (grad_key, 4), (grad_query, 6)):
        for chan in range(CHAN):
            ref[chan * ROWS : (chan + 1) * ROWS, :] = take(wide, start + chan, ROWS, 16).astype(BF16)
    last = take(wide, 15, ROWS, 16)
    both = (last[:, 0:128] + last[:, 128:256]) * (1.0 / math.sqrt(TOTAL))
    proj[0:ROWS, :] = both[:, 0:64]
    proj[ROWS : 2 * ROWS, :] = both[:, 64:128]
    for core in range(2):
        for half in range(2):
            total = wide[half, core * 16 + 8 : core * 16 + 16, :]
            for source in range(core + 2, ROWS, 2):
                total = total + wide[half, source * 16 + 8 : source * 16 + 16, :]
            basis[core, :, half * 128 : half * 128 + 128] = total


SMEM = pl.BlockSpec(memory_space=pltpu.SMEM)
VMEM = pl.BlockSpec(memory_space=pltpu.VMEM)


def call(kernel, name, scalars, args, outs, scratch, flops, moved):
    return pl.pallas_call(
        kernel,
        name=name,
        in_specs=[SMEM] * len(scalars) + [VMEM] * len(args),
        out_specs=[VMEM] * len(outs) if isinstance(outs, list) else VMEM,
        out_shape=outs,
        scratch_shapes=scratch,
        compiler_params=pltpu.CompilerParams(vmem_limit_bytes=48 * 1024 * 1024),
        cost_estimate=pl.CostEstimate(flops=flops, bytes_accessed=moved, transcendentals=0),
    )(*scalars, *args)


def shape(dims, kind=F32):
    return jax.ShapeDtypeStruct(dims, kind)


def run_pack(query_in, key_in, value_in, grad_out):
    return call(
        pack_kernel,
        "pack",
        [],
        [query_in, key_in, value_in, grad_out],
        shape((ROWS, 8, COLS), BF16),
        [pltpu.VMEM((2, 512, 128), F32)],
        1 << 20,
        1 << 19,
    )


def run_filter(own, decay, norm, layer, proj, consts):
    return call(
        filter_kernel,
        "filter",
        [own, decay, norm],
        [layer, proj, consts["pick"], consts["turn"], consts["right"], consts["forward"], consts["twiddle"], consts["full"]],
        [
            shape((ROWS * FEAT, COLS), BF16),
            shape((ROWS * FEAT, COLS), BF16),
            shape((CHAN * ROWS, COLS)),
            shape((CHAN * ROWS, 2 * COLS)),
            shape((CHAN * FEAT, 128)),
        ],
        [
            pltpu.VMEM((ROWS * FEAT, COLS), BF16),
            pltpu.VMEM((512, COLS), F32),
            pltpu.VMEM((CHAN * ROWS, COLS), F32),
        ],
        1 << 33,
        1 << 23,
    )


def run_gradient(own, arrived, short, act, cosine, envelope, columns, consts):
    return call(
        gradient_kernel,
        "gradient",
        [own],
        [arrived, short, act, cosine, envelope, columns, consts["back"], consts["back_turn"], consts["place"], consts["forward"], consts["last"], consts["twiddle"], consts["full"]],
        [
            shape((2, ROWS * 8, 128)),
            shape((2 * CHAN * ROWS, 2 * COLS)),
            shape((2 * CHAN, ROWS, COLS)),
            shape((8, 128)),
            shape((16, 8, COLS)),
        ],
        [
            pltpu.VMEM((8, 128), F32),
            pltpu.VMEM((2, CHAN * ROWS, 128), F32),
            pltpu.VMEM((COLS, COLS), BF16),
            pltpu.VMEM((512, COLS), BF16),
            pltpu.VMEM((512, COLS), F32),
            pltpu.VMEM((512, COLS), F32),
        ],
        1 << 32,
        1 << 23,
    )


def run_output(own, skip, short, feat, spec, filter_spec, signals, proj_row, basis_parts, consts):
    return call(
        output_kernel,
        "output",
        [own, skip],
        [short, feat, spec, filter_spec, signals, proj_row, basis_parts, consts["last"], consts["twiddle"], consts["full"]],
        shape((ROWS, 16, COLS), BF16),
        [pltpu.VMEM((8, 128), F32), pltpu.VMEM((2, ROWS * 8, 128), F32)],
        1 << 31,
        1 << 22,
    )


def run_unpack(arrived):
    block = shape((128, COLS), BF16)
    return call(
        unpack_kernel,
        "unpack",
        [],
        [arrived],
        [block, block, block, block, shape((128, FEAT)), shape((2, 8, COLS))],
        [pltpu.VMEM((2, ROWS * 16, 128), F32)],
        1 << 20,
        1 << 20,
    )


def make_consts():
    forward, last, twiddle, full = transform_tables()
    right, turn, pick, back, back_turn, place = basis_tables()
    return dict(
        forward=jnp.asarray(forward),
        last=jnp.asarray(last),
        twiddle=jnp.asarray(twiddle),
        full=jnp.asarray(full),
        right=jnp.asarray(right),
        turn=jnp.asarray(turn),
        pick=jnp.asarray(pick),
        back=jnp.asarray(back),
        back_turn=jnp.asarray(back_turn),
        place=jnp.asarray(place),
    )


def filter_params(basis_weight, basis_bias, decay_rate):
    energy = jnp.expm1(-2.0 * decay_rate) / jnp.expm1(-2.0 * decay_rate / TOTAL)
    norm = 1.0 / jnp.sqrt(energy)
    layer = jnp.pad(
        jnp.concatenate([basis_weight, basis_bias[:, None]], axis=1), ((0, 0), (0, 128 - EMB - 1))
    )
    return norm, layer


CTX = ("zh", "y", "core")
PAIR = ("core", "x", "zl")


def exchange(value, axes):
    return lax.all_to_all(value, axes, split_axis=0, concat_axis=0, tiled=True)


def on_device(
    query_in,
    key_in,
    value_in,
    short_kernel,
    basis_weight,
    basis_bias,
    filter_proj,
    decay_rate,
    skip_gain,
    grad_out,
):
    consts = make_consts()
    own = lax.axis_index(CTX).astype(jnp.int32).reshape(1)
    with jax.named_scope("spread"):
        arrived = exchange(run_pack(query_in, key_in, value_in, grad_out), CTX)
    norm, layer = filter_params(basis_weight, basis_bias, decay_rate)
    act, cosine, envelope, filter_spec, columns = run_filter(
        own, decay_rate, norm, layer, filter_proj, consts
    )
    feat, spec, signals, proj_row, basis_own = run_gradient(
        own, arrived, short_kernel, act, cosine, envelope, columns, consts
    )
    with jax.named_scope("basis"):
        basis_parts = exchange(basis_own, PAIR)
    packed = run_output(
        own, skip_gain, short_kernel, feat, spec, filter_spec, signals, proj_row, basis_parts, consts
    )
    with jax.named_scope("collect"):
        returned = exchange(packed, CTX)
    mixed, grad_query, grad_key, grad_value, grad_proj, basis_sum = run_unpack(returned)
    grad_basis = (
        basis_sum.reshape(2, 8, 8, 32).transpose(0, 3, 1, 2).reshape(FEAT, 64)[:, :EMB]
        * math.sqrt(FEAT / (TOTAL * 1024))
    )
    return (mixed, grad_query, grad_key, grad_value, grad_proj, grad_basis)


def solution(mesh):
    finer = Mesh(mesh.devices.reshape(4, 8, 2, 4, 2), ("zh", "y", "core", "x", "zl"))
    rows = ("x", "zl")
    block = P(rows, CTX)
    return jax.shard_map(
        on_device,
        mesh=finer,
        in_specs=(
            block,
            block,
            block,
            P(None, rows, None),
            P(),
            P(),
            P(rows, None),
            P(rows),
            P(rows),
            block,
        ),
        out_specs=(block, block, block, block, P(rows, None), P()),
        check_vma=False,
    )
```

time: 544 us -> 105 us (0.19)
  blocking collectives: 370 us -> 43.1 us
  starting transfers between devices: 72.2 us -> 17.6 us
  matrix products: 39.1 us -> 0 us
  waiting for transfers between devices: 37.1 us -> 0.01 us
  Pallas kernels: 0 us -> 24.4 us
  other arithmetic: 9.16 us -> 1.36 us
  local copies, waits for them, and re-layouts: 8.96 us -> 16.6 us
    psum x2 -> x0, blocking collectives: 370 us -> none  [the longest x1 271 us: on_device(): grad_proj = lax.psum(part_proj, 'ctx') * proj_scale]
    all_to_all x0 -> x2, blocking collectives: none -> 43.1 us  [exchange(): return lax.all_to_all(value, axes, split_axis=0, concat_axis=0, tiled=True)]
    dot_general x41 -> x0, matrix products: 39.1 us -> none  [the longest x3 13.3 us: restore(): jnp.einsum('kt,nks->nts', outer[0], turned_re, precision=PRECISE)]
    all_to_all x6 -> x1, waiting for transfers between devices: 34.7 us -> 0.01 us  [exchange(): return lax.all_to_all(value, axes, split_axis=0, concat_axis=0, tiled=True)]
    all_to_all x6 -> x1, starting transfers between devices: 48.8 us -> 17.6 us  [exchange(): return lax.all_to_all(value, axes, split_axis=0, concat_axis=0, tiled=True)]
    pallas_call x0 -> x5, Pallas kernels: none -> 24.4 us  [call(): pl.pallas_call(kernel, name=name, in_specs=[SMEM] * len(scalars) + [VMEM]...]
    ppermute x6 -> x0, starting transfers between devices: 23.4 us -> none  [passed_along(): lax.ppermute(value, axis, [(source, source + steps) for source in range(l...]
    unnamed x20 -> x46, local copies, waits for them, and re-layouts: 2.66 us -> 15.7 us
  transfers between devices with their start and end apart: 12 -> 1, of which waited for: 7 -> 0; matrix products, arithmetic and copies ran while one was open for 7% -> 4% of each run, Pallas kernels for 0% -> 11%
where the time goes in v1:
time: 105 us; the launch traced here: 104 us
  blocking collectives  43.1 us (41%)
  Pallas kernels  24.4 us (23%)
  starting transfers between devices  17.6 us (17%)
  local copies, waits for them, and re-layouts  16.6 us (16%)
  other arithmetic  1.36 us (1%)
    all_to_all x2, blocking collectives, exchange(): return lax.all_to_all(value, axes, split_axis=0, concat_axis=0, tiled=True)  43.1 us
    pallas_call x5, Pallas kernels, call(): pl.pallas_call(kernel, name=name, in_specs=[SMEM] * len(scalars) + [VMEM]...  24.4 us
    all_to_all x1, starting transfers between devices, exchange(): return lax.all_to_all(value, axes, split_axis=0, concat_axis=0, tiled=True)  17.6 us
    unnamed x46, local copies, waits for them, and re-layouts  15.7 us
  transfers between devices with their start and end apart: 1, of which 0 were waited for; matrix products, arithmetic and copies ran while one was open for 4% of the time, Pallas kernels for 11%

profile of v1, /device:TPU:1, one launch (start us, length us, event | category | flops | bytes accessed | tf_op | source)
XLA Modules:
  0.0 103.9 jit_solution(17344997878350112759)
XLA Ops:
  0.6 0.0 copy-start
  0.6 0.8 copy-done
  1.5 0.0 copy-start.1
  1.5 0.8 copy-done.1
  2.3 0.0 copy-start.2
  2.3 0.8 copy-done.2
  3.2 0.8 copy-done.3
  4.0 1.0 %pack.1 = bf16[64,8,256]{2,1,0:T(8,128)(2,1)} custom-call(bf16[128,256]{1,0:T(8,128)(2,1)S(1)} %copy-done, bf16[128,256]{1,0:T(8,128)(2,1)S(1)} %copy-done.1, bf16[128,256]{1,0:T(8,128)(2,1)S(1)} %copy-done.2, bf16[128,256]{1,0:T(8,128)(2,1)S(1)} %copy-done.3), custom_call_target="tpu_custom_call" | custom-call | flops 1048576 | bytes 524288 | tf_op jit(solution)/shard_map/spread/pack/pallas_call | solution.py:573
  5.0 17.6 %all-to-all-start = ((bf16[64,8,256]{2,1,0:T(8,128)(2,1)}), bf16[64,8,256]{2,1,0:T(8,128)(2,1)S(1)}, u32[]{:S(2)}, u32[]{:S(2)}) async-start(bf16[64,8,256]{2,1,0:T(8,128)(2,1)} %pack.1), calls=%async_computation | async-start | bytes 524288 | tf_op jit(solution)/shard_map/spread/all_to_all | solution.py:709
  22.7 0.7 fusion.norm
  23.3 0.8 copy.26
  24.2 0.7 copy.27
  24.9 0.8 copy.28.proj
  25.8 0.8 copy.30.short
  26.6 0.1 select_maximum_fusion.layer
  26.7 0.7 copy-done.4
  27.4 1.2 %copy-done.6 = bf16[2,512,512]{2,1,0:T(8,128)(2,1)S(1)} copy-done((bf16[2,512,512]{2,1,0:T(8,128)(2,1)S(1)}, bf16[2,512,512]{2,1,0:T(8,128)(2,1)}, u32[]{:S(2)}) %copy-start.6) | copy-done | bytes 1048600
  28.6 0.9 copy-done.8
  29.5 0.9 copy-done.11
  30.4 0.9 copy-done.12
  31.3 0.8 copy-done.13
  32.1 0.8 copy-done.15
  32.9 0.0 copy-start.16
  32.9 0.0 copy-start.17
  32.9 0.0 copy-start.18
  33.0 11.1 %filter.1 = (bf16[4096,256]{1,0:T(8,128)(2,1)S(1)}, bf16[4096,256]{1,0:T(8,128)(2,1)}, f32[128,256]{1,0:T(8,128)S(1)}, f32[128,512]{1,0:T(8,128)S(1)}, f32[128,128]{1,0:T(8,128)S(1)}) custom-call(s32[1]{0:T(128)} %bitcast.own, f32[128]{0:T(128)S(1)} %copy-done.4, f32[128]{0:T(128)S(1)} %fusion.norm, f32[64,128]{1,0:T(8,128)S(1)} %select_maximum_fusion.layer, ...), custom_call_target="tpu_custom_call" | custom-call | flops 8589934592 | bytes 8388608 | tf_op jit(solution)/shard_map/filter/pallas_call | solution.py:573
  44.0 1.3 %copy-done.19 = bf16[4096,256]{1,0:T(8,128)(2,1)} copy-done((bf16[4096,256]{1,0:T(8,128)(2,1)}, bf16[4096,256]{1,0:T(8,128)(2,1)S(1)}, u32[]{:S(2)}) %copy-start.19) | copy-done | bytes 2097176
  45.3 0.0 all-to-all-done.arrived
  45.3 0.0 copy-done.7
  45.3 0.0 copy-done.9
  45.3 0.0 copy-done.10
  45.3 0.0 copy-done.14
  45.4 0.0 copy-done.16
  45.4 0.0 copy-done.17
  45.4 0.0 copy-done.18
  45.4 0.0 copy-start.20
  45.4 1.6 %copy-done.20 = bf16[4096,256]{1,0:T(8,128)(2,1)S(1)} copy-done((bf16[4096,256]{1,0:T(8,128)(2,1)S(1)}, bf16[4096,256]{1,0:T(8,128)(2,1)}, u32[]{:S(2)}) %copy-start.20) | copy-done | bytes 2097176
  47.0 9.2 %gradient.1 = (f32[2,512,128]{2,1,0:T(8,128)S(1)}, f32[256,512]{1,0:T(8,128)S(1)}, f32[4,64,256]{2,1,0:T(8,128)S(1)}, f32[8,128]{1,0:T(8,128)S(1)}, f32[16,8,256]{2,1,0:T(8,128)S(1)}) custom-call(s32[1]{0:T(128)} %bitcast.own, bf16[64,8,256]{2,1,0:T(8,128)(2,1)S(1)} %all-to-all-done.arrived, f32[3,128,7]{2,1,0:T(8,128)S(1)} %copy.30.short, ...), custom_call_target="tpu_custom_call" | custom-call | flops 4294967296 | bytes 8388608 | tf_op jit(solution)/shard_map/gradient/pallas_call | solution.py:573
  56.2 11.3 %all_to_all.15.basis_parts = f32[16,8,256]{2,1,0:T(8,128)S(1)} all-to-all(f32[16,8,256]{2,1,0:T(8,128)S(1)} %get-tuple-element.31), channel_id=1, replica_groups=mesh['zh'=4,'y'=8,'core'=2,'x'=4,'zl'=2] {'core','x','zl'}, dimensions={0} | all-to-all | bytes 262144 | tf_op jit(solution)/shard_map/basis/all_to_all | solution.py:709
  67.5 0.0 copy-done.5
  67.5 2.1 %output.1 = bf16[64,16,256]{2,1,0:T(8,128)(2,1)S(1)} custom-call(s32[1]{0:T(128)} %bitcast.own, f32[128]{0:T(128)S(1)} %copy-done.5, f32[3,128,7]{2,1,0:T(8,128)S(1)} %copy.30.short, f32[2,512,128]{2,1,0:T(8,128)S(1)} %get-tuple-element.26.feat, f32[256,512]{1,0:T(8,128)S(1)} %get-tuple-element.27.spec, f32[128,512]{1,0:T(8,128)S(1)} %get-tuple-element.28.filter_spec, ...), custom_call_target="tpu_custom_call" | custom-call | flops 2147483648 | bytes 4194304 | tf_op jit(solution)/shard_map/output/pallas_call | solution.py:573
  69.6 31.8 %all_to_all.16.arrived = bf16[64,16,256]{2,1,0:T(8,128)(2,1)S(1)} all-to-all(bf16[64,16,256]{2,1,0:T(8,128)(2,1)S(1)} %output.1), channel_id=1, replica_groups=mesh['zh'=4,'y'=8,'core'=2,'x'=4,'zl'=2] {'zh','y','core'}, dimensions={0} | all-to-all | bytes 1048576 | tf_op jit(solution)/shard_map/collect/all_to_all | solution.py:709
  101.4 0.9 unpack.1
  102.3 0.7 copy.32
  103.0 0.1 reshape.22
  103.1 0.1 copy.31
  103.1 0.1 reshape.23
  103.2 0.6 slice_multiply_fusion
  (14 shorter events, 0.0 us)
Async XLA Ops:
  0.6 0.8 copy-start
  1.5 0.8 copy-start.1
  2.3 0.8 copy-start.2
  3.2 0.8 copy-start.3
  5.0 40.3 %all-to-all-start = ((bf16[64,8,256]{2,1,0:T(8,128)(2,1)}), bf16[64,8,256]{2,1,0:T(8,128)(2,1)S(1)}, u32[]{:S(2)}, u32[]{:S(2)}) async-start(bf16[64,8,256]{2,1,0:T(8,128)(2,1)} %pack.1), calls=%async_computation | async-start | bytes 524288 | tf_op jit(solution)/shard_map/spread/all_to_all | solution.py:709
  26.7 0.7 copy-start.4
  27.4 1.2 %copy-start.6 = (bf16[2,512,512]{2,1,0:T(8,128)(2,1)S(1)}, bf16[2,512,512]{2,1,0:T(8,128)(2,1)}, u32[]{:S(2)}) copy-start(bf16[2,512,512]{2,1,0:T(8,128)(2,1)} %constant.54.clone.full) | copy-start | bytes 3145732
  28.6 0.9 copy-start.8
  29.5 0.9 copy-start.11
  30.4 0.9 copy-start.12
  31.3 0.8 copy-start.13
  32.1 0.8 copy-start.15
  32.9 12.4 %copy-start.7 = (bf16[2,512,512]{2,1,0:T(8,128)(2,1)S(1)}, bf16[2,512,512]{2,1,0:T(8,128)(2,1)}, u32[]{:S(2)}) copy-start(bf16[2,512,512]{2,1,0:T(8,128)(2,1)} %constant.54.clone.full) | copy-start | bytes 3145732
  32.9 12.4 %copy-start.9 = (f32[2,64,256]{2,1,0:T(8,128)S(1)}, f32[2,64,256]{2,1,0:T(8,128)}, u32[]{:S(2)}) copy-start(f32[2,64,256]{2,1,0:T(8,128)} %constant.53.clone.twiddle) | copy-start | bytes 393220
  32.9 12.4 %copy-start.10 = (bf16[256,256]{1,0:T(8,128)(2,1)S(1)}, bf16[256,256]{1,0:T(8,128)(2,1)}, u32[]{:S(2)}) copy-start(bf16[256,256]{1,0:T(8,128)(2,1)} %constant.58.clone.back) | copy-start | bytes 393220
  32.9 12.4 %copy-start.14 = (bf16[64,384]{1,0:T(8,128)(2,1)S(1)}, bf16[64,384]{1,0:T(8,128)(2,1)}, u32[]{:S(2)}) copy-start(bf16[64,384]{1,0:T(8,128)(2,1)} %constant.52.clone.last) | copy-start | bytes 147460
  32.9 12.4 %copy-start.16 = (bf16[128,128]{1,0:T(8,128)(2,1)S(1)}, bf16[128,128]{1,0:T(8,128)(2,1)}, u32[]{:S(2)}) copy-start(bf16[128,128]{1,0:T(8,128)(2,1)} %constant.51.clone.forward) | copy-start | bytes 98308
  32.9 12.4 %copy-start.17 = (f32[8,8,128]{2,1,0:T(8,128)S(1)}, f32[8,8,128]{2,1,0:T(8,128)}, u32[]{:S(2)}) copy-start(f32[8,8,128]{2,1,0:T(8,128)} %constant.60.clone.place) | copy-start | bytes 98308
  32.9 12.4 %copy-start.18 = (f32[64,128]{1,0:T(8,128)S(1)}, f32[64,128]{1,0:T(8,128)}, u32[]{:S(2)}) copy-start(f32[64,128]{1,0:T(8,128)} %constant.59.clone.back_turn) | copy-start | bytes 98308
  44.0 1.3 %copy-start.19 = (bf16[4096,256]{1,0:T(8,128)(2,1)}, bf16[4096,256]{1,0:T(8,128)(2,1)S(1)}, u32[]{:S(2)}) copy-start(bf16[4096,256]{1,0:T(8,128)(2,1)S(1)} %get-tuple-element.22.act) | copy-start | bytes 6291460
  45.4 1.6 %copy-start.20 = (bf16[4096,256]{1,0:T(8,128)(2,1)S(1)}, bf16[4096,256]{1,0:T(8,128)(2,1)}, u32[]{:S(2)}) copy-start(bf16[4096,256]{1,0:T(8,128)(2,1)} %copy-done.19) | copy-start | bytes 6291460
  47.0 20.5 %copy-start.5 = (f32[128]{0:T(128)S(1)}, f32[128]{0:T(128)}, u32[]{:S(2)}) copy-start(f32[128]{0:T(128)} %skip.1) | copy-start | bytes 1540

commit v2 on v1

--- a/solution.py
+++ b/solution.py
@@ -25,22 +25,18 @@
 TURN = 1.0 / (2.0 * math.pi)
 
 SIN_COEF = (
-    6.2831854820251465,
-    -41.34170150756836,
-    81.60513305664062,
-    -76.70301818847656,
-    42.02592849731445,
-    -14.899847030639648,
-    3.2381374835968018,
+    4.442883014678955,
+    -7.308245658874512,
+    3.606354236602783,
+    -0.8461116552352905,
+    0.1098245158791542,
 )
 COS_COEF = (
-    1.0,
-    -19.73920440673828,
-    64.93911743164062,
-    -85.45014190673828,
-    60.16762924194336,
-    -25.967599868774414,
-    6.528658390045166,
+    1.4142135381698608,
+    -6.978850841522217,
+    5.739460468292236,
+    -1.883557915687561,
+    0.3106880187988281,
 )
 
 
@@ -210,47 +206,107 @@
         ref[half] = value[..., half * 128 : half * 128 + 128].reshape(ref.shape[1], 128)
 
 
-def pack_kernel(query, key, value, grad, out, wide):
-    for index, ref in enumerate((query, key, value, grad)):
-        value = ref[...].astype(F32)
+def begin(sems, pairs):
+    copies = [
+        pltpu.make_async_copy(source, target, sems.at[index])
+        for index, (source, target) in enumerate(pairs)
+    ]
+    for copy in copies:
+        copy.start()
+    return copies
+
+
+def picked(row, wanted):
+    lane = lax.broadcasted_iota(jnp.int32, row.shape, 1)
+    return jnp.sum(jnp.where(lane == wanted, row, 0.0), axis=1, keepdims=True)
+
+
+def pack_kernel(query, key, value, grad, out, held, wide, sems):
+    copies = begin(sems, [(ref, held.at[index]) for index, ref in enumerate((query, key, value, grad))])
+    for index in range(4):
+        copies[index].wait()
+        block = held[index].astype(F32)
         for half in range(2):
-            wide[half, index * 128 : (index + 1) * 128, :] = value[:, half * 128 : half * 128 + 128]
+            wide[half, index * 128 : (index + 1) * 128, :] = block[:, half * 128 : half * 128 + 128]
     for peer in range(ROWS):
         out[peer] = take(wide, peer, 8, ROWS).astype(BF16)
 
 
+def expm1_small(value):
+    series = jnp.ones_like(value)
+    for order in range(9, 1, -1):
+        series = 1.0 + value * series * (1.0 / order)
+    return jnp.where(value > -0.5, value * series, jnp.exp(value) - 1.0)
+
+
 def filter_kernel(
     own,
+    weight_src,
+    bias_src,
+    proj_src,
+    decay_src,
+    pick_src,
+    turn_src,
+    right_src,
+    forward_src,
+    twiddle_src,
+    full_src,
+    act_out,
+    cos_out,
+    env_out,
+    spec_out,
+    column_out,
+    weight,
+    bias,
+    proj,
     decay,
-    norm,
-    layer,
-    proj,
     pick,
     turn,
     right,
     forward,
     twiddle,
     full,
-    act_out,
-    cos_out,
-    env_out,
-    spec_out,
-    column_out,
+    layer,
     left,
     phase,
     filt,
+    act,
+    cosv,
+    out_sems,
+    sems,
 ):
     first = own[0]
-    layer_all = layer[...]
+    copies = begin(
+        sems,
+        [
+            (weight_src, weight),
+            (bias_src, bias),
+            (pick_src, pick),
+            (proj_src, proj),
+            (turn_src, turn),
+            (right_src, right),
+            (decay_src, decay),
+            (forward_src, forward),
+            (twiddle_src, twiddle),
+            (full_src, full),
+        ],
+    )
+    layer[...] = jnp.zeros((128, 128), F32)
+    for copy in copies[:3]:
+        copy.wait()
+    layer[0:EMB, 0:FEAT] = weight[...]
+    layer[EMB : EMB + 1, 0:FEAT] = bias[...]
+    layer_all = layer[...].T[0:FEAT, :]
     same = jnp.dot(layer_all, pick[0], precision=EXACT, preferred_element_type=F32) * TURN
     cross = jnp.dot(layer_all, pick[1], precision=EXACT, preferred_element_type=F32) * TURN
     lane = lax.broadcasted_iota(jnp.int32, (FEAT, 128), 1)
     sublane = lax.broadcasted_iota(jnp.int32, (8, 128), 0)
-    proj_turned = proj[...].T
+    for copy in copies[3:7]:
+        copy.wait()
     columns = []
     for chan in range(CHAN):
         hit = lane == first + 64 * chan
-        column = jnp.sum(jnp.where(hit, proj_turned, 0.0), axis=1, keepdims=True)
+        column = jnp.sum(jnp.where(hit, proj[...], 0.0), axis=1, keepdims=True)
         column_wide = jnp.broadcast_to(column, (FEAT, 128))
         column_out[chan * FEAT : (chan + 1) * FEAT, :] = column_wide
         columns.append(column_wide)
@@ -268,72 +324,107 @@
         left[pl.ds(start, FEAT), 128:256] = two.astype(BF16)
         return carry
 
-    lax.fori_loop(0, ROWS, make_left, 0, unroll=2)
+    lax.fori_loop(0, ROWS, make_left, 0, unroll=4)
 
     def chunk(index, carry):
         base = pl.multiple_of(index * 512, 512)
         phase[...] = dot(left[pl.ds(base, 512), :], right[...])
-
-        def one_block(inner, sums):
-            near = pl.multiple_of(inner * FEAT, FEAT)
-            kept = []
-            for half in range(2):
-                lanes = slice(half * 128, half * 128 + 128)
-                turns = phase[pl.ds(near, FEAT), lanes]
+        for half in range(2):
+            lanes = slice(half * 128, half * 128 + 128)
+            sums = [jnp.zeros((8, 128), F32)] * CHAN
+            for inner in range(8):
+                near = inner * FEAT
+                turns = phase[near : near + FEAT, lanes]
                 rest = turns - jnp.round(turns)
                 square = rest * rest
-                sine = jnp.full_like(rest, SIN_COEF[-1])
-                cosine = jnp.full_like(rest, COS_COEF[-1])
-                for coef in SIN_COEF[-2::-1]:
+                sine = SIN_COEF[-1] * square + SIN_COEF[-2]
+                cosine = COS_COEF[-1] * square + COS_COEF[-2]
+                for coef in SIN_COEF[-3::-1]:
                     sine = sine * square + coef
-                for coef in COS_COEF[-2::-1]:
+                for coef in COS_COEF[-3::-1]:
                     cosine = cosine * square + coef
                 sine = sine * rest
-                act_out[pl.ds(base + near, FEAT), lanes] = sine.astype(BF16)
-                cos_out[pl.ds(base + near, FEAT), lanes] = cosine.astype(BF16)
+                whole_sine = sine * cosine
+                whole_cosine = 1.0 - sine * sine
+                act[pl.ds(base + near, FEAT), lanes] = whole_sine.astype(BF16)
+                cosv[pl.ds(base + near, FEAT), lanes] = whole_cosine.astype(BF16)
                 for chan in range(CHAN):
-                    total = jnp.sum(sine * columns[chan], axis=0, keepdims=True)
-                    kept.append(jnp.where(sublane == inner, total, sums[2 * half + chan]))
-            return tuple(kept)
-
-        sums = lax.fori_loop(0, 8, one_block, (jnp.zeros((8, 128), F32),) * 4)
-        for half in range(2):
+                    total = jnp.sum(whole_sine * columns[chan], axis=0, keepdims=True)
+                    sums[chan] = jnp.where(sublane == inner, total, sums[chan])
             for chan in range(CHAN):
                 start = pl.multiple_of(chan * ROWS + index * 8, 8)
-                filt[pl.ds(start, 8), half * 128 : half * 128 + 128] = sums[2 * half + chan]
+                filt[pl.ds(start, 8), lanes] = sums[chan]
+        send(index, 0).start()
+        send(index, 1).start()
         return carry
 
+    def send(index, which):
+        rows = pl.ds(pl.multiple_of(index * 512, 512), 512)
+        source, target = ((act, act_out), (cosv, cos_out))[which]
+        return pltpu.make_async_copy(source.at[rows], target.at[rows], out_sems.at[which, index])
+
     lax.fori_loop(0, 8, chunk, 0)
+    ratio = decay[...] * (1.0 / TOTAL)
+    energy = expm1_small(-2.0 * decay[...]) / expm1_small(-2.0 * ratio)
+    norm = 1.0 / jnp.sqrt(energy)
+    for copy in copies[7:]:
+        copy.wait()
     position = (
         lax.broadcasted_iota(jnp.int32, (ROWS, COLS), 0) * COLS
         + lax.broadcasted_iota(jnp.int32, (ROWS, COLS), 1)
     ).astype(F32)
     signals = []
     for chan in range(CHAN):
-        rate = decay[first + 64 * chan]
-        envelope = jnp.exp(-(rate * position) * (1.0 / TOTAL)) * norm[first + 64 * chan]
+        rate = picked(decay[...], first + 64 * chan)
+        envelope = jnp.exp(-(rate * position) * (1.0 / TOTAL)) * picked(norm, first + 64 * chan)
         env_out[chan * ROWS : (chan + 1) * ROWS, :] = envelope
         signals.append((filt[chan * ROWS : (chan + 1) * ROWS, :] * envelope).astype(BF16))
     spec_out[...] = spectrum(signals, forward[...], twiddle[0], twiddle[1], full[0], full[1])
+    for index in range(8):
+        send(index, 0).wait()
+        send(index, 1).wait()
 
 
 def own_taps(first, short, taps, order):
-    lane = lax.broadcasted_iota(jnp.int32, (8, 128), 1)
-    taps[...] = jnp.where(lane == 0, 1.0, 0.0)
+    row = lax.broadcasted_iota(jnp.int32, (TAPS, 128), 0)
+    lane = lax.broadcasted_iota(jnp.int32, (TAPS, 128), 1)
+    columns = jnp.where(row == 0, 1.0, 0.0)
     for place, which in order:
         for chan in range(CHAN):
-            taps[place + chan : place + chan + 1, 0:TAPS] = short[which, pl.ds(first + 64 * chan, 1), :]
-    return taps[...]
+            hit = lane == first + 64 * chan
+            column = jnp.sum(jnp.where(hit, short[which], 0.0), axis=1, keepdims=True)
+            columns = jnp.where(lane == place + chan, column, columns)
+    taps[...] = jnp.zeros((128, 128), F32)
+    taps[0:TAPS, :] = columns
+    return taps[...].T[0:8, :]
 
 
 def gradient_kernel(
     own,
+    arrived_src,
+    act_src,
+    cosine_src,
+    envelope_src,
+    columns_src,
+    short_src,
+    back_src,
+    back_turn_src,
+    place_src,
+    forward_src,
+    last_src,
+    twiddle_src,
+    full_src,
+    feat_out,
+    spec_out,
+    signal_out,
+    proj_out,
+    basis_out,
     arrived,
-    short,
     act,
     cosine,
     envelope,
     columns,
+    short,
     back,
     back_turn,
     place,
@@ -341,20 +432,36 @@
     last,
     twiddle,
     full,
-    feat_out,
-    spec_out,
-    signal_out,
-    proj_out,
-    basis_out,
     taps,
     raw,
-    raw_turned,
-    part,
-    product,
-    proj_product,
+    feat,
+    spec,
+    kept,
+    out_sems,
+    sems,
 ):
     first = own[0]
+    copies = begin(
+        sems,
+        [
+            (short_src, short),
+            (arrived_src, arrived),
+            (forward_src, forward),
+            (twiddle_src, twiddle),
+            (full_src, full),
+            (last_src, last),
+            (envelope_src, envelope),
+            (cosine_src, cosine),
+            (act_src, act),
+            (columns_src, columns),
+            (back_src, back),
+            (back_turn_src, back_turn),
+            (place_src, place),
+        ],
+    )
+    copies[0].wait()
     weights = own_taps(first, short, taps, ((0, 0), (2, 1), (4, 2)))
+    copies[1].wait()
     signal = arrived[...].astype(F32)
     lane = lax.broadcasted_iota(jnp.int32, (ROWS, 8, COLS), 2)
     result = weights[None, :, 0:1] * signal
@@ -364,10 +471,11 @@
         before = jnp.concatenate([zeros, moved[:-1]], axis=0)
         shifted = jnp.where(lane < offset, before, moved)
         result = result + weights[None, :, offset : offset + 1] * shifted
-    fill(feat_out, result)
+    fill(feat, result)
+    leaving = begin(out_sems.at[pl.ds(0, 1)], [(feat, feat_out)])
 
     def plane(index):
-        return take(feat_out, index, ROWS, 8)
+        return take(feat, index, ROWS, 8)
 
     signals = []
     for chan in range(CHAN):
@@ -375,11 +483,15 @@
     for chan in range(CHAN):
         signals.append((plane(chan) * plane(6 + chan)).astype(BF16))
     for index in range(4):
-        signal_out[index] = signals[index].astype(F32)
+        kept[index] = signals[index].astype(F32)
+    leaving += begin(out_sems.at[pl.ds(1, 1)], [(kept, signal_out)])
+    for copy in copies[2:5]:
+        copy.wait()
     tables = (twiddle[0], twiddle[1], full[0], full[1])
-    spec = spectrum(signals, forward[...], *tables)
-    spec_out[...] = spec
-    carried, grad = spec[: CHAN * ROWS], spec[CHAN * ROWS :]
+    spec_all = spectrum(signals, forward[...], *tables)
+    spec[...] = spec_all
+    leaving += begin(out_sems.at[pl.ds(2, 1)], [(spec, spec_out)])
+    carried, grad = spec_all[: CHAN * ROWS], spec_all[CHAN * ROWS :]
     carried_re, carried_im = carried[:, :COLS], carried[:, COLS:]
     grad_re, grad_im = grad[:, :COLS], grad[:, COLS:]
     crossed = jnp.concatenate(
@@ -389,64 +501,66 @@
         ],
         axis=1,
     )
+    for copy in copies[5:7]:
+        copy.wait()
     filter_grad = restore(crossed, CHAN, last[...], *tables)
     for chan in range(CHAN):
         rounded = filter_grad[chan].astype(BF16).astype(F32)
         scaled = rounded * envelope[chan * ROWS : (chan + 1) * ROWS, :]
         for half in range(2):
             raw[half, chan * ROWS : (chan + 1) * ROWS, :] = scaled[:, half * 128 : half * 128 + 128]
-    raw_hi, raw_lo = split(jnp.concatenate([raw[half].T for half in range(2)], axis=0))
-    raw_turned[:, 0:128] = raw_hi
-    raw_turned[:, 128:256] = raw_lo
+    for copy in copies[7:]:
+        copy.wait()
     column0 = columns[0:FEAT, :]
     column1 = columns[FEAT : 2 * FEAT, :]
-    wide_lane = lax.broadcasted_iota(jnp.int32, (FEAT, COLS), 1) % ROWS
+    lane128 = lax.broadcasted_iota(jnp.int32, (FEAT, 128), 1)
+    row_lane = lane128 % 8
+    back_all = back[...]
 
     def chunk(index, carry):
+        basis_sum, proj_sum = carry
         base = pl.multiple_of(index * 512, 512)
-
-        def one_block(inner, carry):
-            near = pl.multiple_of(inner * FEAT, FEAT)
-            block = index * 8 + inner
+        start = pl.multiple_of(index * 8, 8)
+        rows = [
+            [raw[half, pl.ds(chan * ROWS + start, 8), :] for half in range(2)] for chan in range(CHAN)
+        ]
+        wide = jnp.concatenate([jnp.concatenate(rows[chan], axis=1) for chan in range(CHAN)], axis=0)
+        hi = wide.astype(BF16).astype(F32)
+        packed = jnp.concatenate([hi, wide - hi, jnp.zeros((128 - 4 * 8, COLS), F32)], axis=0)
+        turned = jnp.concatenate(
+            [packed[:, half * 128 : half * 128 + 128].T for half in range(2)], axis=0
+        ).astype(BF16)
+        parts = []
+        for inner in range(8):
+            near = inner * FEAT
+            pieces = []
             for half in range(2):
                 lanes = slice(half * 128, half * 128 + 128)
                 value = (
-                    column0 * raw[half, pl.ds(block, 1), :]
-                    + column1 * raw[half, pl.ds(ROWS + block, 1), :]
+                    column0 * rows[0][half][inner : inner + 1, :]
+                    + column1 * rows[1][half][inner : inner + 1, :]
                 )
                 value = value * cosine[pl.ds(base + near, FEAT), lanes].astype(F32)
-                part[pl.ds(near, FEAT), lanes] = value.astype(BF16)
-            return carry
-
-        lax.fori_loop(0, 8, one_block, 0)
-        product[...] = dot(part[...], back[...])
-        proj_product[...] = dot(act[pl.ds(base, 512), :], raw_turned[...])
-
-        def gather(inner, carry):
-            basis_sum, proj_sum = carry
-            near = pl.multiple_of(inner * FEAT, FEAT)
-            block = index * 8 + inner
-            angle = back_turn[pl.ds(block, 1), :]
-            both = product[pl.ds(near, FEAT), 0:128] + product[pl.ds(near, FEAT), 128:256]
+                pieces.append(value.astype(BF16))
+            parts.append(jnp.concatenate(pieces, axis=1))
+        product = dot(jnp.concatenate(parts, axis=0), back_all)
+        proj_product = dot(act[pl.ds(base, 512), :], turned)
+        for inner in range(8):
+            near = inner * FEAT
+            angle = back_turn[pl.ds(start, 8), :][inner : inner + 1, :]
+            both = product[near : near + FEAT, 0:128] + product[near : near + FEAT, 128:256]
             basis_sum = basis_sum + both * angle
             proj_sum = proj_sum + jnp.where(
-                wide_lane == block, proj_product[pl.ds(near, FEAT), :], 0.0
+                row_lane == inner, proj_product[near : near + FEAT, :], 0.0
             )
-            return basis_sum, proj_sum
-
-        return lax.fori_loop(0, 8, gather, carry)
+        return basis_sum, proj_sum
 
     basis_sum, proj_sum = lax.fori_loop(
-        0, 8, chunk, (jnp.zeros((FEAT, 128), F32), jnp.zeros((FEAT, COLS), F32))
-    )
-    proj_both = proj_sum[:, 0:128] + proj_sum[:, 128:256]
-    lane128 = lax.broadcasted_iota(jnp.int32, (FEAT, 128), 1)
+        0, 8, chunk, (jnp.zeros((FEAT, 128), F32), jnp.zeros((FEAT, 128), F32))
+    )
+    own_lane = lane128 % 16
     stacked = jnp.concatenate(
-        [
-            jnp.where(lane128 < ROWS, proj_both, 0.0),
-            jnp.where(lane128 >= ROWS, proj_both, 0.0),
-        ],
-        axis=0,
+        [jnp.where(own_lane < 8, proj_sum, 0.0), jnp.where(own_lane >= 8, proj_sum, 0.0)], axis=0
     )
     proj_out[...] = lax.dot_general(
         jnp.ones((8, 128), F32),
@@ -469,27 +583,58 @@
         row = jnp.concatenate([piece[:, core * 32 : core * 32 + 32] for piece in pieces], axis=1)
         for peer in range(8):
             basis_out[core * 8 + peer] = row
+    for copy in leaving:
+        copy.wait()
 
 
 def output_kernel(
     own,
-    skip,
-    short,
+    feat_src,
+    spec_src,
+    filter_spec_src,
+    signals_src,
+    proj_row_src,
+    basis_parts_src,
+    skip_src,
+    short_src,
+    last_src,
+    twiddle_src,
+    full_src,
+    out,
     feat,
     spec,
     filter_spec,
     signals,
     proj_row,
     basis_parts,
+    skip,
+    short,
     last,
     twiddle,
     full,
-    out,
     taps,
     mate,
+    sems,
 ):
     first = own[0]
-    weights = own_taps(first, short, taps, ((2, 2), (4, 1), (6, 0)))
+    copies = begin(
+        sems,
+        [
+            (spec_src, spec),
+            (filter_spec_src, filter_spec),
+            (full_src, full),
+            (twiddle_src, twiddle),
+            (last_src, last),
+            (skip_src, skip),
+            (short_src, short),
+            (signals_src, signals),
+            (feat_src, feat),
+            (proj_row_src, proj_row),
+            (basis_parts_src, basis_parts),
+        ],
+    )
+    for copy in copies[0:5]:
+        copy.wait()
     tables = (twiddle[0], twiddle[1], full[0], full[1])
     carried, grad = spec[0 : CHAN * ROWS, :], spec[CHAN * ROWS : 2 * CHAN * ROWS, :]
     filt = filter_spec[...]
@@ -516,8 +661,11 @@
         axis=0,
     )
     sums = restore(crossed, 2 * CHAN, last[...], *tables)
+    for copy in copies[5:]:
+        copy.wait()
+    weights = own_taps(first, short, taps, ((2, 2), (4, 1), (6, 0)))
     for chan in range(CHAN):
-        gain = skip[first + 64 * chan]
+        gain = picked(skip[...], first + 64 * chan)
         long_out = (sums[chan] + gain * signals[chan]).astype(BF16).astype(F32)
         carried_grad = (sums[CHAN + chan] + gain * signals[CHAN + chan]).astype(BF16).astype(F32)
         put(mate, chan, ROWS, 8, long_out)
@@ -548,38 +696,57 @@
     out[...] = wide.astype(BF16)
 
 
-def unpack_kernel(arrived, mixed, grad_query, grad_key, grad_value, proj, basis, wide):
+def unpack_kernel(
+    arrived, mixed, grad_query, grad_key, grad_value, proj, basis, wide, sorted_rows
+):
     fill(wide, arrived[...].astype(F32))
     for ref, start in ((mixed, 0), (grad_value, 2), (grad_key, 4), (grad_query, 6)):
         for chan in range(CHAN):
             ref[chan * ROWS : (chan + 1) * ROWS, :] = take(wide, start + chan, ROWS, 16).astype(BF16)
     last = take(wide, 15, ROWS, 16)
     both = (last[:, 0:128] + last[:, 128:256]) * (1.0 / math.sqrt(TOTAL))
-    proj[0:ROWS, :] = both[:, 0:64]
-    proj[ROWS : 2 * ROWS, :] = both[:, 64:128]
+    both = jnp.concatenate([both, jnp.zeros_like(both)], axis=0).T
+    proj[:, 0:ROWS] = both[0:FEAT, 0:ROWS]
+    proj[:, ROWS : 2 * ROWS] = both[FEAT : 2 * FEAT, 0:ROWS]
+    totals = []
     for core in range(2):
+        pieces = []
         for half in range(2):
             total = wide[half, core * 16 + 8 : core * 16 + 16, :]
             for source in range(core + 2, ROWS, 2):
                 total = total + wide[half, source * 16 + 8 : source * 16 + 16, :]
-            basis[core, :, half * 128 : half * 128 + 128] = total
+            pieces.append(total)
+        totals.append(jnp.concatenate(pieces, axis=1))
+    scale = math.sqrt(FEAT / (TOTAL * 1024))
+    for group in range(8):
+        lanes = slice(group * 32, group * 32 + 32)
+        merged = jnp.concatenate(
+            [totals[0][:, lanes], totals[1][:, lanes], jnp.zeros((8, 64), F32)], axis=1
+        )
+        sorted_rows[pl.ds(group, 8, stride=8), :] = merged * scale
+    basis[...] = sorted_rows[0:EMB, 0:FEAT]
 
 
 SMEM = pl.BlockSpec(memory_space=pltpu.SMEM)
 VMEM = pl.BlockSpec(memory_space=pltpu.VMEM)
-
-
-def call(kernel, name, scalars, args, outs, scratch, flops, moved):
+HBM = pl.BlockSpec(memory_space=pltpu.HBM)
+LIMIT = 62 * 1024 * 1024
+
+
+def call(kernel, name, own, near, far, outs, scratch, flops, moved, limit=LIMIT):
+    landing = [pltpu.VMEM(value.shape, value.dtype) for value in far]
     return pl.pallas_call(
         kernel,
         name=name,
-        in_specs=[SMEM] * len(scalars) + [VMEM] * len(args),
-        out_specs=[VMEM] * len(outs) if isinstance(outs, list) else VMEM,
-        out_shape=outs,
-        scratch_shapes=scratch,
-        compiler_params=pltpu.CompilerParams(vmem_limit_bytes=48 * 1024 * 1024),
+        in_specs=[SMEM] * len(own) + [VMEM] * len(near) + [HBM] * len(far),
+        out_specs=[HBM if direct else VMEM for _, direct in outs],
+        out_shape=[value for value, _ in outs],
+        scratch_shapes=(landing if kernel is not pack_kernel else [])
+        + scratch
+        + ([pltpu.SemaphoreType.DMA((len(far),))] if far else []),
+        compiler_params=pltpu.CompilerParams(vmem_limit_bytes=limit),
         cost_estimate=pl.CostEstimate(flops=flops, bytes_accessed=moved, transcendentals=0),
-    )(*scalars, *args)
+    )(*own, *near, *far)
 
 
 def shape(dims, kind=F32):
@@ -591,31 +758,38 @@
         pack_kernel,
         "pack",
         [],
+        [],
         [query_in, key_in, value_in, grad_out],
-        shape((ROWS, 8, COLS), BF16),
-        [pltpu.VMEM((2, 512, 128), F32)],
+        [(shape((ROWS, 8, COLS), BF16), False)],
+        [pltpu.VMEM((4, 128, COLS), BF16), pltpu.VMEM((2, 512, 128), F32)],
         1 << 20,
         1 << 19,
-    )
-
-
-def run_filter(own, decay, norm, layer, proj, consts):
+    )[0]
+
+
+def run_filter(own, weight, bias, proj, decay, consts):
+    names = ("pick", "turn", "right", "forward", "twiddle", "full")
     return call(
         filter_kernel,
         "filter",
-        [own, decay, norm],
-        [layer, proj, consts["pick"], consts["turn"], consts["right"], consts["forward"], consts["twiddle"], consts["full"]],
+        [own],
+        [],
+        [weight, bias, proj, decay] + [consts[name] for name in names],
         [
-            shape((ROWS * FEAT, COLS), BF16),
-            shape((ROWS * FEAT, COLS), BF16),
-            shape((CHAN * ROWS, COLS)),
-            shape((CHAN * ROWS, 2 * COLS)),
-            shape((CHAN * FEAT, 128)),
+            (shape((ROWS * FEAT, COLS), BF16), True),
+            (shape((ROWS * FEAT, COLS), BF16), True),
+            (shape((CHAN * ROWS, COLS)), False),
+            (shape((CHAN * ROWS, 2 * COLS)), False),
+            (shape((CHAN * FEAT, 128)), False),
         ],
         [
+            pltpu.VMEM((128, 128), F32),
             pltpu.VMEM((ROWS * FEAT, COLS), BF16),
             pltpu.VMEM((512, COLS), F32),
             pltpu.VMEM((CHAN * ROWS, COLS), F32),
+            pltpu.VMEM((ROWS * FEAT, COLS), BF16),
+            pltpu.VMEM((ROWS * FEAT, COLS), BF16),
+            pltpu.SemaphoreType.DMA((2, 8)),
         ],
         1 << 33,
         1 << 23,
@@ -623,25 +797,27 @@
 
 
 def run_gradient(own, arrived, short, act, cosine, envelope, columns, consts):
+    names = ("back", "back_turn", "place", "forward", "last", "twiddle", "full")
     return call(
         gradient_kernel,
         "gradient",
         [own],
-        [arrived, short, act, cosine, envelope, columns, consts["back"], consts["back_turn"], consts["place"], consts["forward"], consts["last"], consts["twiddle"], consts["full"]],
+        [],
+        [arrived, act, cosine, envelope, columns, short] + [consts[name] for name in names],
         [
-            shape((2, ROWS * 8, 128)),
-            shape((2 * CHAN * ROWS, 2 * COLS)),
-            shape((2 * CHAN, ROWS, COLS)),
-            shape((8, 128)),
-            shape((16, 8, COLS)),
+            (shape((2, ROWS * 8, 128)), True),
+            (shape((2 * CHAN * ROWS, 2 * COLS)), True),
+            (shape((2 * CHAN, ROWS, COLS)), True),
+            (shape((8, 128)), False),
+            (shape((16, 8, COLS)), False),
         ],
         [
-            pltpu.VMEM((8, 128), F32),
+            pltpu.VMEM((128, 128), F32),
             pltpu.VMEM((2, CHAN * ROWS, 128), F32),
-            pltpu.VMEM((COLS, COLS), BF16),
-            pltpu.VMEM((512, COLS), BF16),
-            pltpu.VMEM((512, COLS), F32),
-            pltpu.VMEM((512, COLS), F32),
+            pltpu.VMEM((2, ROWS * 8, 128), F32),
+            pltpu.VMEM((2 * CHAN * ROWS, 2 * COLS), F32),
+            pltpu.VMEM((2 * CHAN, ROWS, COLS), F32),
+            pltpu.SemaphoreType.DMA((3,)),
         ],
         1 << 32,
         1 << 23,
@@ -649,16 +825,18 @@
 
 
 def run_output(own, skip, short, feat, spec, filter_spec, signals, proj_row, basis_parts, consts):
+    names = ("last", "twiddle", "full")
     return call(
         output_kernel,
         "output",
-        [own, skip],
-        [short, feat, spec, filter_spec, signals, proj_row, basis_parts, consts["last"], consts["twiddle"], consts["full"]],
-        shape((ROWS, 16, COLS), BF16),
-        [pltpu.VMEM((8, 128), F32), pltpu.VMEM((2, ROWS * 8, 128), F32)],
+        [own],
+        [],
+        [feat, spec, filter_spec, signals, proj_row, basis_parts, skip, short] + [consts[name] for name in names],
+        [(shape((ROWS, 16, COLS), BF16), False)],
+        [pltpu.VMEM((128, 128), F32), pltpu.VMEM((2, ROWS * 8, 128), F32)],
         1 << 31,
         1 << 22,
-    )
+    )[0]
 
 
 def run_unpack(arrived):
@@ -668,10 +846,12 @@
         "unpack",
         [],
         [arrived],
-        [block, block, block, block, shape((128, FEAT)), shape((2, 8, COLS))],
-        [pltpu.VMEM((2, ROWS * 16, 128), F32)],
+        [],
+        [(value, False) for value in [block] * 4 + [shape((FEAT, 128)), shape((EMB, FEAT))]],
+        [pltpu.VMEM((2, ROWS * 16, 128), F32), pltpu.VMEM((64, 128), F32)],
         1 << 20,
         1 << 20,
+        20 * 1024 * 1024,
     )
 
 
@@ -690,15 +870,6 @@
         back_turn=jnp.asarray(back_turn),
         place=jnp.asarray(place),
     )
-
-
-def filter_params(basis_weight, basis_bias, decay_rate):
-    energy = jnp.expm1(-2.0 * decay_rate) / jnp.expm1(-2.0 * decay_rate / TOTAL)
-    norm = 1.0 / jnp.sqrt(energy)
-    layer = jnp.pad(
-        jnp.concatenate([basis_weight, basis_bias[:, None]], axis=1), ((0, 0), (0, 128 - EMB - 1))
-    )
-    return norm, layer
 
 
 CTX = ("zh", "y", "core")
@@ -725,26 +896,36 @@
     own = lax.axis_index(CTX).astype(jnp.int32).reshape(1)
     with jax.named_scope("spread"):
         arrived = exchange(run_pack(query_in, key_in, value_in, grad_out), CTX)
-    norm, layer = filter_params(basis_weight, basis_bias, decay_rate)
+    short = short_kernel.transpose(0, 2, 1)
     act, cosine, envelope, filter_spec, columns = run_filter(
-        own, decay_rate, norm, layer, filter_proj, consts
+        own,
+        basis_weight.T,
+        basis_bias.reshape(1, FEAT),
+        filter_proj.T,
+        decay_rate.reshape(1, 128),
+        consts,
     )
     feat, spec, signals, proj_row, basis_own = run_gradient(
-        own, arrived, short_kernel, act, cosine, envelope, columns, consts
+        own, arrived, short, act, cosine, envelope, columns, consts
     )
     with jax.named_scope("basis"):
         basis_parts = exchange(basis_own, PAIR)
     packed = run_output(
-        own, skip_gain, short_kernel, feat, spec, filter_spec, signals, proj_row, basis_parts, consts
+        own,
+        skip_gain.reshape(1, 128),
+        short,
+        feat,
+        spec,
+        filter_spec,
+        signals,
+        proj_row,
+        basis_parts,
+        consts,
     )
     with jax.named_scope("collect"):
         returned = exchange(packed, CTX)
-    mixed, grad_query, grad_key, grad_value, grad_proj, basis_sum = run_unpack(returned)
-    grad_basis = (
-        basis_sum.reshape(2, 8, 8, 32).transpose(0, 3, 1, 2).reshape(FEAT, 64)[:, :EMB]
-        * math.sqrt(FEAT / (TOTAL * 1024))
-    )
-    return (mixed, grad_query, grad_key, grad_value, grad_proj, grad_basis)
+    mixed, grad_query, grad_key, grad_value, grad_proj, grad_basis = run_unpack(returned)
+    return (mixed, grad_query, grad_key, grad_value, grad_proj.T, grad_basis.T)
 
 
 def solution(mesh):

time: 105 us -> 87.9 us (0.84)
  local copies, waits for them, and re-layouts: 16.6 us -> 0.7 us
  waiting for transfers between devices: 0.01 us -> 3.91 us
  blocking collectives: 43.1 us -> 39.7 us
  other arithmetic: 1.36 us -> 0 us
    unnamed x46 -> x2, local copies, waits for them, and re-layouts: 15.7 us -> 0.7 us
    all_to_all x1, waiting for transfers between devices: 0.01 us -> 3.91 us  [exchange(): return lax.all_to_all(value, axes, split_axis=0, concat_axis=0, tiled=True)]
    all_to_all x2, blocking collectives: 43.1 us -> 39.7 us  [exchange(): return lax.all_to_all(value, axes, split_axis=0, concat_axis=0, tiled=True)]
  transfers between devices with their start and end apart: 1 -> 1, of which waited for: 0 -> 1; matrix products, arithmetic and copies ran while one was open for 4% -> 0% of each run, Pallas kernels for 11% -> 11%
where the time goes in v2:
time: 87.9 us; the launch traced here: 87.5 us
  blocking collectives  39.7 us (45%)
  Pallas kernels  24.9 us (28%)
  starting transfers between devices  17.6 us (20%)
  waiting for transfers between devices  3.91 us (4%)
    all_to_all x2, blocking collectives, exchange(): return lax.all_to_all(value, axes, split_axis=0, concat_axis=0, tiled=True)  39.7 us
    pallas_call x5, Pallas kernels, call(): pl.pallas_call(kernel, name=name, in_specs=[SMEM] * len(own) + [VMEM] * l...  24.9 us
    all_to_all x1, starting transfers between devices, exchange(): return lax.all_to_all(value, axes, split_axis=0, concat_axis=0, tiled=True)  17.6 us
    all_to_all x1, waiting for transfers between devices, exchange(): return lax.all_to_all(value, axes, split_axis=0, concat_axis=0, tiled=True)  3.91 us
  transfers between devices with their start and end apart: 1, of which 1 were waited for; matrix products, arithmetic and copies ran while one was open for 0% of the time, Pallas kernels for 11%

profile of v2, /device:TPU:1, one launch (start us, length us, event | category | flops | bytes accessed | tf_op | source)
XLA Modules:
  0.0 87.5 jit_solution(16963210680015537427)
XLA Ops:
  0.6 2.0 %pack.1 = bf16[64,8,256]{2,1,0:T(8,128)(2,1)} custom-call(bf16[128,256]{1,0:T(8,128)(2,1)} %query.1, bf16[128,256]{1,0:T(8,128)(2,1)} %key.1, bf16[128,256]{1,0:T(8,128)(2,1)} %value.1, bf16[128,256]{1,0:T(8,128)(2,1)} %grad.1), custom_call_target="tpu_custom_call" | custom-call | flops 1048576 | bytes 524288 | tf_op jit(solution)/shard_map/spread/pack/pallas_call | solution.py:738
  2.6 17.6 %all-to-all-start = ((bf16[64,8,256]{2,1,0:T(8,128)(2,1)}), bf16[64,8,256]{2,1,0:T(8,128)(2,1)S(1)}, u32[]{:S(2)}, u32[]{:S(2)}) async-start(bf16[64,8,256]{2,1,0:T(8,128)(2,1)} %pack.1), calls=%async_computation | async-start | bytes 524288 | tf_op jit(solution)/shard_map/spread/all_to_all | solution.py:880
  20.3 9.9 %filter.1 = (bf16[4096,256]{1,0:T(8,128)(2,1)}, bf16[4096,256]{1,0:T(8,128)(2,1)}, f32[128,256]{1,0:T(8,128)}, f32[128,512]{1,0:T(8,128)}, f32[128,128]{1,0:T(8,128)}) custom-call(s32[1]{0:T(128)} %bitcast.own, f32[33,64]{1,0:T(8,128)} %bitcast.11, f32[1,64]{1,0:T(1,128)} %bitcast.15, f32[64,128]{1,0:T(8,128)} %bitcast.9, f32[1,128]{1,0:T(1,128)} %bitcast.16, ...), custom_call_target="tpu_custom_call" | custom-call | flops 8589934592 | bytes 8388608 | tf_op jit(solution)/shard_map/filter/pallas_call | solution.py:738
  30.2 3.9 %all-to-all-done.arrived_src = bf16[64,8,256]{2,1,0:T(8,128)(2,1)S(1)} async-done(((bf16[64,8,256]{2,1,0:T(8,128)(2,1)}), bf16[64,8,256]{2,1,0:T(8,128)(2,1)S(1)}, u32[]{:S(2)}, u32[]{:S(2)}) %all-to-all-start) | async-done | bytes 262176 | tf_op jit(solution)/shard_map/spread/all_to_all | solution.py:880
  34.1 0.0 copy-start
  34.1 0.7 copy-done
  34.8 7.8 %gradient.1 = (f32[2,512,128]{2,1,0:T(8,128)}, f32[256,512]{1,0:T(8,128)}, f32[4,64,256]{2,1,0:T(8,128)}, f32[8,128]{1,0:T(8,128)}, f32[16,8,256]{2,1,0:T(8,128)}) custom-call(s32[1]{0:T(128)} %bitcast.own, bf16[64,8,256]{2,1,0:T(8,128)(2,1)} %copy-done, bf16[4096,256]{1,0:T(8,128)(2,1)} %get-tuple-element.22.act_src, ...), custom_call_target="tpu_custom_call" | custom-call | flops 4294967296 | bytes 8388608 | tf_op jit(solution)/shard_map/gradient/pallas_call | solution.py:738
  42.6 11.4 %all_to_all.15.basis_parts_src = f32[16,8,256]{2,1,0:T(8,128)} all-to-all(f32[16,8,256]{2,1,0:T(8,128)} %get-tuple-element.31), channel_id=1, replica_groups=mesh['zh'=4,'y'=8,'core'=2,'x'=4,'zl'=2] {'core','x','zl'}, dimensions={0} | all-to-all | bytes 262144 | tf_op jit(solution)/shard_map/basis/all_to_all | solution.py:880
  54.0 4.3 %output.1 = bf16[64,16,256]{2,1,0:T(8,128)(2,1)} custom-call(s32[1]{0:T(128)} %bitcast.own, f32[2,512,128]{2,1,0:T(8,128)} %get-tuple-element.26.feat_src, f32[256,512]{1,0:T(8,128)} %get-tuple-element.27.spec_src, f32[128,512]{1,0:T(8,128)} %get-tuple-element.28.filter_spec_src, f32[4,64,256]{2,1,0:T(8,128)} %get-tuple-element.29.signals_src, ...), custom_call_target="tpu_custom_call" | custom-call | flops 2147483648 | bytes 4194304 | tf_op jit(solution)/shard_map/output/pallas_call | solution.py:738
  58.3 28.3 %all_to_all.16.arrived = bf16[64,16,256]{2,1,0:T(8,128)(2,1)S(1)} all-to-all(bf16[64,16,256]{2,1,0:T(8,128)(2,1)} %output.1), channel_id=1, replica_groups=mesh['zh'=4,'y'=8,'core'=2,'x'=4,'zl'=2] {'zh','y','core'}, dimensions={0} | all-to-all | bytes 1048576 | tf_op jit(solution)/shard_map/collect/all_to_all | solution.py:880
  86.5 1.0 %unpack.1 = (bf16[128,256]{1,0:T(8,128)(2,1)}, bf16[128,256]{1,0:T(8,128)(2,1)}, bf16[128,256]{1,0:T(8,128)(2,1)}, bf16[128,256]{1,0:T(8,128)(2,1)}, f32[64,128]{1,0:T(8,128)}, /*index=5*/f32[33,64]{1,0:T(8,128)}) custom-call(bf16[64,16,256]{2,1,0:T(8,128)(2,1)S(1)} %all_to_all.16.arrived), custom_call_target="tpu_custom_call" | custom-call | flops 1048576 | bytes 1048576 | tf_op jit(solution)/shard_map/unpack/pallas_call | solution.py:738
Async XLA Ops:
  2.6 31.5 %all-to-all-start = ((bf16[64,8,256]{2,1,0:T(8,128)(2,1)}), bf16[64,8,256]{2,1,0:T(8,128)(2,1)S(1)}, u32[]{:S(2)}, u32[]{:S(2)}) async-start(bf16[64,8,256]{2,1,0:T(8,128)(2,1)} %pack.1), calls=%async_computation | async-start | bytes 524288 | tf_op jit(solution)/shard_map/spread/all_to_all | solution.py:880
  34.1 0.7 copy-start

commit v3 on v2

--- a/solution.py
+++ b/solution.py
@@ -402,10 +402,9 @@
 def gradient_kernel(
     own,
     arrived_src,
-    act_src,
-    cosine_src,
     envelope_src,
     columns_src,
+    cosine_src,
     short_src,
     back_src,
     back_turn_src,
@@ -416,14 +415,12 @@
     full_src,
     feat_out,
     spec_out,
-    signal_out,
-    proj_out,
+    raw_out,
     basis_out,
     arrived,
-    act,
-    cosine,
     envelope,
     columns,
+    cosine,
     short,
     back,
     back_turn,
@@ -436,7 +433,6 @@
     raw,
     feat,
     spec,
-    kept,
     out_sems,
     sems,
 ):
@@ -452,7 +448,6 @@
             (last_src, last),
             (envelope_src, envelope),
             (cosine_src, cosine),
-            (act_src, act),
             (columns_src, columns),
             (back_src, back),
             (back_turn_src, back_turn),
@@ -482,15 +477,12 @@
         signals.append((plane(2 + chan) * plane(4 + chan)).astype(BF16))
     for chan in range(CHAN):
         signals.append((plane(chan) * plane(6 + chan)).astype(BF16))
-    for index in range(4):
-        kept[index] = signals[index].astype(F32)
-    leaving += begin(out_sems.at[pl.ds(1, 1)], [(kept, signal_out)])
     for copy in copies[2:5]:
         copy.wait()
     tables = (twiddle[0], twiddle[1], full[0], full[1])
     spec_all = spectrum(signals, forward[...], *tables)
     spec[...] = spec_all
-    leaving += begin(out_sems.at[pl.ds(2, 1)], [(spec, spec_out)])
+    leaving += begin(out_sems.at[pl.ds(1, 1)], [(spec, spec_out)])
     carried, grad = spec_all[: CHAN * ROWS], spec_all[CHAN * ROWS :]
     carried_re, carried_im = carried[:, :COLS], carried[:, COLS:]
     grad_re, grad_im = grad[:, :COLS], grad[:, COLS:]
@@ -509,27 +501,20 @@
         scaled = rounded * envelope[chan * ROWS : (chan + 1) * ROWS, :]
         for half in range(2):
             raw[half, chan * ROWS : (chan + 1) * ROWS, :] = scaled[:, half * 128 : half * 128 + 128]
+    leaving += begin(out_sems.at[pl.ds(2, 1)], [(raw, raw_out)])
     for copy in copies[7:]:
         copy.wait()
     column0 = columns[0:FEAT, :]
     column1 = columns[FEAT : 2 * FEAT, :]
-    lane128 = lax.broadcasted_iota(jnp.int32, (FEAT, 128), 1)
-    row_lane = lane128 % 8
     back_all = back[...]
 
-    def chunk(index, carry):
-        basis_sum, proj_sum = carry
+    def chunk(index, basis_sum):
         base = pl.multiple_of(index * 512, 512)
         start = pl.multiple_of(index * 8, 8)
         rows = [
             [raw[half, pl.ds(chan * ROWS + start, 8), :] for half in range(2)] for chan in range(CHAN)
         ]
-        wide = jnp.concatenate([jnp.concatenate(rows[chan], axis=1) for chan in range(CHAN)], axis=0)
-        hi = wide.astype(BF16).astype(F32)
-        packed = jnp.concatenate([hi, wide - hi, jnp.zeros((128 - 4 * 8, COLS), F32)], axis=0)
-        turned = jnp.concatenate(
-            [packed[:, half * 128 : half * 128 + 128].T for half in range(2)], axis=0
-        ).astype(BF16)
+        angles = back_turn[pl.ds(start, 8), :]
         parts = []
         for inner in range(8):
             near = inner * FEAT
@@ -544,31 +529,13 @@
                 pieces.append(value.astype(BF16))
             parts.append(jnp.concatenate(pieces, axis=1))
         product = dot(jnp.concatenate(parts, axis=0), back_all)
-        proj_product = dot(act[pl.ds(base, 512), :], turned)
         for inner in range(8):
             near = inner * FEAT
-            angle = back_turn[pl.ds(start, 8), :][inner : inner + 1, :]
             both = product[near : near + FEAT, 0:128] + product[near : near + FEAT, 128:256]
-            basis_sum = basis_sum + both * angle
-            proj_sum = proj_sum + jnp.where(
-                row_lane == inner, proj_product[near : near + FEAT, :], 0.0
-            )
-        return basis_sum, proj_sum
-
-    basis_sum, proj_sum = lax.fori_loop(
-        0, 8, chunk, (jnp.zeros((FEAT, 128), F32), jnp.zeros((FEAT, 128), F32))
-    )
-    own_lane = lane128 % 16
-    stacked = jnp.concatenate(
-        [jnp.where(own_lane < 8, proj_sum, 0.0), jnp.where(own_lane >= 8, proj_sum, 0.0)], axis=0
-    )
-    proj_out[...] = lax.dot_general(
-        jnp.ones((8, 128), F32),
-        stacked,
-        (((1,), (1,)), ((), ())),
-        precision=EXACT,
-        preferred_element_type=F32,
-    )
+            basis_sum = basis_sum + both * angles[inner : inner + 1, :]
+        return basis_sum
+
+    basis_sum = lax.fori_loop(0, 8, chunk, jnp.zeros((FEAT, 128), F32), unroll=2)
     pieces = [
         lax.dot_general(
             place[group],
@@ -579,10 +546,12 @@
         )
         for group in range(8)
     ]
-    for core in range(2):
-        row = jnp.concatenate([piece[:, core * 32 : core * 32 + 32] for piece in pieces], axis=1)
+    for quarter in range(4):
+        row = jnp.concatenate(
+            [piece[:, quarter * 16 : quarter * 16 + 16] for piece in pieces], axis=1
+        )
         for peer in range(8):
-            basis_out[core * 8 + peer] = row
+            basis_out[quarter * 8 + peer] = row
     for copy in leaving:
         copy.wait()
 
@@ -592,9 +561,8 @@
     feat_src,
     spec_src,
     filter_spec_src,
-    signals_src,
-    proj_row_src,
-    basis_parts_src,
+    raw_src,
+    act_src,
     skip_src,
     short_src,
     last_src,
@@ -604,9 +572,8 @@
     feat,
     spec,
     filter_spec,
-    signals,
-    proj_row,
-    basis_parts,
+    raw,
+    act,
     skip,
     short,
     last,
@@ -614,6 +581,8 @@
     full,
     taps,
     mate,
+    stage,
+    out_sems,
     sems,
 ):
     first = own[0]
@@ -627,10 +596,9 @@
             (last_src, last),
             (skip_src, skip),
             (short_src, short),
-            (signals_src, signals),
             (feat_src, feat),
-            (proj_row_src, proj_row),
-            (basis_parts_src, basis_parts),
+            (raw_src, raw),
+            (act_src, act),
         ],
     )
     for copy in copies[0:5]:
@@ -661,13 +629,19 @@
         axis=0,
     )
     sums = restore(crossed, 2 * CHAN, last[...], *tables)
-    for copy in copies[5:]:
+    for copy in copies[5:8]:
         copy.wait()
     weights = own_taps(first, short, taps, ((2, 2), (4, 1), (6, 0)))
+
+    def plane(index):
+        return take(feat, index, ROWS, 8)
+
     for chan in range(CHAN):
         gain = picked(skip[...], first + 64 * chan)
-        long_out = (sums[chan] + gain * signals[chan]).astype(BF16).astype(F32)
-        carried_grad = (sums[CHAN + chan] + gain * signals[CHAN + chan]).astype(BF16).astype(F32)
+        carried_own = (plane(2 + chan) * plane(4 + chan)).astype(BF16).astype(F32)
+        grad_own = (plane(chan) * plane(6 + chan)).astype(BF16).astype(F32)
+        long_out = (sums[chan] + gain * carried_own).astype(BF16).astype(F32)
+        carried_grad = (sums[CHAN + chan] + gain * grad_own).astype(BF16).astype(F32)
         put(mate, chan, ROWS, 8, long_out)
         put(mate, 2 + chan, ROWS, 8, carried_grad)
         put(mate, 4 + chan, ROWS, 8, carried_grad)
@@ -684,44 +658,97 @@
         after = jnp.concatenate([moved[1:], zeros], axis=0)
         shifted = jnp.where(lane >= COLS - offset, after, moved)
         result = result + weights[None, :, offset : offset + 1] * shifted
+    stage[:, :, 0:COLS] = result.astype(BF16)
+
+    def leave(start, size, index):
+        lanes = pl.ds(start, size)
+        return pltpu.make_async_copy(
+            stage.at[:, :, lanes], out.at[:, :, lanes], out_sems.at[index]
+        )
+
+    leave(0, COLS, 0).start()
+    lane128 = lax.broadcasted_iota(jnp.int32, (FEAT, 128), 1)
+    row_lane = lane128 % 8
+    copies[8].wait()
+    copies[9].wait()
+
+    def chunk(index, proj_sum):
+        base = pl.multiple_of(index * 512, 512)
+        start = pl.multiple_of(index * 8, 8)
+        rows = [
+            jnp.concatenate(
+                [raw[half, pl.ds(chan * ROWS + start, 8), :] for half in range(2)], axis=1
+            )
+            for chan in range(CHAN)
+        ]
+        wide = jnp.concatenate(rows, axis=0)
+        hi = wide.astype(BF16).astype(F32)
+        packed = jnp.concatenate([hi, wide - hi, jnp.zeros((128 - 4 * 8, COLS), F32)], axis=0)
+        turned = jnp.concatenate(
+            [packed[:, half * 128 : half * 128 + 128].T for half in range(2)], axis=0
+        ).astype(BF16)
+        product = dot(act[pl.ds(base, 512), :], turned)
+        for inner in range(8):
+            near = inner * FEAT
+            proj_sum = proj_sum + jnp.where(row_lane == inner, product[near : near + FEAT, :], 0.0)
+        return proj_sum
+
+    proj_sum = lax.fori_loop(0, 8, chunk, jnp.zeros((FEAT, 128), F32), unroll=2)
+    own_lane = lane128 % 16
+    stacked = jnp.concatenate(
+        [jnp.where(own_lane < 8, proj_sum, 0.0), jnp.where(own_lane >= 8, proj_sum, 0.0)], axis=0
+    )
+    proj_wide = lax.dot_general(
+        jnp.ones((8, 128), F32),
+        stacked,
+        (((1,), (1,)), ((), ())),
+        precision=EXACT,
+        preferred_element_type=F32,
+    )
+    proj_hi = proj_wide.astype(BF16).astype(F32)
+    row = lax.broadcasted_iota(jnp.int32, (8, 128), 0)
+    extra = jnp.where(row == 5, proj_hi, proj_wide - proj_hi)
+    stage[:, :, COLS : COLS + 128] = jnp.broadcast_to(extra[None], (ROWS, 8, 128)).astype(BF16)
+    leave(COLS, 128, 1).start()
+    leave(0, COLS, 0).wait()
+    leave(COLS, 128, 1).wait()
+
+
+def compose_kernel(packed, basis_parts, out):
     basis = basis_parts[0]
-    for source in range(1, 16):
+    for source in range(1, 32):
         basis = basis + basis_parts[source]
-    proj_wide = proj_row[...]
-    proj_hi = proj_wide.astype(BF16).astype(F32)
-    proj_lo = proj_wide - proj_hi
-    row = lax.broadcasted_iota(jnp.int32, (8, COLS), 0)
-    extra = jnp.where(row == 7, jnp.concatenate([proj_hi, proj_lo], axis=1), basis)
-    wide = jnp.concatenate([result, jnp.broadcast_to(extra[None], (ROWS, 8, COLS))], axis=1)
-    out[...] = wide.astype(BF16)
+    row = lax.broadcasted_iota(jnp.int32, (8, 128), 0)
+    proj_rows = packed[0, :, COLS : COLS + 128].astype(F32)
+    extra = jnp.where(row < 5, basis, proj_rows)
+    out[:, :, 0:COLS] = packed[:, :, 0:COLS]
+    out[:, :, COLS : COLS + 128] = jnp.broadcast_to(extra[None], (ROWS, 8, 128)).astype(BF16)
 
 
 def unpack_kernel(
     arrived, mixed, grad_query, grad_key, grad_value, proj, basis, wide, sorted_rows
 ):
-    fill(wide, arrived[...].astype(F32))
+    for part in range(3):
+        wide[part] = arrived[:, :, part * 128 : part * 128 + 128].astype(F32).reshape(ROWS * 8, 128)
     for ref, start in ((mixed, 0), (grad_value, 2), (grad_key, 4), (grad_query, 6)):
         for chan in range(CHAN):
-            ref[chan * ROWS : (chan + 1) * ROWS, :] = take(wide, start + chan, ROWS, 16).astype(BF16)
-    last = take(wide, 15, ROWS, 16)
-    both = (last[:, 0:128] + last[:, 128:256]) * (1.0 / math.sqrt(TOTAL))
+            ref[chan * ROWS : (chan + 1) * ROWS, :] = take(wide, start + chan, ROWS, 8).astype(BF16)
+    both = wide[2, pl.ds(5, ROWS, stride=8), :] + wide[2, pl.ds(6, ROWS, stride=8), :]
+    both = both * (1.0 / math.sqrt(TOTAL))
     both = jnp.concatenate([both, jnp.zeros_like(both)], axis=0).T
     proj[:, 0:ROWS] = both[0:FEAT, 0:ROWS]
     proj[:, ROWS : 2 * ROWS] = both[FEAT : 2 * FEAT, 0:ROWS]
     totals = []
-    for core in range(2):
-        pieces = []
-        for half in range(2):
-            total = wide[half, core * 16 + 8 : core * 16 + 16, :]
-            for source in range(core + 2, ROWS, 2):
-                total = total + wide[half, source * 16 + 8 : source * 16 + 16, :]
-            pieces.append(total)
-        totals.append(jnp.concatenate(pieces, axis=1))
+    for quarter in range(4):
+        total = wide[2, quarter * 8 : quarter * 8 + 8, :]
+        for source in range(quarter + 4, ROWS, 4):
+            total = total + wide[2, source * 8 : source * 8 + 8, :]
+        totals.append(total)
     scale = math.sqrt(FEAT / (TOTAL * 1024))
     for group in range(8):
-        lanes = slice(group * 32, group * 32 + 32)
+        lanes = slice(group * 16, group * 16 + 16)
         merged = jnp.concatenate(
-            [totals[0][:, lanes], totals[1][:, lanes], jnp.zeros((8, 64), F32)], axis=1
+            [total[:, lanes] for total in totals] + [jnp.zeros((8, 64), F32)], axis=1
         )
         sorted_rows[pl.ds(group, 8, stride=8), :] = merged * scale
     basis[...] = sorted_rows[0:EMB, 0:FEAT]
@@ -731,6 +758,7 @@
 VMEM = pl.BlockSpec(memory_space=pltpu.VMEM)
 HBM = pl.BlockSpec(memory_space=pltpu.HBM)
 LIMIT = 62 * 1024 * 1024
+ROOMY = 32 * 1024 * 1024
 
 
 def call(kernel, name, own, near, far, outs, scratch, flops, moved, limit=LIMIT):
@@ -796,27 +824,25 @@
     )
 
 
-def run_gradient(own, arrived, short, act, cosine, envelope, columns, consts):
+def run_gradient(own, arrived, short, cosine, envelope, columns, consts):
     names = ("back", "back_turn", "place", "forward", "last", "twiddle", "full")
     return call(
         gradient_kernel,
         "gradient",
         [own],
         [],
-        [arrived, act, cosine, envelope, columns, short] + [consts[name] for name in names],
+        [arrived, envelope, columns, cosine, short] + [consts[name] for name in names],
         [
             (shape((2, ROWS * 8, 128)), True),
             (shape((2 * CHAN * ROWS, 2 * COLS)), True),
-            (shape((2 * CHAN, ROWS, COLS)), True),
-            (shape((8, 128)), False),
-            (shape((16, 8, COLS)), False),
+            (shape((2, CHAN * ROWS, 128)), True),
+            (shape((32, 8, 128)), False),
         ],
         [
             pltpu.VMEM((128, 128), F32),
             pltpu.VMEM((2, CHAN * ROWS, 128), F32),
             pltpu.VMEM((2, ROWS * 8, 128), F32),
             pltpu.VMEM((2 * CHAN * ROWS, 2 * COLS), F32),
-            pltpu.VMEM((2 * CHAN, ROWS, COLS), F32),
             pltpu.SemaphoreType.DMA((3,)),
         ],
         1 << 32,
@@ -824,18 +850,38 @@
     )
 
 
-def run_output(own, skip, short, feat, spec, filter_spec, signals, proj_row, basis_parts, consts):
+def run_output(own, skip, short, feat, spec, filter_spec, raw, act, consts):
     names = ("last", "twiddle", "full")
     return call(
         output_kernel,
         "output",
         [own],
         [],
-        [feat, spec, filter_spec, signals, proj_row, basis_parts, skip, short] + [consts[name] for name in names],
-        [(shape((ROWS, 16, COLS), BF16), False)],
-        [pltpu.VMEM((128, 128), F32), pltpu.VMEM((2, ROWS * 8, 128), F32)],
+        [feat, spec, filter_spec, raw, act, skip, short] + [consts[name] for name in names],
+        [(shape((ROWS, 8, COLS + 128), BF16), True)],
+        [
+            pltpu.VMEM((128, 128), F32),
+            pltpu.VMEM((2, ROWS * 8, 128), F32),
+            pltpu.VMEM((ROWS, 8, COLS + 128), BF16),
+            pltpu.SemaphoreType.DMA((2,)),
+        ],
         1 << 31,
         1 << 22,
+    )[0]
+
+
+def run_compose(packed, basis_parts):
+    return call(
+        compose_kernel,
+        "compose",
+        [],
+        [packed, basis_parts],
+        [],
+        [(shape((ROWS, 8, COLS + 128), BF16), False)],
+        [],
+        1 << 20,
+        1 << 20,
+        ROOMY,
     )[0]
 
 
@@ -848,10 +894,10 @@
         [arrived],
         [],
         [(value, False) for value in [block] * 4 + [shape((FEAT, 128)), shape((EMB, FEAT))]],
-        [pltpu.VMEM((2, ROWS * 16, 128), F32), pltpu.VMEM((64, 128), F32)],
+        [pltpu.VMEM((3, ROWS * 8, 128), F32), pltpu.VMEM((64, 128), F32)],
         1 << 20,
         1 << 20,
-        20 * 1024 * 1024,
+        ROOMY,
     )
 
 
@@ -872,8 +918,8 @@
     )
 
 
-CTX = ("zh", "y", "core")
-PAIR = ("core", "x", "zl")
+CTX = ("zh", "yh", "yl", "core")
+NEAR = ("yl", "core", "x", "zl")
 
 
 def exchange(value, axes):
@@ -905,31 +951,23 @@
         decay_rate.reshape(1, 128),
         consts,
     )
-    feat, spec, signals, proj_row, basis_own = run_gradient(
-        own, arrived, short, act, cosine, envelope, columns, consts
+    feat, spec, raw, basis_own = run_gradient(
+        own, arrived, short, cosine, envelope, columns, consts
     )
     with jax.named_scope("basis"):
-        basis_parts = exchange(basis_own, PAIR)
+        basis_parts = exchange(basis_own, NEAR)
     packed = run_output(
-        own,
-        skip_gain.reshape(1, 128),
-        short,
-        feat,
-        spec,
-        filter_spec,
-        signals,
-        proj_row,
-        basis_parts,
-        consts,
-    )
+        own, skip_gain.reshape(1, 128), short, feat, spec, filter_spec, raw, act, consts
+    )
+    composed = run_compose(packed, basis_parts)
     with jax.named_scope("collect"):
-        returned = exchange(packed, CTX)
+        returned = exchange(composed, CTX)
     mixed, grad_query, grad_key, grad_value, grad_proj, grad_basis = run_unpack(returned)
     return (mixed, grad_query, grad_key, grad_value, grad_proj.T, grad_basis.T)
 
 
 def solution(mesh):
-    finer = Mesh(mesh.devices.reshape(4, 8, 2, 4, 2), ("zh", "y", "core", "x", "zl"))
+    finer = Mesh(mesh.devices.reshape(4, 4, 2, 2, 4, 2), CTX + ("x", "zl"))
     rows = ("x", "zl")
     block = P(rows, CTX)
     return jax.shard_map(

time: 87.9 us -> 80.7 us (0.918)
  blocking collectives: 39.7 us -> 23.5 us
  starting transfers between devices: 17.6 us -> 24.7 us
  local copies, waits for them, and re-layouts: 0.7 us -> 1.7 us
    all_to_all x2 -> x1, blocking collectives: 39.7 us -> 23.5 us  [exchange(): return lax.all_to_all(value, axes, split_axis=0, concat_axis=0, tiled=True)]
    all_to_all x1 -> x2, starting transfers between devices: 17.6 us -> 24.7 us  [exchange(): return lax.all_to_all(value, axes, split_axis=0, concat_axis=0, tiled=True)]
    unnamed x2 -> x4, local copies, waits for them, and re-layouts: 0.7 us -> 1.7 us
    all_to_all x1 -> x2, waiting for transfers between devices: 3.91 us -> 4.62 us  [exchange(): return lax.all_to_all(value, axes, split_axis=0, concat_axis=0, tiled=True)]
    pallas_call x5 -> x6, Pallas kernels: 24.9 us -> 25 us  [call(): pl.pallas_call(kernel, name=name, in_specs=[SMEM] * len(own) + [VMEM] * l...]
  transfers between devices with their start and end apart: 1 -> 2, of which waited for: 1 -> 2; matrix products, arithmetic and copies ran while one was open for 0% -> 0% of each run, Pallas kernels for 11% -> 20%
where the time goes in v3:
time: 80.7 us; the launch traced here: 80.3 us
  Pallas kernels  25 us (31%)
  starting transfers between devices  24.7 us (31%)
  blocking collectives  23.5 us (29%)
  waiting for transfers between devices  4.62 us (6%)
  local copies, waits for them, and re-layouts  1.7 us (2%)
    pallas_call x6, Pallas kernels, call(): pl.pallas_call(kernel, name=name, in_specs=[SMEM] * len(own) + [VMEM] * l...  25 us
    all_to_all x2, starting transfers between devices, exchange(): return lax.all_to_all(value, axes, split_axis=0, concat_axis=0, tiled=True)  24.7 us
    all_to_all x1, blocking collectives, exchange(): return lax.all_to_all(value, axes, split_axis=0, concat_axis=0, tiled=True)  23.5 us
    all_to_all x2, waiting for transfers between devices, exchange(): return lax.all_to_all(value, axes, split_axis=0, concat_axis=0, tiled=True)  4.62 us
    unnamed x4, local copies, waits for them, and re-layouts  1.7 us
  transfers between devices with their start and end apart: 2, of which 2 were waited for; matrix products, arithmetic and copies ran while one was open for 0% of the time, Pallas kernels for 20%

profile of v3, /device:TPU:1, one launch (start us, length us, event | category | flops | bytes accessed | tf_op | source)
XLA Modules:
  0.0 80.3 jit_solution(1492897418892172732)
XLA Ops:
  0.6 2.0 %pack.1 = bf16[64,8,256]{2,1,0:T(8,128)(2,1)} custom-call(bf16[128,256]{1,0:T(8,128)(2,1)} %query.1, bf16[128,256]{1,0:T(8,128)(2,1)} %key.1, bf16[128,256]{1,0:T(8,128)(2,1)} %value.1, bf16[128,256]{1,0:T(8,128)(2,1)} %grad.1), custom_call_target="tpu_custom_call" | custom-call | flops 1048576 | bytes 524288 | tf_op jit(solution)/shard_map/spread/pack/pallas_call | solution.py:766
  2.6 17.6 %all-to-all-start = ((bf16[64,8,256]{2,1,0:T(8,128)(2,1)}), bf16[64,8,256]{2,1,0:T(8,128)(2,1)S(1)}, u32[]{:S(2)}, u32[]{:S(2)}) async-start(bf16[64,8,256]{2,1,0:T(8,128)(2,1)} %pack.1), calls=%async_computation | async-start | bytes 524288 | tf_op jit(solution)/shard_map/spread/all_to_all | solution.py:926
  20.3 9.9 %filter.1 = (bf16[4096,256]{1,0:T(8,128)(2,1)}, bf16[4096,256]{1,0:T(8,128)(2,1)}, f32[128,256]{1,0:T(8,128)}, f32[128,512]{1,0:T(8,128)}, f32[128,128]{1,0:T(8,128)}) custom-call(s32[1]{0:T(128)} %bitcast.own, f32[33,64]{1,0:T(8,128)} %bitcast.11, f32[1,64]{1,0:T(1,128)} %bitcast.15, f32[64,128]{1,0:T(8,128)} %bitcast.9, f32[1,128]{1,0:T(1,128)} %bitcast.16, ...), custom_call_target="tpu_custom_call" | custom-call | flops 8589934592 | bytes 8388608 | tf_op jit(solution)/shard_map/filter/pallas_call | solution.py:766
  30.2 3.9 %all-to-all-done.arrived_src = bf16[64,8,256]{2,1,0:T(8,128)(2,1)S(1)} async-done(((bf16[64,8,256]{2,1,0:T(8,128)(2,1)}), bf16[64,8,256]{2,1,0:T(8,128)(2,1)S(1)}, u32[]{:S(2)}, u32[]{:S(2)}) %all-to-all-start) | async-done | bytes 262176 | tf_op jit(solution)/shard_map/spread/all_to_all | solution.py:926
  34.1 0.0 copy-start.1
  34.1 0.7 copy-done.1
  34.8 6.1 %gradient.1 = (f32[2,512,128]{2,1,0:T(8,128)}, f32[256,512]{1,0:T(8,128)}, f32[2,128,128]{2,1,0:T(8,128)}, f32[32,8,128]{2,1,0:T(8,128)}) custom-call(s32[1]{0:T(128)} %bitcast.own, bf16[64,8,256]{2,1,0:T(8,128)(2,1)} %copy-done.1, f32[128,256]{1,0:T(8,128)} %get-tuple-element.21.envelope_src, f32[128,128]{1,0:T(8,128)} %get-tuple-element.22.columns_src, ...), custom_call_target="tpu_custom_call" | custom-call | flops 4294967296 | bytes 8388608 | tf_op jit(solution)/shard_map/gradient/pallas_call | solution.py:766
  40.9 7.1 %all-to-all-start.1 = ((f32[32,8,128]{2,1,0:T(8,128)}), f32[32,8,128]{2,1,0:T(8,128)S(1)}, u32[]{:S(2)}, u32[]{:S(2)}) async-start(f32[32,8,128]{2,1,0:T(8,128)} %get-tuple-element.29), calls=%async_computation.1 | async-start | bytes 262144 | tf_op jit(solution)/shard_map/basis/all_to_all | solution.py:926
  48.0 6.1 %output.1.packed = bf16[64,8,384]{2,1,0:T(8,128)(2,1)} custom-call(s32[1]{0:T(128)} %bitcast.own, f32[2,512,128]{2,1,0:T(8,128)} %get-tuple-element.24.feat_src, f32[256,512]{1,0:T(8,128)} %get-tuple-element.25.spec_src, f32[128,512]{1,0:T(8,128)} %get-tuple-element.26.filter_spec_src, f32[2,128,128]{2,1,0:T(8,128)} %get-tuple-element.27.raw_src, ...), custom_call_target="tpu_custom_call" | custom-call | flops 2147483648 | bytes 4194304 | tf_op jit(solution)/shard_map/output/pallas_call | solution.py:766
  54.1 0.7 all-to-all-done.1.basis_parts
  54.8 0.0 copy-start
  54.8 1.0 %copy-done = bf16[64,8,384]{2,1,0:T(8,128)(2,1)S(1)} copy-done((bf16[64,8,384]{2,1,0:T(8,128)(2,1)S(1)}, bf16[64,8,384]{2,1,0:T(8,128)(2,1)}, u32[]{:S(2)}) %copy-start) | copy-done | bytes 393240
  55.8 0.1 compose.1
  55.9 23.5 %all_to_all.15.arrived = bf16[64,8,384]{2,1,0:T(8,128)(2,1)S(1)} all-to-all(bf16[64,8,384]{2,1,0:T(8,128)(2,1)S(1)} %compose.1), channel_id=1, replica_groups=mesh['zh'=4,'yh'=4,'yl'=2,'core'=2,'x'=4,'zl'=2] {'zh','yh','yl','core'}, dimensions={0} | all-to-all | bytes 786432 | tf_op jit(solution)/shard_map/collect/all_to_all | solution.py:926
  79.4 0.9 %unpack.1 = (bf16[128,256]{1,0:T(8,128)(2,1)}, bf16[128,256]{1,0:T(8,128)(2,1)}, bf16[128,256]{1,0:T(8,128)(2,1)}, bf16[128,256]{1,0:T(8,128)(2,1)}, f32[64,128]{1,0:T(8,128)}, /*index=5*/f32[33,64]{1,0:T(8,128)}) custom-call(bf16[64,8,384]{2,1,0:T(8,128)(2,1)S(1)} %all_to_all.15.arrived), custom_call_target="tpu_custom_call" | custom-call | flops 1048576 | bytes 1048576 | tf_op jit(solution)/shard_map/unpack/pallas_call | solution.py:766
Async XLA Ops:
  2.6 31.5 %all-to-all-start = ((bf16[64,8,256]{2,1,0:T(8,128)(2,1)}), bf16[64,8,256]{2,1,0:T(8,128)(2,1)S(1)}, u32[]{:S(2)}, u32[]{:S(2)}) async-start(bf16[64,8,256]{2,1,0:T(8,128)(2,1)} %pack.1), calls=%async_computation | async-start | bytes 524288 | tf_op jit(solution)/shard_map/spread/all_to_all | solution.py:926
  34.1 0.7 copy-start.1
  40.9 13.9 %all-to-all-start.1 = ((f32[32,8,128]{2,1,0:T(8,128)}), f32[32,8,128]{2,1,0:T(8,128)S(1)}, u32[]{:S(2)}, u32[]{:S(2)}) async-start(f32[32,8,128]{2,1,0:T(8,128)} %get-tuple-element.29), calls=%async_computation.1 | async-start | bytes 262144 | tf_op jit(solution)/shard_map/basis/all_to_all | solution.py:926
  54.8 1.0 %copy-start = (bf16[64,8,384]{2,1,0:T(8,128)(2,1)S(1)}, bf16[64,8,384]{2,1,0:T(8,128)(2,1)}, u32[]{:S(2)}) copy-start(bf16[64,8,384]{2,1,0:T(8,128)(2,1)} %output.1.packed) | copy-start | bytes 1179652

commit v4 on v3

--- a/solution.py
+++ b/solution.py
@@ -556,6 +556,9 @@
         copy.wait()
 
 
+HALO = TAPS - 1
+
+
 def output_kernel(
     own,
     feat_src,
@@ -563,8 +566,8 @@
     filter_spec_src,
     raw_src,
     act_src,
+    arrived_src,
     skip_src,
-    short_src,
     last_src,
     twiddle_src,
     full_src,
@@ -574,34 +577,71 @@
     filter_spec,
     raw,
     act,
+    arrived,
     skip,
-    short,
     last,
     twiddle,
     full,
-    taps,
-    mate,
-    stage,
-    out_sems,
+    input_tail,
+    rows_out,
     sems,
 ):
     first = own[0]
     copies = begin(
         sems,
         [
+            (raw_src, raw),
+            (act_src, act),
             (spec_src, spec),
             (filter_spec_src, filter_spec),
             (full_src, full),
             (twiddle_src, twiddle),
             (last_src, last),
             (skip_src, skip),
-            (short_src, short),
             (feat_src, feat),
-            (raw_src, raw),
-            (act_src, act),
+            (arrived_src, arrived),
         ],
     )
-    for copy in copies[0:5]:
+    lane128 = lax.broadcasted_iota(jnp.int32, (FEAT, 128), 1)
+    row_lane = lane128 % 8
+    copies[0].wait()
+    copies[1].wait()
+
+    def chunk(index, proj_sum):
+        base = pl.multiple_of(index * 512, 512)
+        start = pl.multiple_of(index * 8, 8)
+        rows = [
+            jnp.concatenate(
+                [raw[half, pl.ds(chan * ROWS + start, 8), :] for half in range(2)], axis=1
+            )
+            for chan in range(CHAN)
+        ]
+        wide = jnp.concatenate(rows, axis=0)
+        hi = wide.astype(BF16).astype(F32)
+        packed = jnp.concatenate([hi, wide - hi, jnp.zeros((128 - 4 * 8, COLS), F32)], axis=0)
+        turned = jnp.concatenate(
+            [packed[:, half * 128 : half * 128 + 128].T for half in range(2)], axis=0
+        ).astype(BF16)
+        product = dot(act[pl.ds(base, 512), :], turned)
+        for inner in range(8):
+            near = inner * FEAT
+            proj_sum = proj_sum + jnp.where(row_lane == inner, product[near : near + FEAT, :], 0.0)
+        return proj_sum
+
+    proj_sum = lax.fori_loop(0, 8, chunk, jnp.zeros((FEAT, 128), F32), unroll=2)
+    own_lane = lane128 % 16
+    stacked = jnp.concatenate(
+        [jnp.where(own_lane < 8, proj_sum, 0.0), jnp.where(own_lane >= 8, proj_sum, 0.0)], axis=0
+    )
+    proj_wide = lax.dot_general(
+        jnp.ones((8, 128), F32),
+        stacked,
+        (((1,), (1,)), ((), ())),
+        precision=EXACT,
+        preferred_element_type=F32,
+    )
+    proj_hi = proj_wide.astype(BF16).astype(F32)
+    for copy in copies[2:7]:
         copy.wait()
     tables = (twiddle[0], twiddle[1], full[0], full[1])
     carried, grad = spec[0 : CHAN * ROWS, :], spec[CHAN * ROWS : 2 * CHAN * ROWS, :]
@@ -629,89 +669,48 @@
         axis=0,
     )
     sums = restore(crossed, 2 * CHAN, last[...], *tables)
-    for copy in copies[5:8]:
+    for copy in copies[7:]:
         copy.wait()
-    weights = own_taps(first, short, taps, ((2, 2), (4, 1), (6, 0)))
+    input_tail[...] = arrived[:, :, 128:256].astype(F32).reshape(ROWS * 8, 128)
 
     def plane(index):
         return take(feat, index, ROWS, 8)
 
+    blank = jnp.zeros((1, 128), F32)
     for chan in range(CHAN):
         gain = picked(skip[...], first + 64 * chan)
-        carried_own = (plane(2 + chan) * plane(4 + chan)).astype(BF16).astype(F32)
-        grad_own = (plane(chan) * plane(6 + chan)).astype(BF16).astype(F32)
+        query, key, value, cotangent = [plane(2 * index + chan) for index in range(4)]
+        carried_own = (key * value).astype(BF16).astype(F32)
+        grad_own = (query * cotangent).astype(BF16).astype(F32)
         long_out = (sums[chan] + gain * carried_own).astype(BF16).astype(F32)
         carried_grad = (sums[CHAN + chan] + gain * grad_own).astype(BF16).astype(F32)
-        put(mate, chan, ROWS, 8, long_out)
-        put(mate, 2 + chan, ROWS, 8, carried_grad)
-        put(mate, 4 + chan, ROWS, 8, carried_grad)
-        put(mate, 6 + chan, ROWS, 8, long_out)
-    signal = jnp.concatenate(
-        [(feat[half] * mate[half]).astype(BF16).astype(F32).reshape(ROWS, 8, 128) for half in range(2)],
-        axis=2,
-    )
-    lane = lax.broadcasted_iota(jnp.int32, (ROWS, 8, COLS), 2)
-    result = weights[None, :, 0:1] * signal
-    zeros = jnp.zeros((1, 8, COLS), F32)
-    for offset in range(1, TAPS):
-        moved = pltpu.roll(signal, COLS - offset, 2)
-        after = jnp.concatenate([moved[1:], zeros], axis=0)
-        shifted = jnp.where(lane >= COLS - offset, after, moved)
-        result = result + weights[None, :, offset : offset + 1] * shifted
-    stage[:, :, 0:COLS] = result.astype(BF16)
-
-    def leave(start, size, index):
-        lanes = pl.ds(start, size)
-        return pltpu.make_async_copy(
-            stage.at[:, :, lanes], out.at[:, :, lanes], out_sems.at[index]
+        put(rows_out, chan, ROWS, 8, long_out)
+        put(rows_out, 2 + chan, ROWS, 8, carried_grad)
+        follow = jnp.zeros((ROWS, 128), F32)
+        before = jnp.zeros((ROWS, 128), F32)
+        heads = (
+            cotangent[:, 0:128] * long_out[:, 0:128],
+            carried_grad[:, 0:128] * value[:, 0:128],
+            carried_grad[:, 0:128] * key[:, 0:128],
         )
-
-    leave(0, COLS, 0).start()
-    lane128 = lax.broadcasted_iota(jnp.int32, (FEAT, 128), 1)
-    row_lane = lane128 % 8
-    copies[8].wait()
-    copies[9].wait()
-
-    def chunk(index, proj_sum):
-        base = pl.multiple_of(index * 512, 512)
-        start = pl.multiple_of(index * 8, 8)
-        rows = [
-            jnp.concatenate(
-                [raw[half, pl.ds(chan * ROWS + start, 8), :] for half in range(2)], axis=1
-            )
-            for chan in range(CHAN)
-        ]
-        wide = jnp.concatenate(rows, axis=0)
-        hi = wide.astype(BF16).astype(F32)
-        packed = jnp.concatenate([hi, wide - hi, jnp.zeros((128 - 4 * 8, COLS), F32)], axis=0)
-        turned = jnp.concatenate(
-            [packed[:, half * 128 : half * 128 + 128].T for half in range(2)], axis=0
-        ).astype(BF16)
-        product = dot(act[pl.ds(base, 512), :], turned)
-        for inner in range(8):
-            near = inner * FEAT
-            proj_sum = proj_sum + jnp.where(row_lane == inner, product[near : near + FEAT, :], 0.0)
-        return proj_sum
-
-    proj_sum = lax.fori_loop(0, 8, chunk, jnp.zeros((FEAT, 128), F32), unroll=2)
-    own_lane = lane128 % 16
-    stacked = jnp.concatenate(
-        [jnp.where(own_lane < 8, proj_sum, 0.0), jnp.where(own_lane >= 8, proj_sum, 0.0)], axis=0
-    )
-    proj_wide = lax.dot_general(
-        jnp.ones((8, 128), F32),
-        stacked,
-        (((1,), (1,)), ((), ())),
-        precision=EXACT,
-        preferred_element_type=F32,
-    )
-    proj_hi = proj_wide.astype(BF16).astype(F32)
-    row = lax.broadcasted_iota(jnp.int32, (8, 128), 0)
-    extra = jnp.where(row == 5, proj_hi, proj_wide - proj_hi)
-    stage[:, :, COLS : COLS + 128] = jnp.broadcast_to(extra[None], (ROWS, 8, 128)).astype(BF16)
-    leave(COLS, 128, 1).start()
-    leave(0, COLS, 0).wait()
-    leave(COLS, 128, 1).wait()
+        for index in range(3):
+            head = heads[index].astype(BF16).astype(F32)
+            place = HALO * index
+            head = pltpu.roll(head, place, 1) if place else head
+            follow = jnp.where((lane128 >= place) & (lane128 < place + HALO), head, follow)
+            tail = input_tail[pl.ds(2 * index + chan, ROWS, stride=8), :]
+            place = HALO * (3 + index)
+            tail = pltpu.roll(tail, HALO + place, 1)
+            before = jnp.where((lane128 >= place) & (lane128 < place + HALO), tail, before)
+        halo = jnp.concatenate([follow[1:], blank], axis=0) + jnp.concatenate(
+            [blank, before[:-1]], axis=0
+        )
+        rows_out[chan, pl.ds(4, ROWS, stride=8), :] = halo
+    row = lax.broadcasted_iota(jnp.int32, (ROWS, 8, 128), 1)
+    for half, proj_part in enumerate((proj_hi, proj_wide - proj_hi)):
+        extra = jnp.where(row == 7, proj_part[None], 0.0)
+        value = jnp.where(row < 5, rows_out[half].reshape(ROWS, 8, 128), extra)
+        out[:, :, half * 128 : half * 128 + 128] = value.astype(BF16)
 
 
 def compose_kernel(packed, basis_parts, out):
@@ -719,38 +718,135 @@
     for source in range(1, 32):
         basis = basis + basis_parts[source]
     row = lax.broadcasted_iota(jnp.int32, (8, 128), 0)
-    proj_rows = packed[0, :, COLS : COLS + 128].astype(F32)
-    extra = jnp.where(row < 5, basis, proj_rows)
-    out[:, :, 0:COLS] = packed[:, :, 0:COLS]
-    out[:, :, COLS : COLS + 128] = jnp.broadcast_to(extra[None], (ROWS, 8, 128)).astype(BF16)
+    lane = lax.broadcasted_iota(jnp.int32, (8, 128), 1)
+    last = jnp.where((lane >= 64) & (lane < 80), pltpu.roll(basis, 64, 1)[4:5], 0.0)
+    left = jnp.where(
+        row == 4, last, jnp.where(row == 5, basis[0:1], jnp.where(row == 6, basis[2:3], 0.0))
+    )
+    right = jnp.where(row == 5, basis[1:2], jnp.where(row == 6, basis[3:4], 0.0))
+    extra = jnp.concatenate([left, right], axis=1)
+    out[...] = (packed[...].astype(F32) + extra[None]).astype(BF16)
+
+
+def local_kernel(
+    query_src, key_src, value_src, short_src, feat_out, taps_out, query, key, value, short, sems
+):
+    copies = begin(
+        sems, [(query_src, query), (key_src, key), (value_src, value), (short_src, short)]
+    )
+    lane = lax.broadcasted_iota(jnp.int32, (128, 128), 1)
+    for copy in copies:
+        copy.wait()
+    for index, ref in enumerate((query, key, value)):
+        taps_out[index] = jnp.concatenate(
+            [short[index], jnp.zeros((128 - TAPS, 128), F32)], axis=0
+        ).T
+        weights = taps_out[index]
+        block = ref[...].astype(F32)
+        left, right = block[:, 0:128], block[:, 128:256]
+        out_left = weights[:, 0:1] * left
+        out_right = weights[:, 0:1] * right
+        for offset in range(1, TAPS):
+            weight = weights[:, offset : offset + 1]
+            moved_left = pltpu.roll(left, offset, 1)
+            moved_right = pltpu.roll(right, offset, 1)
+            out_left = out_left + weight * jnp.where(lane < offset, 0.0, moved_left)
+            out_right = out_right + weight * jnp.where(lane < offset, moved_left, moved_right)
+        feat_out[index, :, 0:128] = out_left
+        feat_out[index, :, 128:256] = out_right
 
 
 def unpack_kernel(
-    arrived, mixed, grad_query, grad_key, grad_value, proj, basis, wide, sorted_rows
+    arrived,
+    feat_src,
+    taps_src,
+    grad_src,
+    mixed,
+    grad_query,
+    grad_key,
+    grad_value,
+    proj,
+    basis,
+    feat,
+    taps,
+    grad,
+    wide,
+    sorted_rows,
+    sems,
 ):
-    for part in range(3):
-        wide[part] = arrived[:, :, part * 128 : part * 128 + 128].astype(F32).reshape(ROWS * 8, 128)
-    for ref, start in ((mixed, 0), (grad_value, 2), (grad_key, 4), (grad_query, 6)):
-        for chan in range(CHAN):
-            ref[chan * ROWS : (chan + 1) * ROWS, :] = take(wide, start + chan, ROWS, 8).astype(BF16)
-    both = wide[2, pl.ds(5, ROWS, stride=8), :] + wide[2, pl.ds(6, ROWS, stride=8), :]
-    both = both * (1.0 / math.sqrt(TOTAL))
-    both = jnp.concatenate([both, jnp.zeros_like(both)], axis=0).T
-    proj[:, 0:ROWS] = both[0:FEAT, 0:ROWS]
-    proj[:, ROWS : 2 * ROWS] = both[FEAT : 2 * FEAT, 0:ROWS]
+    copies = begin(sems, [(feat_src, feat), (taps_src, taps), (grad_src, grad)])
+    fill(wide, arrived[...].astype(F32))
+
+    def both(half, row):
+        return jnp.concatenate(
+            [wide[half, pl.ds(row + chan, ROWS, stride=8), :] for chan in range(CHAN)], axis=0
+        )
+
+    long_out = [both(half, 0) for half in range(2)]
+    carried_grad = [both(half, 2) for half in range(2)]
+    halo = jnp.concatenate([wide[half, pl.ds(4, ROWS, stride=8), :] for half in range(2)], axis=0)
+    lane = lax.broadcasted_iota(jnp.int32, (128, 128), 1)
+    for copy in copies:
+        copy.wait()
+    feats = []
+    for index in range(3):
+        left = feat[index, :, 0:128]
+        for offset in range(1, TAPS):
+            moved = pltpu.roll(halo, (offset - HALO * (4 + index)) % 128, 1)
+            left = left + taps[index, :, offset : offset + 1] * jnp.where(lane < offset, moved, 0.0)
+        feats.append((left, feat[index, :, 128:256]))
+    cotangent = grad[...].astype(F32)
+    cotangent = (cotangent[:, 0:128], cotangent[:, 128:256])
+    for half in range(2):
+        mixed[:, half * 128 : half * 128 + 128] = (feats[0][half] * long_out[half]).astype(BF16)
+    grads = (
+        [cotangent[half] * long_out[half] for half in range(2)],
+        [carried_grad[half] * feats[2][half] for half in range(2)],
+        [carried_grad[half] * feats[1][half] for half in range(2)],
+    )
+    for index, ref in enumerate((grad_query, grad_key, grad_value)):
+        left, right = [part.astype(BF16).astype(F32) for part in grads[index]]
+        out_left = taps[index, :, 0:1] * left
+        out_right = taps[index, :, 0:1] * right
+        for offset in range(1, TAPS):
+            weight = taps[index, :, offset : offset + 1]
+            moved_left = pltpu.roll(left, 128 - offset, 1)
+            moved_right = pltpu.roll(right, 128 - offset, 1)
+            moved_halo = pltpu.roll(halo, (128 - offset - HALO * index) % 128, 1)
+            edge = lane >= 128 - offset
+            out_left = out_left + weight * jnp.where(edge, moved_right, moved_left)
+            out_right = out_right + weight * jnp.where(edge, moved_halo, moved_right)
+        ref[:, 0:128] = out_left.astype(BF16)
+        ref[:, 128:256] = out_right.astype(BF16)
+    rows = wide[0, pl.ds(7, ROWS, stride=8), :] + wide[1, pl.ds(7, ROWS, stride=8), :]
+    rows = rows * (1.0 / math.sqrt(TOTAL))
+    rows = jnp.concatenate([rows, jnp.zeros_like(rows)], axis=0).T
+    proj[:, 0:ROWS] = rows[0:FEAT, 0:ROWS]
+    proj[:, ROWS : 2 * ROWS] = rows[FEAT : 2 * FEAT, 0:ROWS]
     totals = []
     for quarter in range(4):
-        total = wide[2, quarter * 8 : quarter * 8 + 8, :]
-        for source in range(quarter + 4, ROWS, 4):
-            total = total + wide[2, source * 8 : source * 8 + 8, :]
-        totals.append(total)
+        pair = []
+        for half in range(2):
+            total = wide[half, quarter * 8 : quarter * 8 + 8, :]
+            for source in range(quarter + 4, ROWS, 4):
+                total = total + wide[half, source * 8 : source * 8 + 8, :]
+            pair.append(total)
+        totals.append(pair)
     scale = math.sqrt(FEAT / (TOTAL * 1024))
+    ordered = [
+        jnp.concatenate([left[5:6], right[5:6], left[6:7], right[6:7]], axis=0)
+        for left, right in totals
+    ]
     for group in range(8):
         lanes = slice(group * 16, group * 16 + 16)
         merged = jnp.concatenate(
-            [total[:, lanes] for total in totals] + [jnp.zeros((8, 64), F32)], axis=1
+            [value[:, lanes] for value in ordered] + [jnp.zeros((4, 64), F32)], axis=1
         )
-        sorted_rows[pl.ds(group, 8, stride=8), :] = merged * scale
+        sorted_rows[pl.ds(group, 4, stride=8), :] = merged * scale
+    sorted_rows[32:33, :] = (
+        jnp.concatenate([left[4:5, 64:80] for left, _ in totals] + [jnp.zeros((1, 64), F32)], axis=1)
+        * scale
+    )
     basis[...] = sorted_rows[0:EMB, 0:FEAT]
 
 
@@ -850,21 +946,16 @@
     )
 
 
-def run_output(own, skip, short, feat, spec, filter_spec, raw, act, consts):
+def run_output(own, skip, feat, spec, filter_spec, raw, act, arrived, consts):
     names = ("last", "twiddle", "full")
     return call(
         output_kernel,
         "output",
         [own],
         [],
-        [feat, spec, filter_spec, raw, act, skip, short] + [consts[name] for name in names],
-        [(shape((ROWS, 8, COLS + 128), BF16), True)],
-        [
-            pltpu.VMEM((128, 128), F32),
-            pltpu.VMEM((2, ROWS * 8, 128), F32),
-            pltpu.VMEM((ROWS, 8, COLS + 128), BF16),
-            pltpu.SemaphoreType.DMA((2,)),
-        ],
+        [feat, spec, filter_spec, raw, act, arrived, skip] + [consts[name] for name in names],
+        [(shape((ROWS, 8, COLS), BF16), False)],
+        [pltpu.VMEM((ROWS * 8, 128), F32), pltpu.VMEM((2, ROWS * 8, 128), F32)],
         1 << 31,
         1 << 22,
     )[0]
@@ -877,7 +968,7 @@
         [],
         [packed, basis_parts],
         [],
-        [(shape((ROWS, 8, COLS + 128), BF16), False)],
+        [(shape((ROWS, 8, COLS), BF16), False)],
         [],
         1 << 20,
         1 << 20,
@@ -885,16 +976,30 @@
     )[0]
 
 
-def run_unpack(arrived):
+def run_local(query_in, key_in, value_in, short):
+    return call(
+        local_kernel,
+        "local",
+        [],
+        [],
+        [query_in, key_in, value_in, short],
+        [(shape((3, 128, COLS)), False), (shape((3, 128, 128)), False)],
+        [],
+        1 << 28,
+        1 << 20,
+    )
+
+
+def run_unpack(arrived, feat, taps, grad_out):
     block = shape((128, COLS), BF16)
     return call(
         unpack_kernel,
         "unpack",
         [],
         [arrived],
-        [],
+        [feat, taps, grad_out],
         [(value, False) for value in [block] * 4 + [shape((FEAT, 128)), shape((EMB, FEAT))]],
-        [pltpu.VMEM((3, ROWS * 8, 128), F32), pltpu.VMEM((64, 128), F32)],
+        [pltpu.VMEM((2, ROWS * 8, 128), F32), pltpu.VMEM((64, 128), F32)],
         1 << 20,
         1 << 20,
         ROOMY,
@@ -943,6 +1048,7 @@
     with jax.named_scope("spread"):
         arrived = exchange(run_pack(query_in, key_in, value_in, grad_out), CTX)
     short = short_kernel.transpose(0, 2, 1)
+    block_feat, block_taps = run_local(query_in, key_in, value_in, short)
     act, cosine, envelope, filter_spec, columns = run_filter(
         own,
         basis_weight.T,
@@ -957,12 +1063,14 @@
     with jax.named_scope("basis"):
         basis_parts = exchange(basis_own, NEAR)
     packed = run_output(
-        own, skip_gain.reshape(1, 128), short, feat, spec, filter_spec, raw, act, consts
+        own, skip_gain.reshape(1, 128), feat, spec, filter_spec, raw, act, arrived, consts
     )
     composed = run_compose(packed, basis_parts)
     with jax.named_scope("collect"):
         returned = exchange(composed, CTX)
-    mixed, grad_query, grad_key, grad_value, grad_proj, grad_basis = run_unpack(returned)
+    mixed, grad_query, grad_key, grad_value, grad_proj, grad_basis = run_unpack(
+        returned, block_feat, block_taps, grad_out
+    )
     return (mixed, grad_query, grad_key, grad_value, grad_proj.T, grad_basis.T)
 
 

time: 80.7 us -> 83.8 us (1.038)
  blocking collectives: 23.5 us -> 0 us
  waiting for transfers between devices: 4.62 us -> 16.2 us
  starting transfers between devices: 24.7 us -> 32.4 us
  Pallas kernels: 25 us -> 30.4 us
  local copies, waits for them, and re-layouts: 1.7 us -> 3.59 us
    all_to_all x1 -> x0, blocking collectives: 23.5 us -> none  [exchange(): return lax.all_to_all(value, axes, split_axis=0, concat_axis=0, tiled=True)]
    all_to_all x2 -> x3, waiting for transfers between devices: 4.62 us -> 16.2 us  [exchange(): return lax.all_to_all(value, axes, split_axis=0, concat_axis=0, tiled=True)]
    all_to_all x2 -> x3, starting transfers between devices: 24.7 us -> 32.4 us  [exchange(): return lax.all_to_all(value, axes, split_axis=0, concat_axis=0, tiled=True)]
    pallas_call x6 -> x7, Pallas kernels: 25 us -> 30.4 us  [call(): pl.pallas_call(kernel, name=name, in_specs=[SMEM] * len(own) + [VMEM] * l...]
    unnamed x4 -> x10, local copies, waits for them, and re-layouts: 1.7 us -> 3.59 us
  transfers between devices with their start and end apart: 2 -> 3, of which waited for: 2 -> 3; matrix products, arithmetic and copies ran while one was open for 0% -> 0% of each run, Pallas kernels for 20% -> 22%
where the time goes in v4:
time: 83.8 us; the launch traced here: 83.3 us
  starting transfers between devices  32.4 us (39%)
  Pallas kernels  30.4 us (36%)
  waiting for transfers between devices  16.2 us (19%)
  local copies, waits for them, and re-layouts  3.59 us (4%)
    all_to_all x3, starting transfers between devices, exchange(): return lax.all_to_all(value, axes, split_axis=0, concat_axis=0, tiled=True)  32.4 us
    pallas_call x7, Pallas kernels, call(): pl.pallas_call(kernel, name=name, in_specs=[SMEM] * len(own) + [VMEM] * l...  30.4 us
    all_to_all x3, waiting for transfers between devices, exchange(): return lax.all_to_all(value, axes, split_axis=0, concat_axis=0, tiled=True)  16.2 us
    unnamed x10, local copies, waits for them, and re-layouts  3.59 us
  transfers between devices with their start and end apart: 3, of which 3 were waited for; matrix products, arithmetic and copies ran while one was open for 0% of the time, Pallas kernels for 22%

profile of v4, /device:TPU:1, one launch (start us, length us, event | category | flops | bytes accessed | tf_op | source)
XLA Modules:
  0.0 83.3 jit_solution(504311845063027150)
XLA Ops:
  0.6 2.0 %pack.1 = bf16[64,8,256]{2,1,0:T(8,128)(2,1)} custom-call(bf16[128,256]{1,0:T(8,128)(2,1)} %query_src.1, bf16[128,256]{1,0:T(8,128)(2,1)} %key_src.1, bf16[128,256]{1,0:T(8,128)(2,1)} %value_src.1, bf16[128,256]{1,0:T(8,128)(2,1)} %grad_src.1), custom_call_target="tpu_custom_call" | custom-call | flops 1048576 | bytes 524288 | tf_op jit(solution)/shard_map/spread/pack/pallas_call | solution.py:862
  2.6 17.6 %all-to-all-start = ((bf16[64,8,256]{2,1,0:T(8,128)(2,1)}), bf16[64,8,256]{2,1,0:T(8,128)(2,1)S(1)}, u32[]{:S(2)}, u32[]{:S(2)}) async-start(bf16[64,8,256]{2,1,0:T(8,128)(2,1)} %pack.1), calls=%async_computation | async-start | bytes 524288 | tf_op jit(solution)/shard_map/spread/all_to_all | solution.py:1031
  20.3 9.9 %filter.1 = (bf16[4096,256]{1,0:T(8,128)(2,1)}, bf16[4096,256]{1,0:T(8,128)(2,1)}, f32[128,256]{1,0:T(8,128)}, f32[128,512]{1,0:T(8,128)}, f32[128,128]{1,0:T(8,128)}) custom-call(s32[1]{0:T(128)} %bitcast.own, f32[33,64]{1,0:T(8,128)} %bitcast.11, f32[1,64]{1,0:T(1,128)} %bitcast.15, f32[64,128]{1,0:T(8,128)} %bitcast.9, f32[1,128]{1,0:T(1,128)} %bitcast.16, ...), custom_call_target="tpu_custom_call" | custom-call | flops 8589934592 | bytes 8388608 | tf_op jit(solution)/shard_map/filter/pallas_call | solution.py:862
  30.2 3.9 %all-to-all-done.arrived_src = bf16[64,8,256]{2,1,0:T(8,128)(2,1)S(1)} async-done(((bf16[64,8,256]{2,1,0:T(8,128)(2,1)}), bf16[64,8,256]{2,1,0:T(8,128)(2,1)S(1)}, u32[]{:S(2)}, u32[]{:S(2)}) %all-to-all-start) | async-done | bytes 262176 | tf_op jit(solution)/shard_map/spread/all_to_all | solution.py:1031
  34.1 0.0 copy-start.4
  34.1 0.7 copy-done.4
  34.8 6.1 %gradient.1 = (f32[2,512,128]{2,1,0:T(8,128)}, f32[256,512]{1,0:T(8,128)}, f32[2,128,128]{2,1,0:T(8,128)}, f32[32,8,128]{2,1,0:T(8,128)}) custom-call(s32[1]{0:T(128)} %bitcast.own, bf16[64,8,256]{2,1,0:T(8,128)(2,1)} %copy-done.4, f32[128,256]{1,0:T(8,128)} %get-tuple-element.23.envelope_src, f32[128,128]{1,0:T(8,128)} %get-tuple-element.24.columns_src, ...), custom_call_target="tpu_custom_call" | custom-call | flops 4294967296 | bytes 8388608 | tf_op jit(solution)/shard_map/gradient/pallas_call | solution.py:862
  41.0 7.1 %all-to-all-start.1 = ((f32[32,8,128]{2,1,0:T(8,128)}), f32[32,8,128]{2,1,0:T(8,128)S(1)}, u32[]{:S(2)}, u32[]{:S(2)}) async-start(f32[32,8,128]{2,1,0:T(8,128)} %get-tuple-element.31), calls=%async_computation.1 | async-start | bytes 262144 | tf_op jit(solution)/shard_map/basis/all_to_all | solution.py:1031
  48.1 5.7 %output.1.packed = bf16[64,8,256]{2,1,0:T(8,128)(2,1)} custom-call(s32[1]{0:T(128)} %bitcast.own, f32[2,512,128]{2,1,0:T(8,128)} %get-tuple-element.26.feat_src, f32[256,512]{1,0:T(8,128)} %get-tuple-element.27.spec_src, f32[128,512]{1,0:T(8,128)} %get-tuple-element.28.filter_spec_src, f32[2,128,128]{2,1,0:T(8,128)} %get-tuple-element.29.raw_src, ...), custom_call_target="tpu_custom_call" | custom-call | flops 2147483648 | bytes 4194304 | tf_op jit(solution)/shard_map/output/pallas_call | solution.py:862
  53.8 0.0 copy-start.1
  53.8 1.0 %all-to-all-done.1.basis_parts = f32[32,8,128]{2,1,0:T(8,128)S(1)} async-done(((f32[32,8,128]{2,1,0:T(8,128)}), f32[32,8,128]{2,1,0:T(8,128)S(1)}, u32[]{:S(2)}, u32[]{:S(2)}) %all-to-all-start.1) | async-done | bytes 131104 | tf_op jit(solution)/shard_map/basis/all_to_all | solution.py:1031
  54.9 0.0 copy-start.2
  54.9 0.9 %copy-done.2 = bf16[64,8,256]{2,1,0:T(8,128)(2,1)S(1)} copy-done((bf16[64,8,256]{2,1,0:T(8,128)(2,1)S(1)}, bf16[64,8,256]{2,1,0:T(8,128)(2,1)}, u32[]{:S(2)}) %copy-start.2) | copy-done | bytes 262168
  55.8 0.8 %compose.1 = bf16[64,8,256]{2,1,0:T(8,128)(2,1)} custom-call(bf16[64,8,256]{2,1,0:T(8,128)(2,1)S(1)} %copy-done.2, f32[32,8,128]{2,1,0:T(8,128)S(1)} %all-to-all-done.1.basis_parts), custom_call_target="tpu_custom_call" | custom-call | flops 1048576 | bytes 1048576 | tf_op jit(solution)/shard_map/compose/pallas_call | solution.py:862
  56.7 7.7 %all-to-all-start.2 = ((bf16[64,8,256]{2,1,0:T(8,128)(2,1)}), bf16[64,8,256]{2,1,0:T(8,128)(2,1)S(1)}, u32[]{:S(2)}, u32[]{:S(2)}) async-start(bf16[64,8,256]{2,1,0:T(8,128)(2,1)} %compose.1), calls=%async_computation.2 | async-start | bytes 524288 | tf_op jit(solution)/shard_map/collect/all_to_all | solution.py:1031
  64.3 2.6 %local.1 = (f32[3,128,256]{2,1,0:T(8,128)}, f32[3,128,128]{2,1,0:T(8,128)}) custom-call(bf16[128,256]{1,0:T(8,128)(2,1)} %query_src.1, bf16[128,256]{1,0:T(8,128)(2,1)} %key_src.1, bf16[128,256]{1,0:T(8,128)(2,1)} %value_src.1, f32[3,7,128]{2,1,0:T(8,128)} %bitcast.14), custom_call_target="tpu_custom_call" | custom-call | flops 268435456 | bytes 1048576 | tf_op jit(solution)/shard_map/local/pallas_call | solution.py:862
  67.0 11.2 %all-to-all-done.2.arrived = bf16[64,8,256]{2,1,0:T(8,128)(2,1)S(1)} async-done(((bf16[64,8,256]{2,1,0:T(8,128)(2,1)}), bf16[64,8,256]{2,1,0:T(8,128)(2,1)S(1)}, u32[]{:S(2)}, u32[]{:S(2)}) %all-to-all-start.2) | async-done | bytes 262176 | tf_op jit(solution)/shard_map/collect/all_to_all | solution.py:1031
  78.2 0.0 copy-done.1
  78.2 0.0 copy-start
  78.2 1.0 %copy-done = f32[3,128,256]{2,1,0:T(8,128)S(1)} copy-done((f32[3,128,256]{2,1,0:T(8,128)S(1)}, f32[3,128,256]{2,1,0:T(8,128)}, u32[]{:S(2)}) %copy-start) | copy-done | bytes 393240
  79.2 0.0 copy-start.3
  79.2 0.9 %copy-done.3 = f32[3,128,128]{2,1,0:T(8,128)S(1)} copy-done((f32[3,128,128]{2,1,0:T(8,128)S(1)}, f32[3,128,128]{2,1,0:T(8,128)}, u32[]{:S(2)}) %copy-start.3) | copy-done | bytes 196632
  80.1 3.2 %unpack.1 = (bf16[128,256]{1,0:T(8,128)(2,1)}, bf16[128,256]{1,0:T(8,128)(2,1)}, bf16[128,256]{1,0:T(8,128)(2,1)}, bf16[128,256]{1,0:T(8,128)(2,1)}, f32[64,128]{1,0:T(8,128)}, /*index=5*/f32[33,64]{1,0:T(8,128)}) custom-call(bf16[64,8,256]{2,1,0:T(8,128)(2,1)S(1)} %all-to-all-done.2.arrived, f32[3,128,256]{2,1,0:T(8,128)S(1)} %copy-done, ...), custom_call_target="tpu_custom_call" | custom-call | flops 1048576 | bytes 1048576 | tf_op jit(solution)/shard_map/unpack/pallas_call | solution.py:862
Async XLA Ops:
  2.6 31.5 %all-to-all-start = ((bf16[64,8,256]{2,1,0:T(8,128)(2,1)}), bf16[64,8,256]{2,1,0:T(8,128)(2,1)S(1)}, u32[]{:S(2)}, u32[]{:S(2)}) async-start(bf16[64,8,256]{2,1,0:T(8,128)(2,1)} %pack.1), calls=%async_computation | async-start | bytes 524288 | tf_op jit(solution)/shard_map/spread/all_to_all | solution.py:1031
  34.1 0.7 copy-start.4
  41.0 13.9 %all-to-all-start.1 = ((f32[32,8,128]{2,1,0:T(8,128)}), f32[32,8,128]{2,1,0:T(8,128)S(1)}, u32[]{:S(2)}, u32[]{:S(2)}) async-start(f32[32,8,128]{2,1,0:T(8,128)} %get-tuple-element.31), calls=%async_computation.1 | async-start | bytes 262144 | tf_op jit(solution)/shard_map/basis/all_to_all | solution.py:1031
  53.8 24.4 %copy-start.1 = (bf16[128,256]{1,0:T(8,128)(2,1)S(1)}, bf16[128,256]{1,0:T(8,128)(2,1)}, u32[]{:S(2)}) copy-start(bf16[128,256]{1,0:T(8,128)(2,1)} %grad_src.1) | copy-start | bytes 196612
  54.9 1.0 %copy-start.2 = (bf16[64,8,256]{2,1,0:T(8,128)(2,1)S(1)}, bf16[64,8,256]{2,1,0:T(8,128)(2,1)}, u32[]{:S(2)}) copy-start(bf16[64,8,256]{2,1,0:T(8,128)(2,1)} %output.1.packed) | copy-start | bytes 786436
  56.7 21.5 %all-to-all-start.2 = ((bf16[64,8,256]{2,1,0:T(8,128)(2,1)}), bf16[64,8,256]{2,1,0:T(8,128)(2,1)S(1)}, u32[]{:S(2)}, u32[]{:S(2)}) async-start(bf16[64,8,256]{2,1,0:T(8,128)(2,1)} %compose.1), calls=%async_computation.2 | async-start | bytes 524288 | tf_op jit(solution)/shard_map/collect/all_to_all | solution.py:1031
  78.2 1.0 %copy-start = (f32[3,128,256]{2,1,0:T(8,128)S(1)}, f32[3,128,256]{2,1,0:T(8,128)}, u32[]{:S(2)}) copy-start(f32[3,128,256]{2,1,0:T(8,128)} %get-tuple-element.32.feat_src) | copy-start | bytes 1179652
  79.2 0.9 %copy-start.3 = (f32[3,128,128]{2,1,0:T(8,128)S(1)}, f32[3,128,128]{2,1,0:T(8,128)}, u32[]{:S(2)}) copy-start(f32[3,128,128]{2,1,0:T(8,128)} %get-tuple-element.33.taps_src) | copy-start | bytes 589828

commit v5 on v4

--- a/solution.py
+++ b/solution.py
@@ -24,13 +24,7 @@
 GROUP = 40
 TURN = 1.0 / (2.0 * math.pi)
 
-SIN_COEF = (
-    4.442883014678955,
-    -7.308245658874512,
-    3.606354236602783,
-    -0.8461116552352905,
-    0.1098245158791542,
-)
+SIN_COEF = (4.442879676818848, -7.307816505432129, 3.5977742671966553, -0.7911993861198425)
 COS_COEF = (
     1.4142135381698608,
     -6.978850841522217,
@@ -269,6 +263,7 @@
     layer,
     left,
     phase,
+    phase_odd,
     filt,
     act,
     cosv,
@@ -326,9 +321,12 @@
 
     lax.fori_loop(0, ROWS, make_left, 0, unroll=4)
 
-    def chunk(index, carry):
+    def fetch(index, phase):
         base = pl.multiple_of(index * 512, 512)
         phase[...] = dot(left[pl.ds(base, 512), :], right[...])
+
+    def finish(index, phase):
+        base = pl.multiple_of(index * 512, 512)
         for half in range(2):
             lanes = slice(half * 128, half * 128 + 128)
             sums = [jnp.zeros((8, 128), F32)] * CHAN
@@ -356,6 +354,12 @@
                 filt[pl.ds(start, 8), lanes] = sums[chan]
         send(index, 0).start()
         send(index, 1).start()
+
+    def pair(index, carry):
+        fetch(2 * index + 1, phase_odd)
+        finish(2 * index, phase)
+        fetch(jnp.minimum(2 * index + 2, 7), phase)
+        finish(2 * index + 1, phase_odd)
         return carry
 
     def send(index, which):
@@ -363,7 +367,8 @@
         source, target = ((act, act_out), (cosv, cos_out))[which]
         return pltpu.make_async_copy(source.at[rows], target.at[rows], out_sems.at[which, index])
 
-    lax.fori_loop(0, 8, chunk, 0)
+    fetch(0, phase)
+    lax.fori_loop(0, 4, pair, 0)
     ratio = decay[...] * (1.0 / TOTAL)
     energy = expm1_small(-2.0 * decay[...]) / expm1_small(-2.0 * ratio)
     norm = 1.0 / jnp.sqrt(energy)
@@ -566,7 +571,6 @@
     filter_spec_src,
     raw_src,
     act_src,
-    arrived_src,
     skip_src,
     last_src,
     twiddle_src,
@@ -577,12 +581,10 @@
     filter_spec,
     raw,
     act,
-    arrived,
     skip,
     last,
     twiddle,
     full,
-    input_tail,
     rows_out,
     sems,
 ):
@@ -599,7 +601,6 @@
             (last_src, last),
             (skip_src, skip),
             (feat_src, feat),
-            (arrived_src, arrived),
         ],
     )
     lane128 = lax.broadcasted_iota(jnp.int32, (FEAT, 128), 1)
@@ -671,7 +672,6 @@
     sums = restore(crossed, 2 * CHAN, last[...], *tables)
     for copy in copies[7:]:
         copy.wait()
-    input_tail[...] = arrived[:, :, 128:256].astype(F32).reshape(ROWS * 8, 128)
 
     def plane(index):
         return take(feat, index, ROWS, 8)
@@ -693,18 +693,20 @@
             carried_grad[:, 0:128] * value[:, 0:128],
             carried_grad[:, 0:128] * key[:, 0:128],
         )
-        for index in range(3):
-            head = heads[index].astype(BF16).astype(F32)
+        wanted = [head.astype(BF16).astype(F32) for head in heads]
+        for signal in (query, key, value):
+            wanted.append(signal[:, 0:128].astype(BF16).astype(F32))
+        for signal in (query, key, value):
+            wanted.append(signal[:, 0:128] - signal[:, 0:128].astype(BF16).astype(F32))
+        for index, head in enumerate(wanted):
             place = HALO * index
             head = pltpu.roll(head, place, 1) if place else head
-            follow = jnp.where((lane128 >= place) & (lane128 < place + HALO), head, follow)
-            tail = input_tail[pl.ds(2 * index + chan, ROWS, stride=8), :]
-            place = HALO * (3 + index)
-            tail = pltpu.roll(tail, HALO + place, 1)
-            before = jnp.where((lane128 >= place) & (lane128 < place + HALO), tail, before)
-        halo = jnp.concatenate([follow[1:], blank], axis=0) + jnp.concatenate(
-            [blank, before[:-1]], axis=0
-        )
+            inside = (lane128 >= place) & (lane128 < place + HALO)
+            if index < 3:
+                follow = jnp.where(inside, head, follow)
+            else:
+                before = jnp.where(inside, head, before)
+        halo = jnp.concatenate([follow[1:], blank], axis=0) + before
         rows_out[chan, pl.ds(4, ROWS, stride=8), :] = halo
     row = lax.broadcasted_iota(jnp.int32, (ROWS, 8, 128), 1)
     for half, proj_part in enumerate((proj_hi, proj_wide - proj_hi)):
@@ -738,16 +740,17 @@
     for copy in copies:
         copy.wait()
     for index, ref in enumerate((query, key, value)):
-        taps_out[index] = jnp.concatenate(
-            [short[index], jnp.zeros((128 - TAPS, 128), F32)], axis=0
-        ).T
-        weights = taps_out[index]
+        weights = jnp.concatenate([short[index], jnp.zeros((128 - TAPS, 128), F32)], axis=0).T
+        for offset in range(TAPS):
+            taps_out[index * TAPS + offset] = jnp.broadcast_to(
+                weights[:, offset : offset + 1], (128, 128)
+            )
         block = ref[...].astype(F32)
         left, right = block[:, 0:128], block[:, 128:256]
-        out_left = weights[:, 0:1] * left
-        out_right = weights[:, 0:1] * right
+        out_left = taps_out[index * TAPS] * left
+        out_right = taps_out[index * TAPS] * right
         for offset in range(1, TAPS):
-            weight = weights[:, offset : offset + 1]
+            weight = taps_out[index * TAPS + offset]
             moved_left = pltpu.roll(left, offset, 1)
             moved_right = pltpu.roll(right, offset, 1)
             out_left = out_left + weight * jnp.where(lane < offset, 0.0, moved_left)
@@ -758,23 +761,18 @@
 
 def unpack_kernel(
     arrived,
-    feat_src,
-    taps_src,
-    grad_src,
+    feat,
+    taps,
+    grad,
     mixed,
     grad_query,
     grad_key,
     grad_value,
     proj,
     basis,
-    feat,
-    taps,
-    grad,
     wide,
     sorted_rows,
-    sems,
 ):
-    copies = begin(sems, [(feat_src, feat), (taps_src, taps), (grad_src, grad)])
     fill(wide, arrived[...].astype(F32))
 
     def both(half, row):
@@ -786,14 +784,11 @@
     carried_grad = [both(half, 2) for half in range(2)]
     halo = jnp.concatenate([wide[half, pl.ds(4, ROWS, stride=8), :] for half in range(2)], axis=0)
     lane = lax.broadcasted_iota(jnp.int32, (128, 128), 1)
-    for copy in copies:
-        copy.wait()
     feats = []
     for index in range(3):
-        left = feat[index, :, 0:128]
-        for offset in range(1, TAPS):
-            moved = pltpu.roll(halo, (offset - HALO * (4 + index)) % 128, 1)
-            left = left + taps[index, :, offset : offset + 1] * jnp.where(lane < offset, moved, 0.0)
+        high = pltpu.roll(halo, 128 - HALO * (3 + index), 1)
+        low = pltpu.roll(halo, 128 - HALO * (6 + index), 1)
+        left = jnp.where(lane < HALO, high + low, feat[index, :, 0:128])
         feats.append((left, feat[index, :, 128:256]))
     cotangent = grad[...].astype(F32)
     cotangent = (cotangent[:, 0:128], cotangent[:, 128:256])
@@ -806,10 +801,10 @@
     )
     for index, ref in enumerate((grad_query, grad_key, grad_value)):
         left, right = [part.astype(BF16).astype(F32) for part in grads[index]]
-        out_left = taps[index, :, 0:1] * left
-        out_right = taps[index, :, 0:1] * right
+        out_left = taps[index * TAPS] * left
+        out_right = taps[index * TAPS] * right
         for offset in range(1, TAPS):
-            weight = taps[index, :, offset : offset + 1]
+            weight = taps[index * TAPS + offset]
             moved_left = pltpu.roll(left, 128 - offset, 1)
             moved_right = pltpu.roll(right, 128 - offset, 1)
             moved_halo = pltpu.roll(halo, (128 - offset - HALO * index) % 128, 1)
@@ -910,6 +905,7 @@
             pltpu.VMEM((128, 128), F32),
             pltpu.VMEM((ROWS * FEAT, COLS), BF16),
             pltpu.VMEM((512, COLS), F32),
+            pltpu.VMEM((512, COLS), F32),
             pltpu.VMEM((CHAN * ROWS, COLS), F32),
             pltpu.VMEM((ROWS * FEAT, COLS), BF16),
             pltpu.VMEM((ROWS * FEAT, COLS), BF16),
@@ -946,16 +942,16 @@
     )
 
 
-def run_output(own, skip, feat, spec, filter_spec, raw, act, arrived, consts):
+def run_output(own, skip, feat, spec, filter_spec, raw, act, consts):
     names = ("last", "twiddle", "full")
     return call(
         output_kernel,
         "output",
         [own],
         [],
-        [feat, spec, filter_spec, raw, act, arrived, skip] + [consts[name] for name in names],
+        [feat, spec, filter_spec, raw, act, skip] + [consts[name] for name in names],
         [(shape((ROWS, 8, COLS), BF16), False)],
-        [pltpu.VMEM((ROWS * 8, 128), F32), pltpu.VMEM((2, ROWS * 8, 128), F32)],
+        [pltpu.VMEM((2, ROWS * 8, 128), F32)],
         1 << 31,
         1 << 22,
     )[0]
@@ -983,10 +979,11 @@
         [],
         [],
         [query_in, key_in, value_in, short],
-        [(shape((3, 128, COLS)), False), (shape((3, 128, 128)), False)],
+        [(shape((3, 128, COLS)), False), (shape((3 * TAPS, 128, 128)), False)],
         [],
         1 << 28,
         1 << 20,
+        ROOMY,
     )
 
 
@@ -996,8 +993,8 @@
         unpack_kernel,
         "unpack",
         [],
-        [arrived],
-        [feat, taps, grad_out],
+        [arrived, feat, taps, grad_out],
+        [],
         [(value, False) for value in [block] * 4 + [shape((FEAT, 128)), shape((EMB, FEAT))]],
         [pltpu.VMEM((2, ROWS * 8, 128), F32), pltpu.VMEM((64, 128), F32)],
         1 << 20,
@@ -1063,7 +1060,7 @@
     with jax.named_scope("basis"):
         basis_parts = exchange(basis_own, NEAR)
     packed = run_output(
-        own, skip_gain.reshape(1, 128), feat, spec, filter_spec, raw, act, arrived, consts
+        own, skip_gain.reshape(1, 128), feat, spec, filter_spec, raw, act, consts
     )
     composed = run_compose(packed, basis_parts)
     with jax.named_scope("collect"):

time: 83.8 us -> 78.9 us (0.942)
  Pallas kernels: 30.4 us -> 26.3 us
  waiting for transfers between devices: 16.2 us -> 18.6 us
  local copies, waits for them, and re-layouts: 3.59 us -> 1.7 us
  starting transfers between devices: 32.4 us -> 31.1 us
    pallas_call x7, Pallas kernels: 30.4 us -> 26.3 us  [call(): pl.pallas_call(kernel, name=name, in_specs=[SMEM] * len(own) + [VMEM] * l...]
    all_to_all x3, waiting for transfers between devices: 16.2 us -> 18.6 us  [exchange(): return lax.all_to_all(value, axes, split_axis=0, concat_axis=0, tiled=True)]
    unnamed x10 -> x14, local copies, waits for them, and re-layouts: 3.59 us -> 1.7 us
    all_to_all x3, starting transfers between devices: 32.4 us -> 31.1 us  [exchange(): return lax.all_to_all(value, axes, split_axis=0, concat_axis=0, tiled=True)]
  transfers between devices with their start and end apart: 3 -> 3, of which waited for: 3 -> 3; matrix products, arithmetic and copies ran while one was open for 0% -> 0% of each run, Pallas kernels for 22% -> 20%
where the time goes in v5:
time: 78.9 us; the launch traced here: 78.5 us
  starting transfers between devices  31.1 us (39%)
  Pallas kernels  26.3 us (33%)
  waiting for transfers between devices  18.6 us (24%)
  local copies, waits for them, and re-layouts  1.7 us (2%)
    all_to_all x3, starting transfers between devices, exchange(): return lax.all_to_all(value, axes, split_axis=0, concat_axis=0, tiled=True)  31.1 us
    pallas_call x7, Pallas kernels, call(): pl.pallas_call(kernel, name=name, in_specs=[SMEM] * len(own) + [VMEM] * l...  26.3 us
    all_to_all x3, waiting for transfers between devices, exchange(): return lax.all_to_all(value, axes, split_axis=0, concat_axis=0, tiled=True)  18.6 us
    unnamed x14, local copies, waits for them, and re-layouts  1.7 us
  transfers between devices with their start and end apart: 3, of which 3 were waited for; matrix products, arithmetic and copies ran while one was open for 0% of the time, Pallas kernels for 20%

profile of v5, /device:TPU:1, one launch (start us, length us, event | category | flops | bytes accessed | tf_op | source)
XLA Modules:
  0.0 78.5 jit_solution(2193760158321253942)
XLA Ops:
  0.6 2.0 %pack.1 = bf16[64,8,256]{2,1,0:T(8,128)(2,1)} custom-call(bf16[128,256]{1,0:T(8,128)(2,1)} %query_src.1, bf16[128,256]{1,0:T(8,128)(2,1)} %key_src.1, bf16[128,256]{1,0:T(8,128)(2,1)} %value_src.1, bf16[128,256]{1,0:T(8,128)(2,1)} %grad.3), custom_call_target="tpu_custom_call" | custom-call | flops 1048576 | bytes 524288 | tf_op jit(solution)/shard_map/spread/pack/pallas_call | solution.py:857
  2.6 17.6 %all-to-all-start = ((bf16[64,8,256]{2,1,0:T(8,128)(2,1)}), bf16[64,8,256]{2,1,0:T(8,128)(2,1)S(1)}, u32[]{:S(2)}, u32[]{:S(2)}) async-start(bf16[64,8,256]{2,1,0:T(8,128)(2,1)} %pack.1), calls=%async_computation | async-start | bytes 524288 | tf_op jit(solution)/shard_map/spread/all_to_all | solution.py:1028
  20.3 8.7 %filter.1 = (bf16[4096,256]{1,0:T(8,128)(2,1)}, bf16[4096,256]{1,0:T(8,128)(2,1)}, f32[128,256]{1,0:T(8,128)}, f32[128,512]{1,0:T(8,128)}, f32[128,128]{1,0:T(8,128)}) custom-call(s32[1]{0:T(128)} %bitcast.own, f32[33,64]{1,0:T(8,128)} %bitcast.13, f32[1,64]{1,0:T(1,128)} %bitcast.15, f32[64,128]{1,0:T(8,128)} %bitcast.11, f32[1,128]{1,0:T(1,128)} %bitcast.16, ...), custom_call_target="tpu_custom_call" | custom-call | flops 8589934592 | bytes 8388608 | tf_op jit(solution)/shard_map/filter/pallas_call | solution.py:857
  28.9 5.2 %all-to-all-done.arrived_src = bf16[64,8,256]{2,1,0:T(8,128)(2,1)S(1)} async-done(((bf16[64,8,256]{2,1,0:T(8,128)(2,1)}), bf16[64,8,256]{2,1,0:T(8,128)(2,1)S(1)}, u32[]{:S(2)}, u32[]{:S(2)}) %all-to-all-start) | async-done | bytes 262176 | tf_op jit(solution)/shard_map/spread/all_to_all | solution.py:1028
  34.1 0.0 copy-start.6
  34.1 0.7 copy-done.6
  34.8 6.1 %gradient.1 = (f32[2,512,128]{2,1,0:T(8,128)}, f32[256,512]{1,0:T(8,128)}, f32[2,128,128]{2,1,0:T(8,128)}, f32[32,8,128]{2,1,0:T(8,128)}) custom-call(s32[1]{0:T(128)} %bitcast.own, bf16[64,8,256]{2,1,0:T(8,128)(2,1)} %copy-done.6, f32[128,256]{1,0:T(8,128)} %get-tuple-element.23.envelope_src, f32[128,128]{1,0:T(8,128)} %get-tuple-element.24.columns_src, ...), custom_call_target="tpu_custom_call" | custom-call | flops 4294967296 | bytes 8388608 | tf_op jit(solution)/shard_map/gradient/pallas_call | solution.py:857
  41.0 7.1 %all-to-all-start.1 = ((f32[32,8,128]{2,1,0:T(8,128)}), f32[32,8,128]{2,1,0:T(8,128)S(1)}, u32[]{:S(2)}, u32[]{:S(2)}) async-start(f32[32,8,128]{2,1,0:T(8,128)} %get-tuple-element.31), calls=%async_computation.1 | async-start | bytes 262144 | tf_op jit(solution)/shard_map/basis/all_to_all | solution.py:1028
  48.1 0.0 copy-start.2
  48.1 0.0 copy-start.3
  48.1 0.0 copy-start.4
  48.1 0.0 copy-start.5
  48.1 5.8 %output.1.packed = bf16[64,8,256]{2,1,0:T(8,128)(2,1)} custom-call(s32[1]{0:T(128)} %bitcast.own, f32[2,512,128]{2,1,0:T(8,128)} %get-tuple-element.26.feat_src, f32[256,512]{1,0:T(8,128)} %get-tuple-element.27.spec_src, f32[128,512]{1,0:T(8,128)} %get-tuple-element.28.filter_spec_src, f32[2,128,128]{2,1,0:T(8,128)} %get-tuple-element.29.raw_src, ...), custom_call_target="tpu_custom_call" | custom-call | flops 2147483648 | bytes 4194304 | tf_op jit(solution)/shard_map/output/pallas_call | solution.py:857
  53.9 0.9 %all-to-all-done.1.basis_parts = f32[32,8,128]{2,1,0:T(8,128)S(1)} async-done(((f32[32,8,128]{2,1,0:T(8,128)}), f32[32,8,128]{2,1,0:T(8,128)S(1)}, u32[]{:S(2)}, u32[]{:S(2)}) %all-to-all-start.1) | async-done | bytes 131104 | tf_op jit(solution)/shard_map/basis/all_to_all | solution.py:1028
  54.9 0.0 copy-start
  54.9 0.9 %copy-done = bf16[64,8,256]{2,1,0:T(8,128)(2,1)S(1)} copy-done((bf16[64,8,256]{2,1,0:T(8,128)(2,1)S(1)}, bf16[64,8,256]{2,1,0:T(8,128)(2,1)}, u32[]{:S(2)}) %copy-start) | copy-done | bytes 262168
  55.8 0.0 copy-start.1
  55.8 0.8 %compose.1 = bf16[64,8,256]{2,1,0:T(8,128)(2,1)} custom-call(bf16[64,8,256]{2,1,0:T(8,128)(2,1)S(1)} %copy-done, f32[32,8,128]{2,1,0:T(8,128)S(1)} %all-to-all-done.1.basis_parts), custom_call_target="tpu_custom_call" | custom-call | flops 1048576 | bytes 1048576 | tf_op jit(solution)/shard_map/compose/pallas_call | solution.py:857
  56.7 6.4 %all-to-all-start.2 = ((bf16[64,8,256]{2,1,0:T(8,128)(2,1)}), bf16[64,8,256]{2,1,0:T(8,128)(2,1)S(1)}, u32[]{:S(2)}, u32[]{:S(2)}) async-start(bf16[64,8,256]{2,1,0:T(8,128)(2,1)} %compose.1), calls=%async_computation.2 | async-start | bytes 524288 | tf_op jit(solution)/shard_map/collect/all_to_all | solution.py:1028
  63.1 0.0 copy-done.2
  63.1 0.0 copy-done.3
  63.1 0.0 copy-done.4
  63.1 0.0 copy-done.5
  63.1 1.3 %local.1 = (f32[3,128,256]{2,1,0:T(8,128)S(1)}, f32[21,128,128]{2,1,0:T(8,128)S(1)}) custom-call(bf16[128,256]{1,0:T(8,128)(2,1)S(1)} %copy-done.2, bf16[128,256]{1,0:T(8,128)(2,1)S(1)} %copy-done.3, bf16[128,256]{1,0:T(8,128)(2,1)S(1)} %copy-done.4, f32[3,7,128]{2,1,0:T(8,128)S(1)} %bitcast.10), custom_call_target="tpu_custom_call" | custom-call | flops 268435456 | bytes 1048576 | tf_op jit(solution)/shard_map/local/pallas_call | solution.py:857
  64.4 12.5 %all-to-all-done.2.arrived = bf16[64,8,256]{2,1,0:T(8,128)(2,1)S(1)} async-done(((bf16[64,8,256]{2,1,0:T(8,128)(2,1)}), bf16[64,8,256]{2,1,0:T(8,128)(2,1)S(1)}, u32[]{:S(2)}, u32[]{:S(2)}) %all-to-all-start.2) | async-done | bytes 262176 | tf_op jit(solution)/shard_map/collect/all_to_all | solution.py:1028
  76.9 0.0 copy-done.1
  76.9 1.6 %unpack.1 = (bf16[128,256]{1,0:T(8,128)(2,1)}, bf16[128,256]{1,0:T(8,128)(2,1)}, bf16[128,256]{1,0:T(8,128)(2,1)}, bf16[128,256]{1,0:T(8,128)(2,1)}, f32[64,128]{1,0:T(8,128)}, /*index=5*/f32[33,64]{1,0:T(8,128)}) custom-call(bf16[64,8,256]{2,1,0:T(8,128)(2,1)S(1)} %all-to-all-done.2.arrived, f32[3,128,256]{2,1,0:T(8,128)S(1)} %get-tuple-element.32.feat, ...), custom_call_target="tpu_custom_call" | custom-call | flops 1048576 | bytes 1048576 | tf_op jit(solution)/shard_map/unpack/pallas_call | solution.py:857
Async XLA Ops:
  2.6 31.5 %all-to-all-start = ((bf16[64,8,256]{2,1,0:T(8,128)(2,1)}), bf16[64,8,256]{2,1,0:T(8,128)(2,1)S(1)}, u32[]{:S(2)}, u32[]{:S(2)}) async-start(bf16[64,8,256]{2,1,0:T(8,128)(2,1)} %pack.1), calls=%async_computation | async-start | bytes 524288 | tf_op jit(solution)/shard_map/spread/all_to_all | solution.py:1028
  34.1 0.7 copy-start.6
  41.0 13.9 %all-to-all-start.1 = ((f32[32,8,128]{2,1,0:T(8,128)}), f32[32,8,128]{2,1,0:T(8,128)S(1)}, u32[]{:S(2)}, u32[]{:S(2)}) async-start(f32[32,8,128]{2,1,0:T(8,128)} %get-tuple-element.31), calls=%async_computation.1 | async-start | bytes 262144 | tf_op jit(solution)/shard_map/basis/all_to_all | solution.py:1028
  48.1 15.0 %copy-start.2 = (bf16[128,256]{1,0:T(8,128)(2,1)S(1)}, bf16[128,256]{1,0:T(8,128)(2,1)}, u32[]{:S(2)}) copy-start(bf16[128,256]{1,0:T(8,128)(2,1)} %query_src.1) | copy-start | bytes 196612
  48.1 15.0 %copy-start.3 = (bf16[128,256]{1,0:T(8,128)(2,1)S(1)}, bf16[128,256]{1,0:T(8,128)(2,1)}, u32[]{:S(2)}) copy-start(bf16[128,256]{1,0:T(8,128)(2,1)} %key_src.1) | copy-start | bytes 196612
  48.1 15.0 %copy-start.4 = (bf16[128,256]{1,0:T(8,128)(2,1)S(1)}, bf16[128,256]{1,0:T(8,128)(2,1)}, u32[]{:S(2)}) copy-start(bf16[128,256]{1,0:T(8,128)(2,1)} %value_src.1) | copy-start | bytes 196612
  48.1 15.0 %copy-start.5 = (f32[3,128,7]{1,2,0:T(8,128)S(1)}, f32[3,128,7]{1,2,0:T(8,128)}, u32[]{:S(2)}) copy-start(f32[3,128,7]{1,2,0:T(8,128)} %param.23) | copy-start | bytes 32260
  54.9 1.0 %copy-start = (bf16[64,8,256]{2,1,0:T(8,128)(2,1)S(1)}, bf16[64,8,256]{2,1,0:T(8,128)(2,1)}, u32[]{:S(2)}) copy-start(bf16[64,8,256]{2,1,0:T(8,128)(2,1)} %output.1.packed) | copy-start | bytes 786436
  55.8 21.1 %copy-start.1 = (bf16[128,256]{1,0:T(8,128)(2,1)S(1)}, bf16[128,256]{1,0:T(8,128)(2,1)}, u32[]{:S(2)}) copy-start(bf16[128,256]{1,0:T(8,128)(2,1)} %grad.3) | copy-start | bytes 196612
  56.7 20.3 %all-to-all-start.2 = ((bf16[64,8,256]{2,1,0:T(8,128)(2,1)}), bf16[64,8,256]{2,1,0:T(8,128)(2,1)S(1)}, u32[]{:S(2)}, u32[]{:S(2)}) async-start(bf16[64,8,256]{2,1,0:T(8,128)(2,1)} %compose.1), calls=%async_computation.2 | async-start | bytes 524288 | tf_op jit(solution)/shard_map/collect/all_to_all | solution.py:1028

commit v6 on v5

--- a/solution.py
+++ b/solution.py
@@ -193,6 +193,19 @@
 def put(ref, start, count, stride, value):
     for half in range(2):
         ref[half, pl.ds(start, count, stride=stride), :] = value[:, half * 128 : half * 128 + 128]
+
+
+AT_FEAT = 0
+AT_SPEC = 2 * ROWS * 8
+AT_RAW = AT_SPEC + 4 * 2 * CHAN * ROWS
+AT_FILTER = AT_RAW + 2 * CHAN * ROWS
+HANDED = AT_FILTER + 4 * CHAN * ROWS
+
+
+def tiles(ref, start, stride, count, picked_tiles):
+    return jnp.concatenate(
+        [ref[start + tile * stride : start + tile * stride + count, :] for tile in picked_tiles], axis=1
+    )
 
 
 def fill(ref, value):
@@ -410,6 +423,7 @@
     envelope_src,
     columns_src,
     cosine_src,
+    filter_spec_src,
     short_src,
     back_src,
     back_turn_src,
@@ -418,14 +432,13 @@
     last_src,
     twiddle_src,
     full_src,
-    feat_out,
-    spec_out,
-    raw_out,
+    handed_out,
     basis_out,
     arrived,
     envelope,
     columns,
     cosine,
+    filter_spec,
     short,
     back,
     back_turn,
@@ -436,8 +449,7 @@
     full,
     taps,
     raw,
-    feat,
-    spec,
+    handed,
     out_sems,
     sems,
 ):
@@ -454,6 +466,7 @@
             (envelope_src, envelope),
             (cosine_src, cosine),
             (columns_src, columns),
+            (filter_spec_src, filter_spec),
             (back_src, back),
             (back_turn_src, back_turn),
             (place_src, place),
@@ -463,19 +476,32 @@
     weights = own_taps(first, short, taps, ((0, 0), (2, 1), (4, 2)))
     copies[1].wait()
     signal = arrived[...].astype(F32)
-    lane = lax.broadcasted_iota(jnp.int32, (ROWS, 8, COLS), 2)
-    result = weights[None, :, 0:1] * signal
-    zeros = jnp.zeros((1, 8, COLS), F32)
+    lane = lax.broadcasted_iota(jnp.int32, (ROWS, 8, 128), 2)
+    zeros = jnp.zeros((1, 8, 128), F32)
+    left, right = signal[:, :, 0:128], signal[:, :, 128:256]
+    sum_left = weights[None, :, 0:1] * left
+    sum_right = weights[None, :, 0:1] * right
     for offset in range(1, TAPS):
-        moved = pltpu.roll(signal, offset, 2)
-        before = jnp.concatenate([zeros, moved[:-1]], axis=0)
-        shifted = jnp.where(lane < offset, before, moved)
-        result = result + weights[None, :, offset : offset + 1] * shifted
-    fill(feat, result)
-    leaving = begin(out_sems.at[pl.ds(0, 1)], [(feat, feat_out)])
+        weight = weights[None, :, offset : offset + 1]
+        moved_left = pltpu.roll(left, offset, 2)
+        moved_right = pltpu.roll(right, offset, 2)
+        before = jnp.concatenate([zeros, moved_right[:-1]], axis=0)
+        sum_left = sum_left + weight * jnp.where(lane < offset, before, moved_left)
+        sum_right = sum_right + weight * jnp.where(lane < offset, moved_left, moved_right)
+    for half, result in enumerate((sum_left, sum_right)):
+        handed[AT_FEAT + half * 512 : AT_FEAT + half * 512 + 512, :] = result.reshape(512, 128)
+
+    def leave(part, start, size):
+        rows = pl.ds(start, size)
+        return begin(out_sems.at[pl.ds(part, 1)], [(handed.at[rows], handed_out.at[rows])])
+
+    leaving = leave(0, AT_FEAT, AT_SPEC - AT_FEAT)
 
     def plane(index):
-        return take(feat, index, ROWS, 8)
+        return jnp.concatenate(
+            [handed[pl.ds(AT_FEAT + half * 512 + index, ROWS, stride=8), :] for half in range(2)],
+            axis=1,
+        )
 
     signals = []
     for chan in range(CHAN):
@@ -486,8 +512,11 @@
         copy.wait()
     tables = (twiddle[0], twiddle[1], full[0], full[1])
     spec_all = spectrum(signals, forward[...], *tables)
-    spec[...] = spec_all
-    leaving += begin(out_sems.at[pl.ds(1, 1)], [(spec, spec_out)])
+    for tile in range(4):
+        handed[AT_SPEC + tile * 256 : AT_SPEC + tile * 256 + 256, :] = spec_all[
+            :, tile * 128 : tile * 128 + 128
+        ]
+    leaving += leave(1, AT_SPEC, AT_RAW - AT_SPEC)
     carried, grad = spec_all[: CHAN * ROWS], spec_all[CHAN * ROWS :]
     carried_re, carried_im = carried[:, :COLS], carried[:, COLS:]
     grad_re, grad_im = grad[:, :COLS], grad[:, COLS:]
@@ -506,9 +535,15 @@
         scaled = rounded * envelope[chan * ROWS : (chan + 1) * ROWS, :]
         for half in range(2):
             raw[half, chan * ROWS : (chan + 1) * ROWS, :] = scaled[:, half * 128 : half * 128 + 128]
-    leaving += begin(out_sems.at[pl.ds(2, 1)], [(raw, raw_out)])
     for copy in copies[7:]:
         copy.wait()
+    for half in range(2):
+        handed[AT_RAW + half * 128 : AT_RAW + half * 128 + 128, :] = raw[half]
+    for tile in range(4):
+        handed[AT_FILTER + tile * 128 : AT_FILTER + tile * 128 + 128, :] = filter_spec[
+            :, tile * 128 : tile * 128 + 128
+        ]
+    leaving += leave(2, AT_RAW, HANDED - AT_RAW)
     column0 = columns[0:FEAT, :]
     column1 = columns[FEAT : 2 * FEAT, :]
     back_all = back[...]
@@ -566,20 +601,14 @@
 
 def output_kernel(
     own,
-    feat_src,
-    spec_src,
-    filter_spec_src,
-    raw_src,
+    handed_src,
     act_src,
     skip_src,
     last_src,
     twiddle_src,
     full_src,
     out,
-    feat,
-    spec,
-    filter_spec,
-    raw,
+    handed,
     act,
     skip,
     last,
@@ -592,64 +621,26 @@
     copies = begin(
         sems,
         [
-            (raw_src, raw),
-            (act_src, act),
-            (spec_src, spec),
-            (filter_spec_src, filter_spec),
+            (handed_src, handed),
             (full_src, full),
             (twiddle_src, twiddle),
             (last_src, last),
             (skip_src, skip),
-            (feat_src, feat),
+            (act_src, act),
         ],
     )
     lane128 = lax.broadcasted_iota(jnp.int32, (FEAT, 128), 1)
     row_lane = lane128 % 8
-    copies[0].wait()
-    copies[1].wait()
-
-    def chunk(index, proj_sum):
-        base = pl.multiple_of(index * 512, 512)
-        start = pl.multiple_of(index * 8, 8)
-        rows = [
-            jnp.concatenate(
-                [raw[half, pl.ds(chan * ROWS + start, 8), :] for half in range(2)], axis=1
-            )
-            for chan in range(CHAN)
-        ]
-        wide = jnp.concatenate(rows, axis=0)
-        hi = wide.astype(BF16).astype(F32)
-        packed = jnp.concatenate([hi, wide - hi, jnp.zeros((128 - 4 * 8, COLS), F32)], axis=0)
-        turned = jnp.concatenate(
-            [packed[:, half * 128 : half * 128 + 128].T for half in range(2)], axis=0
-        ).astype(BF16)
-        product = dot(act[pl.ds(base, 512), :], turned)
-        for inner in range(8):
-            near = inner * FEAT
-            proj_sum = proj_sum + jnp.where(row_lane == inner, product[near : near + FEAT, :], 0.0)
-        return proj_sum
-
-    proj_sum = lax.fori_loop(0, 8, chunk, jnp.zeros((FEAT, 128), F32), unroll=2)
-    own_lane = lane128 % 16
-    stacked = jnp.concatenate(
-        [jnp.where(own_lane < 8, proj_sum, 0.0), jnp.where(own_lane >= 8, proj_sum, 0.0)], axis=0
-    )
-    proj_wide = lax.dot_general(
-        jnp.ones((8, 128), F32),
-        stacked,
-        (((1,), (1,)), ((), ())),
-        precision=EXACT,
-        preferred_element_type=F32,
-    )
-    proj_hi = proj_wide.astype(BF16).astype(F32)
-    for copy in copies[2:7]:
+    for copy in copies[0:4]:
         copy.wait()
     tables = (twiddle[0], twiddle[1], full[0], full[1])
-    carried, grad = spec[0 : CHAN * ROWS, :], spec[CHAN * ROWS : 2 * CHAN * ROWS, :]
-    filt = filter_spec[...]
-    carried_re, carried_im = carried[:, :COLS], carried[:, COLS:]
-    grad_re, grad_im = grad[:, :COLS], grad[:, COLS:]
-    filt_re, filt_im = filt[:, :COLS], filt[:, COLS:]
+    own_rows = CHAN * ROWS
+    carried_re = tiles(handed, AT_SPEC, 256, own_rows, (0, 1))
+    carried_im = tiles(handed, AT_SPEC, 256, own_rows, (2, 3))
+    grad_re = tiles(handed, AT_SPEC + own_rows, 256, own_rows, (0, 1))
+    grad_im = tiles(handed, AT_SPEC + own_rows, 256, own_rows, (2, 3))
+    filt_re = tiles(handed, AT_FILTER, 128, own_rows, (0, 1))
+    filt_im = tiles(handed, AT_FILTER, 128, own_rows, (2, 3))
     crossed = jnp.concatenate(
         [
             jnp.concatenate(
@@ -670,11 +661,13 @@
         axis=0,
     )
     sums = restore(crossed, 2 * CHAN, last[...], *tables)
-    for copy in copies[7:]:
-        copy.wait()
+    copies[4].wait()
 
     def plane(index):
-        return take(feat, index, ROWS, 8)
+        return jnp.concatenate(
+            [handed[pl.ds(AT_FEAT + half * 512 + index, ROWS, stride=8), :] for half in range(2)],
+            axis=1,
+        )
 
     blank = jnp.zeros((1, 128), F32)
     for chan in range(CHAN):
@@ -708,6 +701,46 @@
                 before = jnp.where(inside, head, before)
         halo = jnp.concatenate([follow[1:], blank], axis=0) + before
         rows_out[chan, pl.ds(4, ROWS, stride=8), :] = halo
+    copies[5].wait()
+
+    def chunk(index, proj_sum):
+        base = pl.multiple_of(index * 512, 512)
+        start = pl.multiple_of(index * 8, 8)
+        rows = [
+            jnp.concatenate(
+                [
+                    handed[pl.ds(AT_RAW + half * 128 + chan * ROWS + start, 8), :]
+                    for half in range(2)
+                ],
+                axis=1,
+            )
+            for chan in range(CHAN)
+        ]
+        wide = jnp.concatenate(rows, axis=0)
+        hi = wide.astype(BF16).astype(F32)
+        packed = jnp.concatenate([hi, wide - hi, jnp.zeros((128 - 4 * 8, COLS), F32)], axis=0)
+        turned = jnp.concatenate(
+            [packed[:, half * 128 : half * 128 + 128].T for half in range(2)], axis=0
+        ).astype(BF16)
+        product = dot(act[pl.ds(base, 512), :], turned)
+        for inner in range(8):
+            near = inner * FEAT
+            proj_sum = proj_sum + jnp.where(row_lane == inner, product[near : near + FEAT, :], 0.0)
+        return proj_sum
+
+    proj_sum = lax.fori_loop(0, 8, chunk, jnp.zeros((FEAT, 128), F32), unroll=2)
+    own_lane = lane128 % 16
+    stacked = jnp.concatenate(
+        [jnp.where(own_lane < 8, proj_sum, 0.0), jnp.where(own_lane >= 8, proj_sum, 0.0)], axis=0
+    )
+    proj_wide = lax.dot_general(
+        jnp.ones((8, 128), F32),
+        stacked,
+        (((1,), (1,)), ((), ())),
+        precision=EXACT,
+        preferred_element_type=F32,
+    )
+    proj_hi = proj_wide.astype(BF16).astype(F32)
     row = lax.broadcasted_iota(jnp.int32, (ROWS, 8, 128), 1)
     for half, proj_part in enumerate((proj_hi, proj_wide - proj_hi)):
         extra = jnp.where(row == 7, proj_part[None], 0.0)
@@ -916,25 +949,22 @@
     )
 
 
-def run_gradient(own, arrived, short, cosine, envelope, columns, consts):
+def run_gradient(own, arrived, short, cosine, envelope, columns, filter_spec, consts):
     names = ("back", "back_turn", "place", "forward", "last", "twiddle", "full")
     return call(
         gradient_kernel,
         "gradient",
         [own],
         [],
-        [arrived, envelope, columns, cosine, short] + [consts[name] for name in names],
+        [arrived, envelope, columns, cosine, filter_spec, short] + [consts[name] for name in names],
         [
-            (shape((2, ROWS * 8, 128)), True),
-            (shape((2 * CHAN * ROWS, 2 * COLS)), True),
-            (shape((2, CHAN * ROWS, 128)), True),
+            (shape((HANDED, 128)), True),
             (shape((32, 8, 128)), False),
         ],
         [
             pltpu.VMEM((128, 128), F32),
             pltpu.VMEM((2, CHAN * ROWS, 128), F32),
-            pltpu.VMEM((2, ROWS * 8, 128), F32),
-            pltpu.VMEM((2 * CHAN * ROWS, 2 * COLS), F32),
+            pltpu.VMEM((HANDED, 128), F32),
             pltpu.SemaphoreType.DMA((3,)),
         ],
         1 << 32,
@@ -942,18 +972,19 @@
     )
 
 
-def run_output(own, skip, feat, spec, filter_spec, raw, act, consts):
+def run_output(own, skip, handed, act, consts):
     names = ("last", "twiddle", "full")
     return call(
         output_kernel,
         "output",
         [own],
         [],
-        [feat, spec, filter_spec, raw, act, skip] + [consts[name] for name in names],
+        [handed, act, skip] + [consts[name] for name in names],
         [(shape((ROWS, 8, COLS), BF16), False)],
         [pltpu.VMEM((2, ROWS * 8, 128), F32)],
         1 << 31,
         1 << 22,
+        52 * 1024 * 1024,
     )[0]
 
 
@@ -1054,13 +1085,13 @@
         decay_rate.reshape(1, 128),
         consts,
     )
-    feat, spec, raw, basis_own = run_gradient(
-        own, arrived, short, cosine, envelope, columns, consts
+    handed, basis_own = run_gradient(
+        own, arrived, short, cosine, envelope, columns, filter_spec, consts
     )
     with jax.named_scope("basis"):
         basis_parts = exchange(basis_own, NEAR)
     packed = run_output(
-        own, skip_gain.reshape(1, 128), feat, spec, filter_spec, raw, act, consts
+        own, skip_gain.reshape(1, 128), handed, act, consts
     )
     composed = run_compose(packed, basis_parts)
     with jax.named_scope("collect"):

time: 78.9 us -> 77.9 us (0.987)
  Pallas kernels: 26.3 us -> 25 us
  waiting for transfers between devices: 18.6 us -> 19.9 us
  local copies, waits for them, and re-layouts: 1.7 us -> 0.74 us
    pallas_call x7, Pallas kernels: 26.3 us -> 25 us  [call(): pl.pallas_call(kernel, name=name, in_specs=[SMEM] * len(own) + [VMEM] * l...]
    all_to_all x3, waiting for transfers between devices: 18.6 us -> 19.9 us  [exchange(): return lax.all_to_all(value, axes, split_axis=0, concat_axis=0, tiled=True)]
    unnamed x14 -> x20, local copies, waits for them, and re-layouts: 1.7 us -> 0.74 us
  transfers between devices with their start and end apart: 3 -> 3, of which waited for: 3 -> 3; matrix products, arithmetic and copies ran while one was open for 0% -> 0% of each run, Pallas kernels for 20% -> 19%
where the time goes in v6:
time: 77.9 us; the launch traced here: 77.6 us
  starting transfers between devices  31.1 us (40%)
  Pallas kernels  25 us (32%)
  waiting for transfers between devices  19.9 us (26%)
  between operations  0.82 us (1%)
    all_to_all x3, starting transfers between devices, exchange(): return lax.all_to_all(value, axes, split_axis=0, concat_axis=0, tiled=True)  31.1 us
    pallas_call x7, Pallas kernels, call(): pl.pallas_call(kernel, name=name, in_specs=[SMEM] * len(own) + [VMEM] * l...  25 us
    all_to_all x3, waiting for transfers between devices, exchange(): return lax.all_to_all(value, axes, split_axis=0, concat_axis=0, tiled=True)  19.9 us
  transfers between devices with their start and end apart: 3, of which 3 were waited for; matrix products, arithmetic and copies ran while one was open for 0% of the time, Pallas kernels for 19%

profile of v6, /device:TPU:1, one launch (start us, length us, event | category | flops | bytes accessed | tf_op | source)
XLA Modules:
  0.0 77.6 jit_solution(3398217336932605275)
XLA Ops:
  0.6 2.0 %pack.1 = bf16[64,8,256]{2,1,0:T(8,128)(2,1)} custom-call(bf16[128,256]{1,0:T(8,128)(2,1)} %query_src.1, bf16[128,256]{1,0:T(8,128)(2,1)} %key_src.1, bf16[128,256]{1,0:T(8,128)(2,1)} %value_src.1, bf16[128,256]{1,0:T(8,128)(2,1)} %grad.3), custom_call_target="tpu_custom_call" | custom-call | flops 1048576 | bytes 524288 | tf_op jit(solution)/shard_map/spread/pack/pallas_call | solution.py:890
  2.6 17.6 %all-to-all-start = ((bf16[64,8,256]{2,1,0:T(8,128)(2,1)}), bf16[64,8,256]{2,1,0:T(8,128)(2,1)S(1)}, u32[]{:S(2)}, u32[]{:S(2)}) async-start(bf16[64,8,256]{2,1,0:T(8,128)(2,1)} %pack.1), calls=%async_computation | async-start | bytes 524288 | tf_op jit(solution)/shard_map/spread/all_to_all | solution.py:1059
  20.3 8.6 %filter.1 = (bf16[4096,256]{1,0:T(8,128)(2,1)}, bf16[4096,256]{1,0:T(8,128)(2,1)}, f32[128,256]{1,0:T(8,128)}, f32[128,512]{1,0:T(8,128)}, f32[128,128]{1,0:T(8,128)}) custom-call(s32[1]{0:T(128)} %bitcast.own, f32[33,64]{1,0:T(8,128)} %bitcast.14, f32[1,64]{1,0:T(1,128)} %bitcast.16, f32[64,128]{1,0:T(8,128)} %bitcast.12, f32[1,128]{1,0:T(1,128)} %bitcast.17, ...), custom_call_target="tpu_custom_call" | custom-call | flops 8589934592 | bytes 8388608 | tf_op jit(solution)/shard_map/filter/pallas_call | solution.py:890
  28.9 5.2 %all-to-all-done.arrived_src = bf16[64,8,256]{2,1,0:T(8,128)(2,1)S(1)} async-done(((bf16[64,8,256]{2,1,0:T(8,128)(2,1)}), bf16[64,8,256]{2,1,0:T(8,128)(2,1)S(1)}, u32[]{:S(2)}, u32[]{:S(2)}) %all-to-all-start) | async-done | bytes 262176 | tf_op jit(solution)/shard_map/spread/all_to_all | solution.py:1059
  34.1 0.0 copy-start.9
  34.1 0.7 copy-done.9
  34.8 0.0 copy-start.5
  34.8 0.0 copy-start.6
  34.8 0.0 copy-start.7
  34.8 0.0 copy-start.8
  34.8 6.1 %gradient.1 = (f32[2816,128]{1,0:T(8,128)}, f32[32,8,128]{2,1,0:T(8,128)}) custom-call(s32[1]{0:T(128)} %bitcast.own, bf16[64,8,256]{2,1,0:T(8,128)(2,1)} %copy-done.9, f32[128,256]{1,0:T(8,128)} %get-tuple-element.21.envelope_src, f32[128,128]{1,0:T(8,128)} %get-tuple-element.22.columns_src, bf16[4096,256]{1,0:T(8,128)(2,1)} %get-tuple-element.23.cosine_src, ...), custom_call_target="tpu_custom_call" | custom-call | flops 4294967296 | bytes 8388608 | tf_op jit(solution)/shard_map/gradient/pallas_call | solution.py:890
  41.0 7.1 %all-to-all-start.1 = ((f32[32,8,128]{2,1,0:T(8,128)}), f32[32,8,128]{2,1,0:T(8,128)S(1)}, u32[]{:S(2)}, u32[]{:S(2)}) async-start(f32[32,8,128]{2,1,0:T(8,128)} %get-tuple-element.27), calls=%async_computation.1 | async-start | bytes 262144 | tf_op jit(solution)/shard_map/basis/all_to_all | solution.py:1059
  48.1 0.0 copy-done.5
  48.1 0.0 copy-done.6
  48.1 0.0 copy-done.7
  48.1 0.0 copy-done.8
  48.1 0.0 copy-start.1
  48.1 0.0 copy-start.2
  48.1 0.0 copy-start.3
  48.1 0.0 copy-start.4
  48.1 4.5 %output.1.packed = bf16[64,8,256]{2,1,0:T(8,128)(2,1)S(1)} custom-call(s32[1]{0:T(128)} %bitcast.own, f32[2816,128]{1,0:T(8,128)} %get-tuple-element.25.handed_src, bf16[4096,256]{1,0:T(8,128)(2,1)} %get-tuple-element.26.act_src, f32[1,128]{1,0:T(1,128)S(1)} %bitcast.11, bf16[64,384]{1,0:T(8,128)(2,1)S(1)} %copy-done.8, f32[2,64,256]{2,1,0:T(8,128)S(1)} %copy-done.7, ...), custom_call_target="tpu_custom_call" | custom-call | flops 2147483648 | bytes 4194304 | tf_op jit(solution)/shard_map/output/pallas_call | solution.py:890
  52.6 0.0 copy-start
  52.6 2.2 %all-to-all-done.1.basis_parts = f32[32,8,128]{2,1,0:T(8,128)S(1)} async-done(((f32[32,8,128]{2,1,0:T(8,128)}), f32[32,8,128]{2,1,0:T(8,128)S(1)}, u32[]{:S(2)}, u32[]{:S(2)}) %all-to-all-start.1) | async-done | bytes 131104 | tf_op jit(solution)/shard_map/basis/all_to_all | solution.py:1059
  54.9 0.8 %compose.1 = bf16[64,8,256]{2,1,0:T(8,128)(2,1)} custom-call(bf16[64,8,256]{2,1,0:T(8,128)(2,1)S(1)} %output.1.packed, f32[32,8,128]{2,1,0:T(8,128)S(1)} %all-to-all-done.1.basis_parts), custom_call_target="tpu_custom_call" | custom-call | flops 1048576 | bytes 1048576 | tf_op jit(solution)/shard_map/compose/pallas_call | solution.py:890
  55.7 6.4 %all-to-all-start.2 = ((bf16[64,8,256]{2,1,0:T(8,128)(2,1)}), bf16[64,8,256]{2,1,0:T(8,128)(2,1)S(1)}, u32[]{:S(2)}, u32[]{:S(2)}) async-start(bf16[64,8,256]{2,1,0:T(8,128)(2,1)} %compose.1), calls=%async_computation.2 | async-start | bytes 524288 | tf_op jit(solution)/shard_map/collect/all_to_all | solution.py:1059
  62.1 0.0 copy-done.1
  62.1 0.0 copy-done.2
  62.1 0.0 copy-done.3
  62.1 0.0 copy-done.4
  62.1 1.3 %local.1 = (f32[3,128,256]{2,1,0:T(8,128)S(1)}, f32[21,128,128]{2,1,0:T(8,128)S(1)}) custom-call(bf16[128,256]{1,0:T(8,128)(2,1)S(1)} %copy-done.1, bf16[128,256]{1,0:T(8,128)(2,1)S(1)} %copy-done.2, bf16[128,256]{1,0:T(8,128)(2,1)S(1)} %copy-done.3, f32[3,7,128]{2,1,0:T(8,128)S(1)} %bitcast.10), custom_call_target="tpu_custom_call" | custom-call | flops 268435456 | bytes 1048576 | tf_op jit(solution)/shard_map/local/pallas_call | solution.py:890
  63.5 12.5 %all-to-all-done.2.arrived = bf16[64,8,256]{2,1,0:T(8,128)(2,1)S(1)} async-done(((bf16[64,8,256]{2,1,0:T(8,128)(2,1)}), bf16[64,8,256]{2,1,0:T(8,128)(2,1)S(1)}, u32[]{:S(2)}, u32[]{:S(2)}) %all-to-all-start.2) | async-done | bytes 262176 | tf_op jit(solution)/shard_map/collect/all_to_all | solution.py:1059
  75.9 0.0 copy-done
  75.9 1.6 %unpack.1 = (bf16[128,256]{1,0:T(8,128)(2,1)}, bf16[128,256]{1,0:T(8,128)(2,1)}, bf16[128,256]{1,0:T(8,128)(2,1)}, bf16[128,256]{1,0:T(8,128)(2,1)}, f32[64,128]{1,0:T(8,128)}, /*index=5*/f32[33,64]{1,0:T(8,128)}) custom-call(bf16[64,8,256]{2,1,0:T(8,128)(2,1)S(1)} %all-to-all-done.2.arrived, f32[3,128,256]{2,1,0:T(8,128)S(1)} %get-tuple-element.28.feat, ...), custom_call_target="tpu_custom_call" | custom-call | flops 1048576 | bytes 1048576 | tf_op jit(solution)/shard_map/unpack/pallas_call | solution.py:890
Async XLA Ops:
  2.6 31.5 %all-to-all-start = ((bf16[64,8,256]{2,1,0:T(8,128)(2,1)}), bf16[64,8,256]{2,1,0:T(8,128)(2,1)S(1)}, u32[]{:S(2)}, u32[]{:S(2)}) async-start(bf16[64,8,256]{2,1,0:T(8,128)(2,1)} %pack.1), calls=%async_computation | async-start | bytes 524288 | tf_op jit(solution)/shard_map/spread/all_to_all | solution.py:1059
  34.1 0.7 copy-start.9
  34.8 13.2 %copy-start.5 = (f32[128]{0:T(128)S(1)}, f32[128]{0:T(128)}, u32[]{:S(2)}) copy-start(f32[128]{0:T(128)} %param.28) | copy-start | bytes 1540
  34.8 13.2 %copy-start.6 = (bf16[2,512,512]{2,1,0:T(8,128)(2,1)S(1)}, bf16[2,512,512]{2,1,0:T(8,128)(2,1)}, u32[]{:S(2)}) copy-start(bf16[2,512,512]{2,1,0:T(8,128)(2,1)} %constant.48.clone.full_src) | copy-start | bytes 3145732
  34.8 13.2 %copy-start.7 = (f32[2,64,256]{2,1,0:T(8,128)S(1)}, f32[2,64,256]{2,1,0:T(8,128)}, u32[]{:S(2)}) copy-start(f32[2,64,256]{2,1,0:T(8,128)} %constant.47.clone.twiddle_src) | copy-start | bytes 393220
  34.8 13.3 %copy-start.8 = (bf16[64,384]{1,0:T(8,128)(2,1)S(1)}, bf16[64,384]{1,0:T(8,128)(2,1)}, u32[]{:S(2)}) copy-start(bf16[64,384]{1,0:T(8,128)(2,1)} %constant.46.clone.last_src) | copy-start | bytes 147460
  41.0 13.9 %all-to-all-start.1 = ((f32[32,8,128]{2,1,0:T(8,128)}), f32[32,8,128]{2,1,0:T(8,128)S(1)}, u32[]{:S(2)}, u32[]{:S(2)}) async-start(f32[32,8,128]{2,1,0:T(8,128)} %get-tuple-element.27), calls=%async_computation.1 | async-start | bytes 262144 | tf_op jit(solution)/shard_map/basis/all_to_all | solution.py:1059
  48.1 14.0 %copy-start.1 = (bf16[128,256]{1,0:T(8,128)(2,1)S(1)}, bf16[128,256]{1,0:T(8,128)(2,1)}, u32[]{:S(2)}) copy-start(bf16[128,256]{1,0:T(8,128)(2,1)} %query_src.1) | copy-start | bytes 196612
  48.1 14.0 %copy-start.2 = (bf16[128,256]{1,0:T(8,128)(2,1)S(1)}, bf16[128,256]{1,0:T(8,128)(2,1)}, u32[]{:S(2)}) copy-start(bf16[128,256]{1,0:T(8,128)(2,1)} %key_src.1) | copy-start | bytes 196612
  48.1 14.0 %copy-start.3 = (bf16[128,256]{1,0:T(8,128)(2,1)S(1)}, bf16[128,256]{1,0:T(8,128)(2,1)}, u32[]{:S(2)}) copy-start(bf16[128,256]{1,0:T(8,128)(2,1)} %value_src.1) | copy-start | bytes 196612
  48.1 14.0 %copy-start.4 = (f32[3,128,7]{1,2,0:T(8,128)S(1)}, f32[3,128,7]{1,2,0:T(8,128)}, u32[]{:S(2)}) copy-start(f32[3,128,7]{1,2,0:T(8,128)} %param.23) | copy-start | bytes 32260
  52.6 23.3 %copy-start = (bf16[128,256]{1,0:T(8,128)(2,1)S(1)}, bf16[128,256]{1,0:T(8,128)(2,1)}, u32[]{:S(2)}) copy-start(bf16[128,256]{1,0:T(8,128)(2,1)} %grad.3) | copy-start | bytes 196612
  55.7 20.3 %all-to-all-start.2 = ((bf16[64,8,256]{2,1,0:T(8,128)(2,1)}), bf16[64,8,256]{2,1,0:T(8,128)(2,1)S(1)}, u32[]{:S(2)}, u32[]{:S(2)}) async-start(bf16[64,8,256]{2,1,0:T(8,128)(2,1)} %compose.1), calls=%async_computation.2 | async-start | bytes 524288 | tf_op jit(solution)/shard_map/collect/all_to_all | solution.py:1059

commit v7 on v6

--- a/solution.py
+++ b/solution.py
@@ -228,15 +228,21 @@
     return jnp.sum(jnp.where(lane == wanted, row, 0.0), axis=1, keepdims=True)
 
 
-def pack_kernel(query, key, value, grad, out, held, wide, sems):
+def pack_kernel(query, key, value, grad, out, held, wide, stage, out_sems, sems):
     copies = begin(sems, [(ref, held.at[index]) for index, ref in enumerate((query, key, value, grad))])
     for index in range(4):
         copies[index].wait()
         block = held[index].astype(F32)
         for half in range(2):
             wide[half, index * 128 : (index + 1) * 128, :] = block[:, half * 128 : half * 128 + 128]
-    for peer in range(ROWS):
-        out[peer] = take(wide, peer, 8, ROWS).astype(BF16)
+    leaving = []
+    for part in range(4):
+        for peer in range(part * 16, part * 16 + 16):
+            stage[peer] = take(wide, peer, 8, ROWS).astype(BF16)
+        rows = pl.ds(part * 16, 16)
+        leaving += begin(out_sems.at[pl.ds(part, 1)], [(stage.at[rows], out.at[rows])])
+    for copy in leaving:
+        copy.wait()
 
 
 def expm1_small(value):
@@ -575,7 +581,7 @@
             basis_sum = basis_sum + both * angles[inner : inner + 1, :]
         return basis_sum
 
-    basis_sum = lax.fori_loop(0, 8, chunk, jnp.zeros((FEAT, 128), F32), unroll=2)
+    basis_sum = lax.fori_loop(0, 8, chunk, jnp.zeros((FEAT, 128), F32), unroll=4)
     pieces = [
         lax.dot_general(
             place[group],
@@ -748,7 +754,7 @@
         out[:, :, half * 128 : half * 128 + 128] = value.astype(BF16)
 
 
-def compose_kernel(packed, basis_parts, out):
+def compose_kernel(packed, basis_parts, out, stage, out_sems):
     basis = basis_parts[0]
     for source in range(1, 32):
         basis = basis + basis_parts[source]
@@ -760,7 +766,13 @@
     )
     right = jnp.where(row == 5, basis[1:2], jnp.where(row == 6, basis[3:4], 0.0))
     extra = jnp.concatenate([left, right], axis=1)
-    out[...] = (packed[...].astype(F32) + extra[None]).astype(BF16)
+    leaving = []
+    for part in range(4):
+        rows = pl.ds(part * 16, 16)
+        stage[rows] = (packed[rows].astype(F32) + extra[None]).astype(BF16)
+        leaving += begin(out_sems.at[pl.ds(part, 1)], [(stage.at[rows], out.at[rows])])
+    for copy in leaving:
+        copy.wait()
 
 
 def local_kernel(
@@ -912,8 +924,13 @@
         [],
         [],
         [query_in, key_in, value_in, grad_out],
-        [(shape((ROWS, 8, COLS), BF16), False)],
-        [pltpu.VMEM((4, 128, COLS), BF16), pltpu.VMEM((2, 512, 128), F32)],
+        [(shape((ROWS, 8, COLS), BF16), True)],
+        [
+            pltpu.VMEM((4, 128, COLS), BF16),
+            pltpu.VMEM((2, 512, 128), F32),
+            pltpu.VMEM((ROWS, 8, COLS), BF16),
+            pltpu.SemaphoreType.DMA((4,)),
+        ],
         1 << 20,
         1 << 19,
     )[0]
@@ -995,8 +1012,8 @@
         [],
         [packed, basis_parts],
         [],
-        [(shape((ROWS, 8, COLS), BF16), False)],
-        [],
+        [(shape((ROWS, 8, COLS), BF16), True)],
+        [pltpu.VMEM((ROWS, 8, COLS), BF16), pltpu.SemaphoreType.DMA((4,))],
         1 << 20,
         1 << 20,
         ROOMY,

time: 77.9 us -> 77.7 us (level)
  no operation moved by 1% of the time
where the time goes in v7:
time: 77.7 us; the launch traced here: 77.3 us
  starting transfers between devices  31.1 us (40%)
  Pallas kernels  24.7 us (32%)
  waiting for transfers between devices  19.9 us (26%)
  between operations  0.82 us (1%)
    all_to_all x3, starting transfers between devices, exchange(): return lax.all_to_all(value, axes, split_axis=0, concat_axis=0, tiled=True)  31.1 us
    pallas_call x7, Pallas kernels, call(): pl.pallas_call(kernel, name=name, in_specs=[SMEM] * len(own) + [VMEM] * l...  24.7 us
    all_to_all x3, waiting for transfers between devices, exchange(): return lax.all_to_all(value, axes, split_axis=0, concat_axis=0, tiled=True)  19.9 us
  transfers between devices with their start and end apart: 3, of which 3 were waited for; matrix products, arithmetic and copies ran while one was open for 0% of the time, Pallas kernels for 19%

profile of v7, /device:TPU:1, one launch (start us, length us, event | category | flops | bytes accessed | tf_op | source)
XLA Modules:
  0.0 77.3 jit_solution(7973156547752348651)
XLA Ops:
  0.6 1.9 %pack.1 = bf16[64,8,256]{2,1,0:T(8,128)(2,1)} custom-call(bf16[128,256]{1,0:T(8,128)(2,1)} %query_src.1, bf16[128,256]{1,0:T(8,128)(2,1)} %key_src.1, bf16[128,256]{1,0:T(8,128)(2,1)} %value_src.1, bf16[128,256]{1,0:T(8,128)(2,1)} %grad.3), custom_call_target="tpu_custom_call" | custom-call | flops 1048576 | bytes 524288 | tf_op jit(solution)/shard_map/spread/pack/pallas_call | solution.py:902
  2.6 17.6 %all-to-all-start = ((bf16[64,8,256]{2,1,0:T(8,128)(2,1)}), bf16[64,8,256]{2,1,0:T(8,128)(2,1)S(1)}, u32[]{:S(2)}, u32[]{:S(2)}) async-start(bf16[64,8,256]{2,1,0:T(8,128)(2,1)} %pack.1), calls=%async_computation | async-start | bytes 524288 | tf_op jit(solution)/shard_map/spread/all_to_all | solution.py:1076
  20.2 8.6 %filter.1 = (bf16[4096,256]{1,0:T(8,128)(2,1)}, bf16[4096,256]{1,0:T(8,128)(2,1)}, f32[128,256]{1,0:T(8,128)}, f32[128,512]{1,0:T(8,128)}, f32[128,128]{1,0:T(8,128)}) custom-call(s32[1]{0:T(128)} %bitcast.own, f32[33,64]{1,0:T(8,128)} %bitcast.14, f32[1,64]{1,0:T(1,128)} %bitcast.16, f32[64,128]{1,0:T(8,128)} %bitcast.12, f32[1,128]{1,0:T(1,128)} %bitcast.17, ...), custom_call_target="tpu_custom_call" | custom-call | flops 8589934592 | bytes 8388608 | tf_op jit(solution)/shard_map/filter/pallas_call | solution.py:902
  28.9 5.2 %all-to-all-done.arrived_src = bf16[64,8,256]{2,1,0:T(8,128)(2,1)S(1)} async-done(((bf16[64,8,256]{2,1,0:T(8,128)(2,1)}), bf16[64,8,256]{2,1,0:T(8,128)(2,1)S(1)}, u32[]{:S(2)}, u32[]{:S(2)}) %all-to-all-start) | async-done | bytes 262176 | tf_op jit(solution)/shard_map/spread/all_to_all | solution.py:1076
  34.1 0.0 copy-start.9
  34.1 0.7 copy-done.9
  34.8 0.0 copy-start.5
  34.8 0.0 copy-start.6
  34.8 0.0 copy-start.7
  34.8 0.0 copy-start.8
  34.8 5.9 %gradient.1 = (f32[2816,128]{1,0:T(8,128)}, f32[32,8,128]{2,1,0:T(8,128)}) custom-call(s32[1]{0:T(128)} %bitcast.own, bf16[64,8,256]{2,1,0:T(8,128)(2,1)} %copy-done.9, f32[128,256]{1,0:T(8,128)} %get-tuple-element.21.envelope_src, f32[128,128]{1,0:T(8,128)} %get-tuple-element.22.columns_src, bf16[4096,256]{1,0:T(8,128)(2,1)} %get-tuple-element.23.cosine_src, ...), custom_call_target="tpu_custom_call" | custom-call | flops 4294967296 | bytes 8388608 | tf_op jit(solution)/shard_map/gradient/pallas_call | solution.py:902
  40.7 7.1 %all-to-all-start.1 = ((f32[32,8,128]{2,1,0:T(8,128)}), f32[32,8,128]{2,1,0:T(8,128)S(1)}, u32[]{:S(2)}, u32[]{:S(2)}) async-start(f32[32,8,128]{2,1,0:T(8,128)} %get-tuple-element.27), calls=%async_computation.1 | async-start | bytes 262144 | tf_op jit(solution)/shard_map/basis/all_to_all | solution.py:1076
  47.8 0.0 copy-done.5
  47.8 0.0 copy-done.6
  47.8 0.0 copy-done.7
  47.8 0.0 copy-done.8
  47.8 0.0 copy-start.1
  47.8 0.0 copy-start.2
  47.8 0.0 copy-start.3
  47.9 0.0 copy-start.4
  47.9 4.4 %output.1.packed = bf16[64,8,256]{2,1,0:T(8,128)(2,1)S(1)} custom-call(s32[1]{0:T(128)} %bitcast.own, f32[2816,128]{1,0:T(8,128)} %get-tuple-element.25.handed_src, bf16[4096,256]{1,0:T(8,128)(2,1)} %get-tuple-element.26.act_src, f32[1,128]{1,0:T(1,128)S(1)} %bitcast.11, bf16[64,384]{1,0:T(8,128)(2,1)S(1)} %copy-done.8, f32[2,64,256]{2,1,0:T(8,128)S(1)} %copy-done.7, ...), custom_call_target="tpu_custom_call" | custom-call | flops 2147483648 | bytes 4194304 | tf_op jit(solution)/shard_map/output/pallas_call | solution.py:902
  52.3 0.0 copy-start
  52.3 2.2 %all-to-all-done.1.basis_parts = f32[32,8,128]{2,1,0:T(8,128)S(1)} async-done(((f32[32,8,128]{2,1,0:T(8,128)}), f32[32,8,128]{2,1,0:T(8,128)S(1)}, u32[]{:S(2)}, u32[]{:S(2)}) %all-to-all-start.1) | async-done | bytes 131104 | tf_op jit(solution)/shard_map/basis/all_to_all | solution.py:1076
  54.6 0.8 %compose.1 = bf16[64,8,256]{2,1,0:T(8,128)(2,1)} custom-call(bf16[64,8,256]{2,1,0:T(8,128)(2,1)S(1)} %output.1.packed, f32[32,8,128]{2,1,0:T(8,128)S(1)} %all-to-all-done.1.basis_parts), custom_call_target="tpu_custom_call" | custom-call | flops 1048576 | bytes 1048576 | tf_op jit(solution)/shard_map/compose/pallas_call | solution.py:902
  55.4 6.4 %all-to-all-start.2 = ((bf16[64,8,256]{2,1,0:T(8,128)(2,1)}), bf16[64,8,256]{2,1,0:T(8,128)(2,1)S(1)}, u32[]{:S(2)}, u32[]{:S(2)}) async-start(bf16[64,8,256]{2,1,0:T(8,128)(2,1)} %compose.1), calls=%async_computation.2 | async-start | bytes 524288 | tf_op jit(solution)/shard_map/collect/all_to_all | solution.py:1076
  61.8 0.0 copy-done.1
  61.8 0.0 copy-done.2
  61.8 0.0 copy-done.3
  61.8 0.0 copy-done.4
  61.8 1.3 %local.1 = (f32[3,128,256]{2,1,0:T(8,128)S(1)}, f32[21,128,128]{2,1,0:T(8,128)S(1)}) custom-call(bf16[128,256]{1,0:T(8,128)(2,1)S(1)} %copy-done.1, bf16[128,256]{1,0:T(8,128)(2,1)S(1)} %copy-done.2, bf16[128,256]{1,0:T(8,128)(2,1)S(1)} %copy-done.3, f32[3,7,128]{2,1,0:T(8,128)S(1)} %bitcast.10), custom_call_target="tpu_custom_call" | custom-call | flops 268435456 | bytes 1048576 | tf_op jit(solution)/shard_map/local/pallas_call | solution.py:902
  63.2 12.5 %all-to-all-done.2.arrived = bf16[64,8,256]{2,1,0:T(8,128)(2,1)S(1)} async-done(((bf16[64,8,256]{2,1,0:T(8,128)(2,1)}), bf16[64,8,256]{2,1,0:T(8,128)(2,1)S(1)}, u32[]{:S(2)}, u32[]{:S(2)}) %all-to-all-start.2) | async-done | bytes 262176 | tf_op jit(solution)/shard_map/collect/all_to_all | solution.py:1076
  75.7 0.0 copy-done
  75.7 1.6 %unpack.1 = (bf16[128,256]{1,0:T(8,128)(2,1)}, bf16[128,256]{1,0:T(8,128)(2,1)}, bf16[128,256]{1,0:T(8,128)(2,1)}, bf16[128,256]{1,0:T(8,128)(2,1)}, f32[64,128]{1,0:T(8,128)}, /*index=5*/f32[33,64]{1,0:T(8,128)}) custom-call(bf16[64,8,256]{2,1,0:T(8,128)(2,1)S(1)} %all-to-all-done.2.arrived, f32[3,128,256]{2,1,0:T(8,128)S(1)} %get-tuple-element.28.feat, ...), custom_call_target="tpu_custom_call" | custom-call | flops 1048576 | bytes 1048576 | tf_op jit(solution)/shard_map/unpack/pallas_call | solution.py:902
Async XLA Ops:
  2.6 31.5 %all-to-all-start = ((bf16[64,8,256]{2,1,0:T(8,128)(2,1)}), bf16[64,8,256]{2,1,0:T(8,128)(2,1)S(1)}, u32[]{:S(2)}, u32[]{:S(2)}) async-start(bf16[64,8,256]{2,1,0:T(8,128)(2,1)} %pack.1), calls=%async_computation | async-start | bytes 524288 | tf_op jit(solution)/shard_map/spread/all_to_all | solution.py:1076
  34.1 0.7 copy-start.9
  34.8 13.0 %copy-start.5 = (f32[128]{0:T(128)S(1)}, f32[128]{0:T(128)}, u32[]{:S(2)}) copy-start(f32[128]{0:T(128)} %param.28) | copy-start | bytes 1540
  34.8 13.0 %copy-start.6 = (bf16[2,512,512]{2,1,0:T(8,128)(2,1)S(1)}, bf16[2,512,512]{2,1,0:T(8,128)(2,1)}, u32[]{:S(2)}) copy-start(bf16[2,512,512]{2,1,0:T(8,128)(2,1)} %constant.48.clone.full_src) | copy-start | bytes 3145732
  34.8 13.0 %copy-start.7 = (f32[2,64,256]{2,1,0:T(8,128)S(1)}, f32[2,64,256]{2,1,0:T(8,128)}, u32[]{:S(2)}) copy-start(f32[2,64,256]{2,1,0:T(8,128)} %constant.47.clone.twiddle_src) | copy-start | bytes 393220
  34.8 13.0 %copy-start.8 = (bf16[64,384]{1,0:T(8,128)(2,1)S(1)}, bf16[64,384]{1,0:T(8,128)(2,1)}, u32[]{:S(2)}) copy-start(bf16[64,384]{1,0:T(8,128)(2,1)} %constant.46.clone.last_src) | copy-start | bytes 147460
  40.7 13.9 %all-to-all-start.1 = ((f32[32,8,128]{2,1,0:T(8,128)}), f32[32,8,128]{2,1,0:T(8,128)S(1)}, u32[]{:S(2)}, u32[]{:S(2)}) async-start(f32[32,8,128]{2,1,0:T(8,128)} %get-tuple-element.27), calls=%async_computation.1 | async-start | bytes 262144 | tf_op jit(solution)/shard_map/basis/all_to_all | solution.py:1076
  47.8 14.0 %copy-start.1 = (bf16[128,256]{1,0:T(8,128)(2,1)S(1)}, bf16[128,256]{1,0:T(8,128)(2,1)}, u32[]{:S(2)}) copy-start(bf16[128,256]{1,0:T(8,128)(2,1)} %query_src.1) | copy-start | bytes 196612
  47.8 14.0 %copy-start.2 = (bf16[128,256]{1,0:T(8,128)(2,1)S(1)}, bf16[128,256]{1,0:T(8,128)(2,1)}, u32[]{:S(2)}) copy-start(bf16[128,256]{1,0:T(8,128)(2,1)} %key_src.1) | copy-start | bytes 196612
  47.8 14.0 %copy-start.3 = (bf16[128,256]{1,0:T(8,128)(2,1)S(1)}, bf16[128,256]{1,0:T(8,128)(2,1)}, u32[]{:S(2)}) copy-start(bf16[128,256]{1,0:T(8,128)(2,1)} %value_src.1) | copy-start | bytes 196612
  47.9 14.0 %copy-start.4 = (f32[3,128,7]{1,2,0:T(8,128)S(1)}, f32[3,128,7]{1,2,0:T(8,128)}, u32[]{:S(2)}) copy-start(f32[3,128,7]{1,2,0:T(8,128)} %param.23) | copy-start | bytes 32260
  52.3 23.3 %copy-start = (bf16[128,256]{1,0:T(8,128)(2,1)S(1)}, bf16[128,256]{1,0:T(8,128)(2,1)}, u32[]{:S(2)}) copy-start(bf16[128,256]{1,0:T(8,128)(2,1)} %grad.3) | copy-start | bytes 196612
  55.4 20.2 %all-to-all-start.2 = ((bf16[64,8,256]{2,1,0:T(8,128)(2,1)}), bf16[64,8,256]{2,1,0:T(8,128)(2,1)S(1)}, u32[]{:S(2)}, u32[]{:S(2)}) async-start(bf16[64,8,256]{2,1,0:T(8,128)(2,1)} %compose.1), calls=%async_computation.2 | async-start | bytes 524288 | tf_op jit(solution)/shard_map/collect/all_to_all | solution.py:1076

commit v8 on v7

--- a/solution.py
+++ b/solution.py
@@ -734,7 +734,7 @@
             proj_sum = proj_sum + jnp.where(row_lane == inner, product[near : near + FEAT, :], 0.0)
         return proj_sum
 
-    proj_sum = lax.fori_loop(0, 8, chunk, jnp.zeros((FEAT, 128), F32), unroll=2)
+    proj_sum = lax.fori_loop(0, 8, chunk, jnp.zeros((FEAT, 128), F32), unroll=4)
     own_lane = lane128 % 16
     stacked = jnp.concatenate(
         [jnp.where(own_lane < 8, proj_sum, 0.0), jnp.where(own_lane >= 8, proj_sum, 0.0)], axis=0

time: 77.7 us -> 77.7 us (level)
  transfers between devices with their start and end apart: 3 -> 3, of which waited for: 3 -> 3; matrix products, arithmetic and copies ran while one was open for 0% -> 0% of each run, Pallas kernels for 19% -> 18%
where the time goes in v8:
time: 77.7 us; the launch traced here: 77.3 us
  starting transfers between devices  31.1 us (40%)
  Pallas kernels  24.2 us (31%)
  waiting for transfers between devices  20.4 us (26%)
  between operations  0.82 us (1%)
    all_to_all x3, starting transfers between devices, exchange(): return lax.all_to_all(value, axes, split_axis=0, concat_axis=0, tiled=True)  31.1 us
    pallas_call x7, Pallas kernels, call(): pl.pallas_call(kernel, name=name, in_specs=[SMEM] * len(own) + [VMEM] * l...  24.2 us
    all_to_all x3, waiting for transfers between devices, exchange(): return lax.all_to_all(value, axes, split_axis=0, concat_axis=0, tiled=True)  20.4 us
  transfers between devices with their start and end apart: 3, of which 3 were waited for; matrix products, arithmetic and copies ran while one was open for 0% of the time, Pallas kernels for 18%

profile of v8, /device:TPU:1, one launch (start us, length us, event | category | flops | bytes accessed | tf_op | source)
XLA Modules:
  0.0 77.3 jit_solution(8249831684625776962)
XLA Ops:
  0.6 1.9 %pack.1 = bf16[64,8,256]{2,1,0:T(8,128)(2,1)} custom-call(bf16[128,256]{1,0:T(8,128)(2,1)} %query_src.1, bf16[128,256]{1,0:T(8,128)(2,1)} %key_src.1, bf16[128,256]{1,0:T(8,128)(2,1)} %value_src.1, bf16[128,256]{1,0:T(8,128)(2,1)} %grad.3), custom_call_target="tpu_custom_call" | custom-call | flops 1048576 | bytes 524288 | tf_op jit(solution)/shard_map/spread/pack/pallas_call | solution.py:902
  2.6 17.6 %all-to-all-start = ((bf16[64,8,256]{2,1,0:T(8,128)(2,1)}), bf16[64,8,256]{2,1,0:T(8,128)(2,1)S(1)}, u32[]{:S(2)}, u32[]{:S(2)}) async-start(bf16[64,8,256]{2,1,0:T(8,128)(2,1)} %pack.1), calls=%async_computation | async-start | bytes 524288 | tf_op jit(solution)/shard_map/spread/all_to_all | solution.py:1076
  20.2 8.6 %filter.1 = (bf16[4096,256]{1,0:T(8,128)(2,1)}, bf16[4096,256]{1,0:T(8,128)(2,1)}, f32[128,256]{1,0:T(8,128)}, f32[128,512]{1,0:T(8,128)}, f32[128,128]{1,0:T(8,128)}) custom-call(s32[1]{0:T(128)} %bitcast.own, f32[33,64]{1,0:T(8,128)} %bitcast.14, f32[1,64]{1,0:T(1,128)} %bitcast.16, f32[64,128]{1,0:T(8,128)} %bitcast.12, f32[1,128]{1,0:T(1,128)} %bitcast.17, ...), custom_call_target="tpu_custom_call" | custom-call | flops 8589934592 | bytes 8388608 | tf_op jit(solution)/shard_map/filter/pallas_call | solution.py:902
  28.9 5.2 %all-to-all-done.arrived_src = bf16[64,8,256]{2,1,0:T(8,128)(2,1)S(1)} async-done(((bf16[64,8,256]{2,1,0:T(8,128)(2,1)}), bf16[64,8,256]{2,1,0:T(8,128)(2,1)S(1)}, u32[]{:S(2)}, u32[]{:S(2)}) %all-to-all-start) | async-done | bytes 262176 | tf_op jit(solution)/shard_map/spread/all_to_all | solution.py:1076
  34.1 0.0 copy-start.9
  34.1 0.7 copy-done.9
  34.8 0.0 copy-start.5
  34.8 0.0 copy-start.6
  34.8 0.0 copy-start.7
  34.8 0.0 copy-start.8
  34.8 5.9 %gradient.1 = (f32[2816,128]{1,0:T(8,128)}, f32[32,8,128]{2,1,0:T(8,128)}) custom-call(s32[1]{0:T(128)} %bitcast.own, bf16[64,8,256]{2,1,0:T(8,128)(2,1)} %copy-done.9, f32[128,256]{1,0:T(8,128)} %get-tuple-element.21.envelope_src, f32[128,128]{1,0:T(8,128)} %get-tuple-element.22.columns_src, bf16[4096,256]{1,0:T(8,128)(2,1)} %get-tuple-element.23.cosine_src, ...), custom_call_target="tpu_custom_call" | custom-call | flops 4294967296 | bytes 8388608 | tf_op jit(solution)/shard_map/gradient/pallas_call | solution.py:902
  40.7 7.1 %all-to-all-start.1 = ((f32[32,8,128]{2,1,0:T(8,128)}), f32[32,8,128]{2,1,0:T(8,128)S(1)}, u32[]{:S(2)}, u32[]{:S(2)}) async-start(f32[32,8,128]{2,1,0:T(8,128)} %get-tuple-element.27), calls=%async_computation.1 | async-start | bytes 262144 | tf_op jit(solution)/shard_map/basis/all_to_all | solution.py:1076
  47.8 0.0 copy-done.5
  47.8 0.0 copy-done.6
  47.8 0.0 copy-done.7
  47.8 0.0 copy-done.8
  47.8 0.0 copy-start.1
  47.8 0.0 copy-start.2
  47.8 0.0 copy-start.3
  47.9 0.0 copy-start.4
  47.9 3.9 %output.1.packed = bf16[64,8,256]{2,1,0:T(8,128)(2,1)S(1)} custom-call(s32[1]{0:T(128)} %bitcast.own, f32[2816,128]{1,0:T(8,128)} %get-tuple-element.25.handed_src, bf16[4096,256]{1,0:T(8,128)(2,1)} %get-tuple-element.26.act_src, f32[1,128]{1,0:T(1,128)S(1)} %bitcast.11, bf16[64,384]{1,0:T(8,128)(2,1)S(1)} %copy-done.8, f32[2,64,256]{2,1,0:T(8,128)S(1)} %copy-done.7, ...), custom_call_target="tpu_custom_call" | custom-call | flops 2147483648 | bytes 4194304 | tf_op jit(solution)/shard_map/output/pallas_call | solution.py:902
  51.8 0.0 copy-start
  51.8 2.7 %all-to-all-done.1.basis_parts = f32[32,8,128]{2,1,0:T(8,128)S(1)} async-done(((f32[32,8,128]{2,1,0:T(8,128)}), f32[32,8,128]{2,1,0:T(8,128)S(1)}, u32[]{:S(2)}, u32[]{:S(2)}) %all-to-all-start.1) | async-done | bytes 131104 | tf_op jit(solution)/shard_map/basis/all_to_all | solution.py:1076
  54.6 0.8 %compose.1 = bf16[64,8,256]{2,1,0:T(8,128)(2,1)} custom-call(bf16[64,8,256]{2,1,0:T(8,128)(2,1)S(1)} %output.1.packed, f32[32,8,128]{2,1,0:T(8,128)S(1)} %all-to-all-done.1.basis_parts), custom_call_target="tpu_custom_call" | custom-call | flops 1048576 | bytes 1048576 | tf_op jit(solution)/shard_map/compose/pallas_call | solution.py:902
  55.4 6.4 %all-to-all-start.2 = ((bf16[64,8,256]{2,1,0:T(8,128)(2,1)}), bf16[64,8,256]{2,1,0:T(8,128)(2,1)S(1)}, u32[]{:S(2)}, u32[]{:S(2)}) async-start(bf16[64,8,256]{2,1,0:T(8,128)(2,1)} %compose.1), calls=%async_computation.2 | async-start | bytes 524288 | tf_op jit(solution)/shard_map/collect/all_to_all | solution.py:1076
  61.8 0.0 copy-done.1
  61.8 0.0 copy-done.2
  61.8 0.0 copy-done.3
  61.8 0.0 copy-done.4
  61.8 1.3 %local.1 = (f32[3,128,256]{2,1,0:T(8,128)S(1)}, f32[21,128,128]{2,1,0:T(8,128)S(1)}) custom-call(bf16[128,256]{1,0:T(8,128)(2,1)S(1)} %copy-done.1, bf16[128,256]{1,0:T(8,128)(2,1)S(1)} %copy-done.2, bf16[128,256]{1,0:T(8,128)(2,1)S(1)} %copy-done.3, f32[3,7,128]{2,1,0:T(8,128)S(1)} %bitcast.10), custom_call_target="tpu_custom_call" | custom-call | flops 268435456 | bytes 1048576 | tf_op jit(solution)/shard_map/local/pallas_call | solution.py:902
  63.2 12.5 %all-to-all-done.2.arrived = bf16[64,8,256]{2,1,0:T(8,128)(2,1)S(1)} async-done(((bf16[64,8,256]{2,1,0:T(8,128)(2,1)}), bf16[64,8,256]{2,1,0:T(8,128)(2,1)S(1)}, u32[]{:S(2)}, u32[]{:S(2)}) %all-to-all-start.2) | async-done | bytes 262176 | tf_op jit(solution)/shard_map/collect/all_to_all | solution.py:1076
  75.7 0.0 copy-done
  75.7 1.6 %unpack.1 = (bf16[128,256]{1,0:T(8,128)(2,1)}, bf16[128,256]{1,0:T(8,128)(2,1)}, bf16[128,256]{1,0:T(8,128)(2,1)}, bf16[128,256]{1,0:T(8,128)(2,1)}, f32[64,128]{1,0:T(8,128)}, /*index=5*/f32[33,64]{1,0:T(8,128)}) custom-call(bf16[64,8,256]{2,1,0:T(8,128)(2,1)S(1)} %all-to-all-done.2.arrived, f32[3,128,256]{2,1,0:T(8,128)S(1)} %get-tuple-element.28.feat, ...), custom_call_target="tpu_custom_call" | custom-call | flops 1048576 | bytes 1048576 | tf_op jit(solution)/shard_map/unpack/pallas_call | solution.py:902
Async XLA Ops:
  2.6 31.5 %all-to-all-start = ((bf16[64,8,256]{2,1,0:T(8,128)(2,1)}), bf16[64,8,256]{2,1,0:T(8,128)(2,1)S(1)}, u32[]{:S(2)}, u32[]{:S(2)}) async-start(bf16[64,8,256]{2,1,0:T(8,128)(2,1)} %pack.1), calls=%async_computation | async-start | bytes 524288 | tf_op jit(solution)/shard_map/spread/all_to_all | solution.py:1076
  34.1 0.7 copy-start.9
  34.8 13.0 %copy-start.5 = (f32[128]{0:T(128)S(1)}, f32[128]{0:T(128)}, u32[]{:S(2)}) copy-start(f32[128]{0:T(128)} %param.28) | copy-start | bytes 1540
  34.8 13.0 %copy-start.6 = (bf16[2,512,512]{2,1,0:T(8,128)(2,1)S(1)}, bf16[2,512,512]{2,1,0:T(8,128)(2,1)}, u32[]{:S(2)}) copy-start(bf16[2,512,512]{2,1,0:T(8,128)(2,1)} %constant.48.clone.full_src) | copy-start | bytes 3145732
  34.8 13.0 %copy-start.7 = (f32[2,64,256]{2,1,0:T(8,128)S(1)}, f32[2,64,256]{2,1,0:T(8,128)}, u32[]{:S(2)}) copy-start(f32[2,64,256]{2,1,0:T(8,128)} %constant.47.clone.twiddle_src) | copy-start | bytes 393220
  34.8 13.0 %copy-start.8 = (bf16[64,384]{1,0:T(8,128)(2,1)S(1)}, bf16[64,384]{1,0:T(8,128)(2,1)}, u32[]{:S(2)}) copy-start(bf16[64,384]{1,0:T(8,128)(2,1)} %constant.46.clone.last_src) | copy-start | bytes 147460
  40.7 13.9 %all-to-all-start.1 = ((f32[32,8,128]{2,1,0:T(8,128)}), f32[32,8,128]{2,1,0:T(8,128)S(1)}, u32[]{:S(2)}, u32[]{:S(2)}) async-start(f32[32,8,128]{2,1,0:T(8,128)} %get-tuple-element.27), calls=%async_computation.1 | async-start | bytes 262144 | tf_op jit(solution)/shard_map/basis/all_to_all | solution.py:1076
  47.8 14.0 %copy-start.1 = (bf16[128,256]{1,0:T(8,128)(2,1)S(1)}, bf16[128,256]{1,0:T(8,128)(2,1)}, u32[]{:S(2)}) copy-start(bf16[128,256]{1,0:T(8,128)(2,1)} %query_src.1) | copy-start | bytes 196612
  47.8 14.0 %copy-start.2 = (bf16[128,256]{1,0:T(8,128)(2,1)S(1)}, bf16[128,256]{1,0:T(8,128)(2,1)}, u32[]{:S(2)}) copy-start(bf16[128,256]{1,0:T(8,128)(2,1)} %key_src.1) | copy-start | bytes 196612
  47.8 14.0 %copy-start.3 = (bf16[128,256]{1,0:T(8,128)(2,1)S(1)}, bf16[128,256]{1,0:T(8,128)(2,1)}, u32[]{:S(2)}) copy-start(bf16[128,256]{1,0:T(8,128)(2,1)} %value_src.1) | copy-start | bytes 196612
  47.9 14.0 %copy-start.4 = (f32[3,128,7]{1,2,0:T(8,128)S(1)}, f32[3,128,7]{1,2,0:T(8,128)}, u32[]{:S(2)}) copy-start(f32[3,128,7]{1,2,0:T(8,128)} %param.23) | copy-start | bytes 32260
  51.8 23.9 %copy-start = (bf16[128,256]{1,0:T(8,128)(2,1)S(1)}, bf16[128,256]{1,0:T(8,128)(2,1)}, u32[]{:S(2)}) copy-start(bf16[128,256]{1,0:T(8,128)(2,1)} %grad.3) | copy-start | bytes 196612
  55.4 20.2 %all-to-all-start.2 = ((bf16[64,8,256]{2,1,0:T(8,128)(2,1)}), bf16[64,8,256]{2,1,0:T(8,128)(2,1)S(1)}, u32[]{:S(2)}, u32[]{:S(2)}) async-start(bf16[64,8,256]{2,1,0:T(8,128)(2,1)} %compose.1), calls=%async_computation.2 | async-start | bytes 524288 | tf_op jit(solution)/shard_map/collect/all_to_all | solution.py:1076
